TPU v7x, 256 devices: a whole 4x4x8 slice. The times are simulated.
256 devices in a mesh: rep: 16 (over x_hi, z), head: 8 (over y, core), pair: 2 (over x_lo).
Axes of the slice: x: 4 (x_hi: 2, x_lo: 2; x = x_hi * 2 + x_lo), y: 4, z: 8, core: 2. Of those that a mesh axis runs over, the one named last changes fastest.
Arguments:
- queries: bfloat16 [384, 8192], P(('rep', 'pair'), 'head'), may hold values from -24 to 24
- new_keys: bfloat16 [384, 1024], P(('rep', 'pair'), 'head'), may hold values from -6 to 6
- new_values: bfloat16 [384, 1024], P(('rep', 'pair'), 'head'), may hold values from -6 to 6
- key_cache: bfloat16 [384, 1024, 1024], P(('rep', 'pair'), None, 'head'), may hold values from -6 to 6
- value_cache: bfloat16 [384, 1024, 1024], P(('rep', 'pair'), None, 'head'), may hold values from -6 to 6
- lengths: int32 [384], P(('rep', 'pair')), may hold values from 2 to 1024
- residual: bfloat16 [384, 8192], P('head', ('rep', 'pair')), may hold values from -36 to 36
- norm_gain: float32 [8192], replicated, may hold values from 0.5 to 1.5
- out_weight: bfloat16 [8192, 8192], P('head', ('rep', 'pair')), may hold values from -0.5 to 0.5
- gate_weight: bfloat16 [8192, 28672], P('head', ('rep', 'pair')), may hold values from -0.0625 to 0.0625
- up_weight: bfloat16 [8192, 28672], P('head', ('rep', 'pair')), may hold values from -0.0625 to 0.0625
- down_weight: bfloat16 [28672, 8192], P(('rep', 'pair'), 'head'), may hold values from -0.03125 to 0.03125
Outputs:
- hidden_state: bfloat16 [384, 8192], P('head', ('rep', 'pair'))
- ffn_out: bfloat16 [384, 8192], P(('rep', 'pair'), 'head')
Inputs may be any that keep to these rules, and one draw needn't show every extreme that they name: Cache slots 0 to lengths - 1 of a row are live, the others are ignored.
All inputs are finite; a program needn't handle non-finite values.
Results may differ from a plain program's by a relative error of at most 0.0095.
Values may be sent and summed in bfloat16 or wider, within the bound.
No kernel may reach another device: no remote copies, remote signals or barrier semaphores. Data moves between devices by JAX's collectives and lax.ppermute only.
A program may use at most 64 MiB of HBM per device.

v0:
```python
import jax
import jax.numpy as jnp
from jax import lax
from jax.sharding import PartitionSpec as P

HEADS = 64
KV_HEADS = 8
HEAD_DIM = 128


def sent_to_all(array, axis):
    copies = jnp.broadcast_to(array, (lax.axis_size(axis), *array.shape))
    return lax.all_to_all(copies, axis, split_axis=0, concat_axis=0, tiled=True)


def in_order(pieces, dim):
    dims = list(pieces.shape[1:])
    dims[dim] *= pieces.shape[0]
    return jnp.moveaxis(pieces, 0, dim).reshape(dims)


def gathered_copies(array, axis, dim):
    pieces = sent_to_all(array, axis)
    return in_order(pieces, dim)


def cut_along(array, dim, size):
    dims = array.shape
    pieces = array.reshape(*dims[:dim], size, dims[dim] // size, *dims[dim + 1 :])
    return jnp.moveaxis(pieces, dim, 0)


def sent_and_summed(array, axis, dim):
    size = lax.axis_size(axis)
    pieces = lax.all_to_all(cut_along(array, dim, size), axis, 0, 0, tiled=True)
    return jnp.sum(pieces, axis=0)


def side_by_side(arrays, axis, dim, along):
    both = jnp.concatenate(arrays, axis=along)
    filled, at, done = (sent_and_summed(both, axis, dim), 0, [])
    for a in arrays:
        done.append(lax.slice_in_dim(filled, at, at + a.shape[along], axis=along))
        at += a.shape[along]
    return tuple(done)


def local(
    queries,
    new_keys,
    new_values,
    key_cache,
    value_cache,
    lengths,
    residual,
    norm_gain,
    out_weight,
    gate_weight,
    up_weight,
    down_weight,
):
    row_count = queries.shape[0]
    slot_count = key_cache.shape[1]
    kv_local = key_cache.shape[2] // HEAD_DIM
    group_size = HEADS // KV_HEADS
    score_scale = HEAD_DIM ** (-0.5)
    query_heads = queries.reshape(row_count, kv_local, group_size, HEAD_DIM)
    cached_keys = key_cache.reshape(row_count, slot_count, kv_local, HEAD_DIM)
    cached_values = value_cache.reshape(row_count, slot_count, kv_local, HEAD_DIM)
    key_new = new_keys.reshape(row_count, kv_local, HEAD_DIM)
    value_new = new_values.reshape(row_count, kv_local, HEAD_DIM).astype(jnp.float32)
    scores = (
        jnp.einsum("rhgd,rchd->rhgc", query_heads, cached_keys, preferred_element_type=jnp.float32)
        * score_scale
    )
    slot_ids = lax.broadcasted_iota(jnp.int32, (row_count, 1, 1, slot_count), 3)
    live_mask = slot_ids < lengths[:, None, None, None]
    scores = jnp.where(live_mask, scores, -jnp.inf)
    own_score = (
        jnp.einsum("rhgd,rhd->rhg", query_heads, key_new, preferred_element_type=jnp.float32)
        * score_scale
    )
    row_top = jnp.maximum(jnp.max(scores, axis=3), own_score)
    weights = jnp.exp(scores - row_top[..., None])
    own_weight = jnp.exp(own_score - row_top)
    weight_total = jnp.sum(weights, axis=3) + own_weight
    weights_low = weights.astype(jnp.bfloat16)
    own_low = own_weight.astype(jnp.bfloat16).astype(jnp.float32)
    mixture = jnp.einsum(
        "rhgc,rchd->rhgd", weights_low, cached_values, preferred_element_type=jnp.float32
    )
    mixture = mixture + own_low[..., None] * value_new[:, :, None, :]
    attn = (mixture / weight_total[..., None]).astype(jnp.bfloat16).reshape(row_count, -1)
    projected_terms = jnp.dot(
        gathered_copies(attn, ("rep", "pair"), 0), out_weight, preferred_element_type=jnp.float32
    )
    projected = sent_and_summed(projected_terms, "head", 0)
    hidden_state = (residual.astype(jnp.float32) + projected).astype(jnp.bfloat16)
    full_rows = gathered_copies(hidden_state, ("rep", "pair"), 1)
    state_f = full_rows.astype(jnp.float32)
    mean_square = jnp.mean(state_f * state_f, axis=1, keepdims=True)
    normed = (state_f * lax.rsqrt(mean_square + 1e-05) * norm_gain).astype(jnp.bfloat16)
    normed_cols = lax.all_to_all(normed, "head", split_axis=1, concat_axis=0, tiled=True)
    gate_part = jnp.dot(normed_cols, gate_weight, preferred_element_type=jnp.float32)
    up_part = jnp.dot(normed_cols, up_weight, preferred_element_type=jnp.float32)
    gate_share, up_share = side_by_side((gate_part, up_part), "head", 1, 0)
    hidden_share = (jax.nn.silu(gate_share) * up_share).astype(jnp.bfloat16)
    hidden = gathered_copies(hidden_share, "head", 1)
    ffn_out = sent_and_summed(
        jnp.dot(hidden, down_weight, preferred_element_type=jnp.float32), ("rep", "pair"), 0
    )
    return (hidden_state, ffn_out.astype(jnp.bfloat16))


def solution(mesh):
    placed = (
        P(("rep", "pair"), "head"),
        P(("rep", "pair"), "head"),
        P(("rep", "pair"), "head"),
        P(("rep", "pair"), None, "head"),
        P(("rep", "pair"), None, "head"),
        P(("rep", "pair")),
        P("head", ("rep", "pair")),
        P(),
        P("head", ("rep", "pair")),
        P("head", ("rep", "pair")),
        P("head", ("rep", "pair")),
        P(("rep", "pair"), "head"),
    )
    return jax.shard_map(
        local,
        mesh=mesh,
        in_specs=placed,
        out_specs=(P("head", ("rep", "pair")), P(("rep", "pair"), "head")),
        check_vma=False,
    )
```

profile of v0, /device:TPU:6, one launch (start us, length us, event | category | flops | bytes accessed | tf_op | source)
XLA Modules:
  0.0 250.5 jit_solution(8546242657127766554)
XLA Ops:
  0.6 0.8 convert_element_type.54
  1.5 0.8 iota_compare_fusion
  2.3 0.8 copy.25
  3.1 0.8 fusion.14
  3.9 1.0 fusion.22
  6.5 39.0 %all_to_all.46 = bf16[32,12,1024]{2,1,0:T(8,128)(2,1)} all-to-all(bf16[32,12,1024]{2,1,0:T(8,128)(2,1)S(1)} %broadcast_in_dim.30), channel_id=1, replica_groups=mesh['rep'=16,'head'=8,'pair'=2] {'rep','pair'}, dimensions={0} | all-to-all | bytes 1572864 | tf_op jit(solution)/shard_map/all_to_all | solution.py:13
  45.6 2.1 dot_general.28
  47.7 1.6 fusion.7
  49.3 13.2 %all_to_all.47 = f32[8,48,256]{2,1,0:T(8,128)S(1)} all-to-all(f32[8,48,256]{2,1,0:T(8,128)S(1)} %fusion.7), channel_id=1, replica_groups=mesh['rep'=16,'head'=8,'pair'=2] {'head'}, dimensions={0} | all-to-all | bytes 786432 | tf_op jit(solution)/shard_map/all_to_all | solution.py:35
  63.2 0.8 add_convert_fusion
  64.0 1.0 broadcast_in_dim.31
  65.0 6.9 %all-to-all-start.2 = ((bf16[32,48,256]{2,1,0:T(8,128)(2,1)}), bf16[32,48,256]{2,1,0:T(8,128)(2,1)}, u32[]{:S(2)}, u32[]{:S(2)}) async-start(bf16[32,48,256]{2,1,0:T(8,128)(2,1)} %broadcast_in_dim.31), calls=%async_computation.2 | async-start | bytes 1572864 | tf_op jit(solution)/shard_map/all_to_all | solution.py:13
  71.9 22.3 %all-to-all-done.2 = bf16[32,48,256]{2,1,0:T(8,128)(2,1)} async-done(((bf16[32,48,256]{2,1,0:T(8,128)(2,1)}), bf16[32,48,256]{2,1,0:T(8,128)(2,1)}, u32[]{:S(2)}, u32[]{:S(2)}) %all-to-all-start.2) | async-done | bytes 786464 | tf_op jit(solution)/shard_map/all_to_all | solution.py:13
  94.2 1.4 fusion.2
  95.6 1.3 convert_bitcast_fusion
  97.0 2.1 copy.17
  99.0 2.7 %reshape.129 = f32[48,8,1024]{2,1,0:T(8,128)} reshape(f32[48,32,256]{2,1,0:T(8,128)} %copy.17) | data formatting | bytes 3145728 | tf_op jit(solution)/shard_map/convert_element_type | solution.py:100
  101.7 1.6 multiply_convert_fusion
  103.8 15.8 %all_to_all.48 = bf16[48,8,1024]{2,0,1:T(8,128)(2,1)S(1)} all-to-all(bf16[48,8,1024]{2,0,1:T(8,128)(2,1)S(1)} %copy.18), channel_id=1, replica_groups=mesh['rep'=16,'head'=8,'pair'=2] {'head'}, dimensions={1} | all-to-all | bytes 1572864 | tf_op jit(solution)/shard_map/all_to_all | solution.py:103
  119.6 1.0 fusion.24
  121.1 1.0 fusion.23
  122.1 1.7 pad_maximum_fusion
  123.8 3.4 %copy.19 = f32[768,896]{0,1:T(8,128)} copy(f32[768,896]{1,0:T(8,128)} %pad_maximum_fusion) | data formatting | bytes 5505024 | tf_op jit(solution)/shard_map/concatenate | solution.py:40
  127.2 39.0 %all_to_all.49 = f32[8,768,112]{1,2,0:T(8,128)} all-to-all(f32[8,768,112]{1,2,0:T(8,128)} %bitcast.45), channel_id=1, replica_groups=mesh['rep'=16,'head'=8,'pair'=2] {'head'}, dimensions={0} | all-to-all | bytes 5505024 | tf_op jit(solution)/shard_map/all_to_all | solution.py:35
  166.2 2.0 reduce_sum.48
  168.3 15.2 %all_to_all.50 = bf16[8,384,112]{1,2,0:T(8,128)(2,1)} all-to-all(bf16[8,384,112]{1,2,0:T(8,128)(2,1)S(1)} %broadcast_in_dim.32), channel_id=1, replica_groups=mesh['rep'=16,'head'=8,'pair'=2] {'head'}, dimensions={0} | all-to-all | bytes 1376256 | tf_op jit(solution)/shard_map/all_to_all | solution.py:13
  183.5 2.4 copy.20
  186.0 2.6 %dot_general.32 = bf16[32,12,896]{2,1,0:T(8,128)(2,1)} reshape(bf16[384,8,112]{2,1,0:T(8,128)(2,1)} %copy.20) | data formatting | bytes 1376256 | tf_op jit(solution)/shard_map/dot_general | solution.py:110
  188.6 2.8 %fusion = f32[32,12,1024]{2,0,1:T(8,128)S(1)} fusion(bf16[896,1024]{1,0:T(8,128)(2,1)} %param.23, bf16[32,12,896]{2,1,0:T(8,128)(2,1)} %dot_general.32), kind=kOutput, calls=%fused_computation.3 | convolution fusion | flops 704643072 | bytes 4096000 | tf_op jit(solution)/shard_map/dot_general | solution.py:110
  191.4 0.9 copy.22
  192.3 55.9 %all_to_all.51 = f32[32,12,1024]{2,1,0:T(8,128)} all-to-all(f32[32,12,1024]{2,1,0:T(8,128)S(1)} %copy.22), channel_id=1, replica_groups=mesh['rep'=16,'head'=8,'pair'=2] {'rep','pair'}, dimensions={0} | all-to-all | bytes 3145728 | tf_op jit(solution)/shard_map/all_to_all | solution.py:35
  248.2 2.3 reduce_sum.49
  (25 shorter events, 3.3 us)
Async XLA Ops:
  0.6 3.3 %copy-start = (bf16[12,1024,128]{2,1,0:T(8,128)(2,1)S(1)}, bf16[12,1024,128]{2,1,0:T(8,128)(2,1)}, u32[]{:S(2)}) copy-start(bf16[12,1024,128]{2,1,0:T(8,128)(2,1)} %param.15) | copy-start | bytes 9437188
  3.9 1.9 copy-start.1
  63.2 8.6 %copy-start.3 = (f32[8192]{0:T(1024)S(1)}, f32[8192]{0:T(1024)}, u32[]{:S(2)}) copy-start(f32[8192]{0:T(1024)} %param.19) | copy-start | bytes 98308
  64.0 33.0 %copy-start.2 = (bf16[48,256]{1,0:T(8,128)(2,1)}, bf16[48,256]{1,0:T(8,128)(2,1)S(1)}, u32[]{:S(2)}) copy-start(bf16[48,256]{1,0:T(8,128)(2,1)S(1)} %add_convert_fusion) | copy-start | bytes 73732
  65.0 29.2 %all-to-all-start.2 = ((bf16[32,48,256]{2,1,0:T(8,128)(2,1)}), bf16[32,48,256]{2,1,0:T(8,128)(2,1)}, u32[]{:S(2)}, u32[]{:S(2)}) async-start(bf16[32,48,256]{2,1,0:T(8,128)(2,1)} %broadcast_in_dim.31), calls=%async_computation.2 | async-start | bytes 1572864 | tf_op jit(solution)/shard_map/all_to_all | solution.py:13
  103.3 16.3 %copy-start.4 = (bf16[1024,896]{1,0:T(8,128)(2,1)S(1)}, bf16[1024,896]{1,0:T(8,128)(2,1)}, u32[]{:S(2)}) copy-start(bf16[1024,896]{1,0:T(8,128)(2,1)} %param.22) | copy-start | bytes 5505028
  119.6 1.5 copy-start.5
where the time goes:
time: 253 us; the launch traced here: 251 us
  blocking collectives  178 us (70%)
  waiting for transfers between devices  22.3 us (9%)
  local copies, waits for them, and re-layouts  19.8 us (8%)
  other arithmetic  13.8 us (5%)
  matrix products  8.74 us (3%)
  starting transfers between devices  6.86 us (3%)
    all_to_all x3, blocking collectives, sent_and_summed(): pieces = lax.all_to_all(cut_along(array, dim, size), axis, 0, 0, tiled=True)  108 us
    all_to_all x2, blocking collectives, sent_to_all(): return lax.all_to_all(copies, axis, split_axis=0, concat_axis=0, tiled=True)  54.2 us
    all_to_all x1, waiting for transfers between devices, sent_to_all(): return lax.all_to_all(copies, axis, split_axis=0, concat_axis=0, tiled=True)  22.3 us
    all_to_all x1, blocking collectives, local(): lax.all_to_all(normed, 'head', split_axis=1, concat_axis=0, tiled=True)  15.8 us
    all_to_all x1, starting transfers between devices, sent_to_all(): return lax.all_to_all(copies, axis, split_axis=0, concat_axis=0, tiled=True)  6.86 us
  transfers between devices with their start and end apart: 1, of which 1 were waited for; matrix products, arithmetic and copies ran while one was open for 0% of the time, Pallas kernels for 0%

commit v1 on v0

v1 whole, which is shorter than its diff:
```python
import jax
import jax.numpy as jnp
from jax import lax
from jax.sharding import Mesh, PartitionSpec as P

HEADS = 64
KV_HEADS = 8
HEAD_DIM = 128
D = 8192
X = ("xh", "xl")
HEAD = ("y", "c")
ALL = ("xh", "z", "y", "c", "xl")
BF = jnp.bfloat16
F4 = jnp.float32


def shift(array, axis, size, step):
    return lax.ppermute(array, axis, [(i, (i + step) % size) for i in range(size)])


def copies_by_a2a(array, axis, size):
    copies = jnp.broadcast_to(array, (size, *array.shape))
    return lax.all_to_all(copies, axis, 0, 0, tiled=True)


def gather4(array, axis, me):
    got = [array] + [shift(array, axis, 4, k) for k in (1, 3, 2)]
    rel = jnp.stack([got[0], got[1], got[3], got[2]])
    return jnp.stack([lax.dynamic_index_in_dim(rel, (me - j) % 4, 0, False) for j in range(4)])


def summed4(pieces, axis, me):
    send = lambda k: lax.dynamic_index_in_dim(pieces, (me + k) % 4, 0, False).astype(BF)
    got = [shift(send(k), axis, 4, k) for k in (1, 3, 2)]
    own = lax.dynamic_index_in_dim(pieces, me, 0, False).astype(F4)
    return own + got[0].astype(F4) + got[1].astype(F4) + got[2].astype(F4)


def swapped(array, axis):
    return lax.ppermute(array, axis, [(0, 1), (1, 0)])


def transpose_perm():
    pairs = []
    for xh in range(2):
        for z in range(8):
            for y in range(4):
                for c in range(2):
                    for xl in range(2):
                        src = (((xh * 8 + z) * 4 + y) * 2 + c) * 2 + xl
                        z2, z1, z0 = z >> 2, (z >> 1) & 1, z & 1
                        nxh, nz = y >> 1, ((y & 1) << 2) | (c << 1) | z0
                        ny, nc = xh * 2 + z2, z1
                        pairs.append((src, (((nxh * 8 + nz) * 4 + ny) * 2 + nc) * 2 + xl))
    return pairs


def attention(queries, new_keys, new_values, key_cache, value_cache, lengths):
    row_count = queries.shape[0]
    slot_count = key_cache.shape[1]
    group_size = HEADS // KV_HEADS
    scale = HEAD_DIM ** (-0.5)
    q = queries.reshape(row_count, group_size, HEAD_DIM)
    scores = jnp.einsum("rgd,rcd->rgc", q, key_cache, preferred_element_type=F4) * scale
    slot_ids = lax.broadcasted_iota(jnp.int32, (row_count, 1, slot_count), 2)
    scores = jnp.where(slot_ids < lengths[:, None, None], scores, -jnp.inf)
    own_score = jnp.einsum("rgd,rd->rg", q, new_keys, preferred_element_type=F4) * scale
    top = jnp.maximum(jnp.max(scores, axis=2), own_score)
    weights = jnp.exp(scores - top[..., None])
    own_weight = jnp.exp(own_score - top)
    total = jnp.sum(weights, axis=2) + own_weight
    own_low = own_weight.astype(BF).astype(F4)
    mixture = jnp.einsum("rgc,rcd->rgd", weights.astype(BF), value_cache, preferred_element_type=F4)
    mixture = mixture + own_low[..., None] * new_values.astype(F4)[:, None, :]
    return (mixture / total[..., None]).astype(BF).reshape(row_count, -1)


def local(
    queries,
    new_keys,
    new_values,
    key_cache,
    value_cache,
    lengths,
    residual,
    norm_gain,
    out_weight,
    gate_weight,
    up_weight,
    down_weight,
):
    x = lax.axis_index("xh") * 2 + lax.axis_index("xl")
    y = lax.axis_index("y")
    c = lax.axis_index("c")
    head = y * 2 + c
    res = residual.reshape(2, 2, 12, 256).swapaxes(0, 1).reshape(48, 256).astype(F4)
    gain = lax.dynamic_slice_in_dim(norm_gain, head * 1024, 1024, 0)

    attn = attention(queries, new_keys, new_values, key_cache, value_cache, lengths)
    along_z = copies_by_a2a(attn, "z", 8).reshape(96, 1024)
    rows = gather4(along_z, X, x)
    projected = jnp.dot(rows.reshape(384, 1024), out_weight, preferred_element_type=F4)
    pieces = projected.astype(BF).reshape(2, 2, 4, 24, 256).swapaxes(1, 2).reshape(8, 48, 256)
    pieces = lax.all_to_all(pieces, HEAD, 0, 0, tiled=True)
    state = (res + jnp.sum(pieces.astype(F4), axis=0)).astype(BF)
    hidden_state = state.reshape(2, 2, 12, 256).swapaxes(0, 1).reshape(48, 256)

    moved = lax.ppermute(state, ALL, transpose_perm())
    along_z = copies_by_a2a(moved, "z", 8)
    along_z = along_z.reshape(4, 2, 48, 256).swapaxes(1, 2).reshape(192, 512)
    full = gather4(along_z, X, x).reshape(2, 2, 192, 2, 256)
    full = full.transpose(0, 2, 3, 1, 4).reshape(384, 1024)
    full_f = full.astype(F4)
    squares = jnp.sum(full_f * full_f, axis=1, keepdims=True)
    scaled = (full_f * gain).astype(BF)
    gate = jnp.dot(scaled, gate_weight, preferred_element_type=F4)
    up = jnp.dot(scaled, up_weight, preferred_element_type=F4)
    sq_hi = squares.astype(BF)
    sq_lo = (squares - sq_hi.astype(F4)).astype(BF)
    lanes = lax.broadcasted_iota(jnp.int32, (1, 128), 1)
    sq = jnp.where(lanes == 0, sq_hi.astype(F4), jnp.where(lanes == 1, sq_lo.astype(F4), 0.0))
    both = jnp.concatenate([gate, up, sq], axis=1)
    both = both.reshape(4, 2, 48, 1920)
    other = lax.dynamic_index_in_dim(both, 1 - c, 1, False).astype(BF)
    mine = lax.dynamic_index_in_dim(both, c, 1, False)
    pair_sum = mine + swapped(other, "c").astype(F4)
    share = summed4(pair_sum, "y", y)
    mean_square = jnp.sum(share[:, 1792:], axis=1, keepdims=True) / D
    inv = lax.rsqrt(mean_square + 1e-05)
    gate = share[:, :896] * inv
    up = share[:, 896:1792] * inv
    hidden = (jax.nn.silu(gate) * up).astype(BF)
    hidden = gather4(hidden, "y", y)
    theirs = swapped(hidden, "c")
    both = jnp.stack([jnp.where(c == 0, hidden, theirs), jnp.where(c == 0, theirs, hidden)], axis=1)
    hidden = both.reshape(384, 896)

    part = jnp.dot(hidden, down_weight, preferred_element_type=F4)
    part = part.reshape(2, 4, 2, 24, 1024).swapaxes(1, 2).reshape(4, 96, 1024)
    part = summed4(part, X, x).astype(BF).reshape(8, 12, 1024)
    part = lax.all_to_all(part, "z", 0, 0, tiled=True)
    ffn_out = jnp.sum(part.astype(F4), axis=0).astype(BF)
    return (hidden_state, ffn_out)


def solution(mesh):
    fine = Mesh(mesh.devices.reshape(2, 8, 4, 2, 2), ALL)
    plane = ("xh", "z", "xl")
    placed = (
        P(plane, HEAD),
        P(plane, HEAD),
        P(plane, HEAD),
        P(plane, None, HEAD),
        P(plane, None, HEAD),
        P(plane),
        P(HEAD, plane),
        P(),
        P(HEAD, plane),
        P(HEAD, plane),
        P(HEAD, plane),
        P(plane, HEAD),
    )
    return jax.shard_map(
        local,
        mesh=fine,
        in_specs=placed,
        out_specs=(P(HEAD, plane), P(plane, HEAD)),
        check_vma=False,
    )
```

time: 253 us -> 182 us (0.72)
  blocking collectives: 178 us -> 37.2 us
  waiting for transfers between devices: 22.3 us -> 65.6 us
  starting transfers between devices: 6.86 us -> 26.8 us
  local copies, waits for them, and re-layouts: 19.8 us -> 26.8 us
    all_to_all x6 -> x2, blocking collectives: 178 us -> 37.2 us  [copies_by_a2a(): return lax.all_to_all(copies, axis, 0, 0, tiled=True)]
    ppermute x0 -> x18, waiting for transfers between devices: none -> 48.7 us  [the longest x15 37.9 us: shift(): lax.ppermute(array, axis, [(i, (i + step) % size) for i in range(size)])]
    ppermute x0 -> x18, starting transfers between devices: none -> 18.9 us  [the longest x15 15.6 us: shift(): lax.ppermute(array, axis, [(i, (i + step) % size) for i in range(size)])]
    convert_element_type x3 -> x9, local copies, waits for them, and re-layouts: 5.18 us -> 12.8 us  [the longest x3 10.2 us: local(): full_f = full.astype(F4)]
    unnamed x15 -> x34, local copies, waits for them, and re-layouts: 1.96 us -> 8.39 us
    dot_general x3 -> x0, local copies, waits for them, and re-layouts: 5.72 us -> none  [the longest x2 3.58 us: local(): jnp.dot(hidden, down_weight, preferred_element_type=jnp.float32)]
    all_to_all x1 -> x2, waiting for transfers between devices: 22.3 us -> 16.9 us  [the longest x1 10.1 us: local(): part = lax.all_to_all(part, 'z', 0, 0, tiled=True)]
    reduce_sum x5 -> x6, other arithmetic: 6.55 us -> 1.28 us  [the longest x1 0.66 us: local(): ffn_out = jnp.sum(part.astype(F4), axis=0).astype(BF)]
  transfers between devices with their start and end apart: 1 -> 20, of which waited for: 1 -> 17; matrix products, arithmetic and copies ran while one was open for 0% -> 2% of each run, Pallas kernels for 0% -> 0%
where the time goes in v1:
time: 182 us; the launch traced here: 179 us
  waiting for transfers between devices  65.6 us (36%)
  blocking collectives  37.2 us (20%)
  local copies, waits for them, and re-layouts  26.8 us (15%)
  starting transfers between devices  26.8 us (15%)
  other arithmetic  13.9 us (8%)
  matrix products  7.8 us (4%)
    ppermute x15, waiting for transfers between devices, shift(): lax.ppermute(array, axis, [(i, (i + step) % size) for i in range(size)])  37.9 us
    all_to_all x2, blocking collectives, copies_by_a2a(): return lax.all_to_all(copies, axis, 0, 0, tiled=True)  37.2 us
    ppermute x15, starting transfers between devices, shift(): lax.ppermute(array, axis, [(i, (i + step) % size) for i in range(size)])  15.6 us
    convert_element_type x3, local copies, waits for them, and re-layouts, local(): full_f = full.astype(F4)  10.2 us
    all_to_all x1, waiting for transfers between devices, local(): part = lax.all_to_all(part, 'z', 0, 0, tiled=True)  10.1 us
    unnamed x34, local copies, waits for them, and re-layouts  8.39 us
    all_to_all x1, waiting for transfers between devices, local(): pieces = lax.all_to_all(pieces, HEAD, 0, 0, tiled=True)  6.78 us
    ppermute x1, waiting for transfers between devices, local(): moved = lax.ppermute(state, ALL, transpose_perm())  6.32 us
  transfers between devices with their start and end apart: 20, of which 17 were waited for; matrix products, arithmetic and copies ran while one was open for 2% of the time, Pallas kernels for 0%

profile of v1, /device:TPU:6, one launch (start us, length us, event | category | flops | bytes accessed | tf_op | source)
XLA Modules:
  0.0 179.2 jit_solution(9302000588015182439)
XLA Ops:
  5.7 20.1 %all_to_all.20 = bf16[8,12,1024]{2,1,0:T(8,128)(2,1)S(1)} all-to-all(bf16[8,12,1024]{2,1,0:T(8,128)(2,1)S(1)} %broadcast_in_dim.64), channel_id=1, replica_groups=mesh['xh'=2,'z'=8,'y'=4,'c'=2,'xl'=2] {'z'}, dimensions={0} | all-to-all | bytes 393216 | tf_op jit(solution)/shard_map/all_to_all | solution.py:23
  28.5 2.1 %collective-permute-start = (bf16[96,1024]{1,0:T(8,128)(2,1)}, bf16[96,1024]{1,0:T(8,128)(2,1)}, u32[]{:S(2)}, u32[]{:S(2)}) collective-permute-start(bf16[96,1024]{1,0:T(8,128)(2,1)} %reshape.136), channel_id=1, source_target_pairs={{0,1},{1,128},{128,129},{129,0},{2,3},{3,130},{130,131},{131,2},{4... | collective-permute-start | bytes 589832 | tf_op jit(solution)/shard_map/ppermute | solution.py:18
  31.3 5.8 %collective-permute-done.2 = bf16[96,1024]{1,0:T(8,128)(2,1)} collective-permute-done((bf16[96,1024]{1,0:T(8,128)(2,1)}, bf16[96,1024]{1,0:T(8,128)(2,1)}, u32[]{:S(2)}, u32[]{:S(2)}) %collective-permute-start.2) | collective-permute-done | bytes 196640 | tf_op jit(solution)/shard_map/ppermute | solution.py:18
  37.8 1.3 pad_maximum_fusion.1
  41.3 4.5 %all-to-all-start.1 = ((bf16[8,48,256]{2,1,0:T(8,128)(2,1)}), bf16[8,48,256]{2,1,0:T(8,128)(2,1)S(1)}, u32[]{:S(2)}, u32[]{:S(2)}) async-start(bf16[8,48,256]{2,1,0:T(8,128)(2,1)} %bitcast.9), calls=%async_computation.1 | async-start | bytes 393216 | tf_op jit(solution)/shard_map/all_to_all | solution.py:104
  45.8 6.8 %all-to-all-done.1 = bf16[8,48,256]{2,1,0:T(8,128)(2,1)S(1)} async-done(((bf16[8,48,256]{2,1,0:T(8,128)(2,1)}), bf16[8,48,256]{2,1,0:T(8,128)(2,1)S(1)}, u32[]{:S(2)}, u32[]{:S(2)}) %all-to-all-start.1) | async-done | bytes 196640 | tf_op jit(solution)/shard_map/all_to_all | solution.py:104
  52.6 3.3 %collective-permute-start.3 = (bf16[48,256]{1,0:T(8,128)(2,1)S(1)}, bf16[48,256]{1,0:T(8,128)(2,1)S(1)}, u32[]{:S(2)}, u32[]{:S(2)}) collective-permute-start(bf16[48,256]{1,0:T(8,128)(2,1)S(1)} %add_convert_fusion), channel_id=1, source_target_pairs={{0,0},{1,1},{2,32},{3,33},{4,64},{5,65},{6,96},{7,97},{8,128},{9,1... | collective-permute-start | bytes 73736 | tf_op jit(solution)/shard_map/ppermute | solution.py:108
  55.9 6.3 %collective-permute-done.3 = bf16[48,256]{1,0:T(8,128)(2,1)S(1)} collective-permute-done((bf16[48,256]{1,0:T(8,128)(2,1)S(1)}, bf16[48,256]{1,0:T(8,128)(2,1)S(1)}, u32[]{:S(2)}, u32[]{:S(2)}) %collective-permute-start.3) | collective-permute-done | bytes 24608 | tf_op jit(solution)/shard_map/ppermute | solution.py:108
  62.3 17.1 %all_to_all.21 = bf16[8,48,256]{2,1,0:T(8,128)(2,1)S(1)} all-to-all(bf16[8,48,256]{2,1,0:T(8,128)(2,1)S(1)} %broadcast_in_dim.65), channel_id=1, replica_groups=mesh['xh'=2,'z'=8,'y'=4,'c'=2,'xl'=2] {'z'}, dimensions={0} | all-to-all | bytes 393216 | tf_op jit(solution)/shard_map/all_to_all | solution.py:23
  81.0 2.7 %collective-permute-start.4 = (bf16[192,512]{1,0:T(8,128)(2,1)}, bf16[192,512]{1,0:T(8,128)(2,1)}, u32[]{:S(2)}, u32[]{:S(2)}) collective-permute-start(bf16[192,512]{1,0:T(8,128)(2,1)} %bitcast.50), channel_id=1, source_target_pairs={{0,1},{1,128},{128,129},{129,0},{2,3},{3,130},{130,131},{131,2},{4... | collective-permute-start | bytes 589832 | tf_op jit(solution)/shard_map/ppermute | solution.py:18
  84.5 5.3 %collective-permute-done.6 = bf16[192,512]{1,0:T(8,128)(2,1)} collective-permute-done((bf16[192,512]{1,0:T(8,128)(2,1)}, bf16[192,512]{1,0:T(8,128)(2,1)}, u32[]{:S(2)}, u32[]{:S(2)}) %collective-permute-start.6) | collective-permute-done | bytes 196640 | tf_op jit(solution)/shard_map/ppermute | solution.py:18
  93.4 3.1 %reshape.150 = f32[2,2,192,2,256]{4,3,2,1,0:T(2,128)} reshape(f32[4,192,512]{2,1,0:T(8,128)} %maximum_convert_fusion) | data formatting | bytes 3145728 | tf_op jit(solution)/shard_map/convert_element_type | solution.py:113
  96.4 3.8 %copy.66 = f32[2,2,192,2,256]{4,1,3,2,0:T(2,128)} copy(f32[2,2,192,2,256]{4,3,2,1,0:T(2,128)} %reshape.150) | data formatting | bytes 3145728 | tf_op jit(solution)/shard_map/convert_element_type | solution.py:113
  100.2 3.3 %reshape.147 = f32[384,1024]{1,0:T(8,128)} reshape(f32[2,192,2,2,256]{4,3,2,1,0:T(2,128)} %bitcast.107) | data formatting | bytes 3145728 | tf_op jit(solution)/shard_map/convert_element_type | solution.py:113
  103.5 3.1 %fusion.16 = f32[384,896]{1,0:T(8,128)S(1)} fusion(bf16[1024,896]{1,0:T(8,128)(2,1)} %param.22, f32[384,1024]{1,0:T(8,128)} %reshape.147, f32[1024]{0:T(1024)S(1)} %dynamic_slice.83), kind=kOutput, calls=%fused_computation.42 | convolution fusion | flops 705429504 | bytes 4788224 | tf_op jit(solution)/shard_map/dot_general | solution.py:117
  108.0 1.6 copy-done.1
  110.6 2.6 %collective-permute-done.7 = bf16[4,48,1920]{2,1,0:T(8,128)(2,1)} collective-permute-done((bf16[4,48,1920]{2,1,0:T(8,128)(2,1)}, bf16[4,48,1920]{2,1,0:T(8,128)(2,1)}, u32[]{:S(2)}, u32[]{:S(2)}) %collective-permute-start.7) | collective-permute-done | bytes 737312 | tf_op jit(solution)/shard_map/ppermute | solution.py:40
  113.1 1.7 bitcast_add_fusion
  116.8 1.6 collective-permute-start.9
  118.8 7.2 %collective-permute-done.10 = bf16[48,1920]{1,0:T(8,128)(2,1)S(1)} collective-permute-done((bf16[48,1920]{1,0:T(8,128)(2,1)}, bf16[48,1920]{1,0:T(8,128)(2,1)S(1)}, u32[]{:S(2)}, u32[]{:S(2)}) %collective-permute-start.10) | collective-permute-done | bytes 184352 | tf_op jit(solution)/shard_map/ppermute | solution.py:18
  126.0 1.3 collective-permute-done.9
  127.3 1.9 %collective-permute-done.8 = bf16[48,1920]{1,0:T(8,128)(2,1)} collective-permute-done((bf16[48,1920]{1,0:T(8,128)(2,1)S(1)}, bf16[48,1920]{1,0:T(8,128)(2,1)}, u32[]{:S(2)}, u32[]{:S(2)}) %collective-permute-start.8) | collective-permute-done | bytes 184352 | tf_op jit(solution)/shard_map/ppermute | solution.py:18
  133.0 3.2 %collective-permute-done.13 = bf16[48,896]{1,0:T(8,128)(2,1)S(1)} collective-permute-done((bf16[48,896]{1,0:T(8,128)(2,1)S(1)}, bf16[48,896]{1,0:T(8,128)(2,1)S(1)}, u32[]{:S(2)}, u32[]{:S(2)}) %collective-permute-start.13) | collective-permute-done | bytes 86048 | tf_op jit(solution)/shard_map/ppermute | solution.py:18
  136.2 1.9 %collective-permute-done.12 = bf16[48,896]{1,0:T(8,128)(2,1)S(1)} collective-permute-done((bf16[48,896]{1,0:T(8,128)(2,1)S(1)}, bf16[48,896]{1,0:T(8,128)(2,1)S(1)}, u32[]{:S(2)}, u32[]{:S(2)}) %collective-permute-start.12) | collective-permute-done | bytes 86048 | tf_op jit(solution)/shard_map/ppermute | solution.py:18
  140.0 2.0 %collective-permute-done.14 = bf16[4,48,896]{2,1,0:T(8,128)(2,1)} collective-permute-done((bf16[4,48,896]{2,1,0:T(8,128)(2,1)}, bf16[4,48,896]{2,1,0:T(8,128)(2,1)}, u32[]{:S(2)}, u32[]{:S(2)}) %collective-permute-start.14) | collective-permute-done | bytes 344096 | tf_op jit(solution)/shard_map/ppermute | solution.py:40
  143.2 1.3 copy-done.14
  148.5 2.3 %collective-permute-start.16 = (bf16[96,1024]{1,0:T(8,128)(2,1)}, bf16[96,1024]{1,0:T(8,128)(2,1)}, u32[]{:S(2)}, u32[]{:S(2)}) collective-permute-start(bf16[96,1024]{1,0:T(8,128)(2,1)} %get-tuple-element.4), channel_id=1, source_target_pairs={{0,129},{1,0},{128,1},{129,128},{2,131},{3,2},{130,3},{131,130},{4... | collective-permute-start | bytes 589832 | tf_op jit(solution)/shard_map/ppermute | solution.py:18
  151.8 5.6 %collective-permute-done.17 = bf16[96,1024]{1,0:T(8,128)(2,1)} collective-permute-done((bf16[96,1024]{1,0:T(8,128)(2,1)}, bf16[96,1024]{1,0:T(8,128)(2,1)}, u32[]{:S(2)}, u32[]{:S(2)}) %collective-permute-start.17) | collective-permute-done | bytes 196640 | tf_op jit(solution)/shard_map/ppermute | solution.py:18
  157.4 3.4 %collective-permute-done.16 = bf16[96,1024]{1,0:T(8,128)(2,1)} collective-permute-done((bf16[96,1024]{1,0:T(8,128)(2,1)}, bf16[96,1024]{1,0:T(8,128)(2,1)}, u32[]{:S(2)}, u32[]{:S(2)}) %collective-permute-start.16) | collective-permute-done | bytes 196640 | tf_op jit(solution)/shard_map/ppermute | solution.py:18
  160.7 1.4 fusion.11
  162.9 3.4 %all-to-all-start.3 = ((bf16[8,12,1024]{2,1,0:T(8,128)(2,1)}), bf16[8,12,1024]{2,1,0:T(8,128)(2,1)S(1)}, u32[]{:S(2)}, u32[]{:S(2)}) async-start(bf16[8,12,1024]{2,1,0:T(8,128)(2,1)} %reshape.145), calls=%async_computation.3 | async-start | bytes 524288 | tf_op jit(solution)/shard_map/all_to_all | solution.py:141
  168.4 10.1 %all-to-all-done.3 = bf16[8,12,1024]{2,1,0:T(8,128)(2,1)S(1)} async-done(((bf16[8,12,1024]{2,1,0:T(8,128)(2,1)}), bf16[8,12,1024]{2,1,0:T(8,128)(2,1)S(1)}, u32[]{:S(2)}, u32[]{:S(2)}) %all-to-all-start.3) | async-done | bytes 196640 | tf_op jit(solution)/shard_map/all_to_all | solution.py:141
  (108 shorter events, 37.1 us)
Async XLA Ops:
  0.6 2.5 %copy-start = (bf16[12,1024,128]{2,1,0:T(8,128)(2,1)S(1)}, bf16[12,1024,128]{2,1,0:T(8,128)(2,1)}, u32[]{:S(2)}) copy-start(bf16[12,1024,128]{2,1,0:T(8,128)(2,1)} %param.15) | copy-start | bytes 9437188
  3.1 1.3 copy-start.12
  3.2 1.9 %copy-start.4 = (bf16[12,1024,128]{2,1,0:T(8,128)(2,1)S(1)}, bf16[12,1024,128]{2,1,0:T(8,128)(2,1)}, u32[]{:S(2)}) copy-start(bf16[12,1024,128]{2,1,0:T(8,128)(2,1)} %param.16) | copy-start | bytes 9437188
  26.6 10.6 %collective-permute-start.2 = (bf16[96,1024]{1,0:T(8,128)(2,1)}, bf16[96,1024]{1,0:T(8,128)(2,1)}, u32[]{:S(2)}, u32[]{:S(2)}) collective-permute-start(bf16[96,1024]{1,0:T(8,128)(2,1)} %reshape.136), channel_id=1, source_target_pairs={{0,129},{1,0},{128,1},{129,128},{2,131},{3,2},{130,3},{131,130},{4... | collective-permute-start | bytes 589832 | tf_op jit(solution)/shard_map/ppermute | solution.py:18
  27.4 9.8 %collective-permute-start.1 = (bf16[96,1024]{1,0:T(8,128)(2,1)}, bf16[96,1024]{1,0:T(8,128)(2,1)}, u32[]{:S(2)}, u32[]{:S(2)}) collective-permute-start(bf16[96,1024]{1,0:T(8,128)(2,1)} %reshape.136), channel_id=1, source_target_pairs={{0,128},{1,129},{128,0},{129,1},{2,130},{3,131},{130,2},{131,3},{4... | collective-permute-start | bytes 589832 | tf_op jit(solution)/shard_map/ppermute | solution.py:18
  28.5 9.3 %collective-permute-start = (bf16[96,1024]{1,0:T(8,128)(2,1)}, bf16[96,1024]{1,0:T(8,128)(2,1)}, u32[]{:S(2)}, u32[]{:S(2)}) collective-permute-start(bf16[96,1024]{1,0:T(8,128)(2,1)} %reshape.136), channel_id=1, source_target_pairs={{0,1},{1,128},{128,129},{129,0},{2,3},{3,130},{130,131},{131,2},{4... | collective-permute-start | bytes 589832 | tf_op jit(solution)/shard_map/ppermute | solution.py:18
  39.2 6.5 %copy-start.11 = (bf16[48,256]{1,0:T(8,128)(2,1)S(1)}, bf16[48,256]{1,0:T(8,128)(2,1)}, u32[]{:S(2)}) copy-start(bf16[48,256]{1,0:T(8,128)(2,1)} %param.18) | copy-start | bytes 73732
  41.3 11.3 %all-to-all-start.1 = ((bf16[8,48,256]{2,1,0:T(8,128)(2,1)}), bf16[8,48,256]{2,1,0:T(8,128)(2,1)S(1)}, u32[]{:S(2)}, u32[]{:S(2)}) async-start(bf16[8,48,256]{2,1,0:T(8,128)(2,1)} %bitcast.9), calls=%async_computation.1 | async-start | bytes 393216 | tf_op jit(solution)/shard_map/all_to_all | solution.py:104
  45.7 38.6 %copy-start.6 = (f32[2,2,12,256]{3,2,1,0:T(8,128)}, f32[2,2,12,256]{3,2,1,0:T(8,128)S(1)}, u32[]{:S(2)}) copy-start(f32[2,2,12,256]{3,2,1,0:T(8,128)S(1)} %reshape.148) | copy-start | bytes 147460
  52.6 3.3 %copy-start.9 = (f32[48,256]{1,0:T(8,128)}, f32[48,256]{1,0:T(8,128)S(1)}, u32[]{:S(2)}) copy-start(f32[48,256]{1,0:T(8,128)S(1)} %convert_reduce_fusion) | copy-start | bytes 147460
  52.6 9.6 %collective-permute-start.3 = (bf16[48,256]{1,0:T(8,128)(2,1)S(1)}, bf16[48,256]{1,0:T(8,128)(2,1)S(1)}, u32[]{:S(2)}, u32[]{:S(2)}) collective-permute-start(bf16[48,256]{1,0:T(8,128)(2,1)S(1)} %add_convert_fusion), channel_id=1, source_target_pairs={{0,0},{1,1},{2,32},{3,33},{4,64},{5,65},{6,96},{7,97},{8,128},{9,1... | collective-permute-start | bytes 73736 | tf_op jit(solution)/shard_map/ppermute | solution.py:108
  80.2 9.6 %collective-permute-start.6 = (bf16[192,512]{1,0:T(8,128)(2,1)}, bf16[192,512]{1,0:T(8,128)(2,1)}, u32[]{:S(2)}, u32[]{:S(2)}) collective-permute-start(bf16[192,512]{1,0:T(8,128)(2,1)} %bitcast.50), channel_id=1, source_target_pairs={{0,129},{1,0},{128,1},{129,128},{2,131},{3,2},{130,3},{131,130},{4... | collective-permute-start | bytes 589832 | tf_op jit(solution)/shard_map/ppermute | solution.py:18
  81.0 8.8 %collective-permute-start.5 = (bf16[192,512]{1,0:T(8,128)(2,1)}, bf16[192,512]{1,0:T(8,128)(2,1)}, u32[]{:S(2)}, u32[]{:S(2)}) collective-permute-start(bf16[192,512]{1,0:T(8,128)(2,1)} %bitcast.50), channel_id=1, source_target_pairs={{0,128},{1,129},{128,0},{129,1},{2,130},{3,131},{130,2},{131,3},{4... | collective-permute-start | bytes 589832 | tf_op jit(solution)/shard_map/ppermute | solution.py:18
  81.0 9.4 %collective-permute-start.4 = (bf16[192,512]{1,0:T(8,128)(2,1)}, bf16[192,512]{1,0:T(8,128)(2,1)}, u32[]{:S(2)}, u32[]{:S(2)}) collective-permute-start(bf16[192,512]{1,0:T(8,128)(2,1)} %bitcast.50), channel_id=1, source_target_pairs={{0,1},{1,128},{128,129},{129,0},{2,3},{3,130},{130,131},{131,2},{4... | collective-permute-start | bytes 589832 | tf_op jit(solution)/shard_map/ppermute | solution.py:18
  103.5 3.1 %copy-start.5 = (f32[384,1024]{1,0:T(8,128)S(1)}, f32[384,1024]{1,0:T(8,128)}, u32[]{:S(2)}) copy-start(f32[384,1024]{1,0:T(8,128)} %reshape.147) | copy-start | bytes 4718596
  103.5 3.1 %copy-start.13 = (bf16[1024,896]{1,0:T(8,128)(2,1)S(1)}, bf16[1024,896]{1,0:T(8,128)(2,1)}, u32[]{:S(2)}) copy-start(bf16[1024,896]{1,0:T(8,128)(2,1)} %param.21) | copy-start | bytes 5505028
  108.0 1.6 copy-start.1
  110.5 2.6 %collective-permute-start.7 = (bf16[4,48,1920]{2,1,0:T(8,128)(2,1)}, bf16[4,48,1920]{2,1,0:T(8,128)(2,1)}, u32[]{:S(2)}, u32[]{:S(2)}) collective-permute-start(bf16[4,48,1920]{2,1,0:T(8,128)(2,1)} %fusion.8), channel_id=1, source_target_pairs={{0,2},{2,0},{1,3},{3,1},{4,6},{6,4},{5,7},{7,5},{8,10},{10,8},{9,1... | collective-permute-start | bytes 2211848 | tf_op jit(solution)/shard_map/ppermute | solution.py:40
  116.8 9.2 %collective-permute-start.10 = (bf16[48,1920]{1,0:T(8,128)(2,1)}, bf16[48,1920]{1,0:T(8,128)(2,1)S(1)}, u32[]{:S(2)}, u32[]{:S(2)}) collective-permute-start(bf16[48,1920]{1,0:T(8,128)(2,1)} %get-tuple-element.6), channel_id=1, source_target_pairs={{0,8},{4,12},{8,0},{12,4},{1,9},{5,13},{9,1},{13,5},{2,10},{6,14},... | collective-permute-start | bytes 552968 | tf_op jit(solution)/shard_map/ppermute | solution.py:18
  116.8 10.5 %collective-permute-start.9 = (bf16[48,1920]{1,0:T(8,128)(2,1)}, bf16[48,1920]{1,0:T(8,128)(2,1)}, u32[]{:S(2)}, u32[]{:S(2)}) collective-permute-start(bf16[48,1920]{1,0:T(8,128)(2,1)} %get-tuple-element.7), channel_id=1, source_target_pairs={{0,12},{4,0},{8,4},{12,8},{1,13},{5,1},{9,5},{13,9},{2,14},{6,2},{... | collective-permute-start | bytes 552968 | tf_op jit(solution)/shard_map/ppermute | solution.py:18
  118.4 10.8 %collective-permute-start.8 = (bf16[48,1920]{1,0:T(8,128)(2,1)S(1)}, bf16[48,1920]{1,0:T(8,128)(2,1)}, u32[]{:S(2)}, u32[]{:S(2)}) collective-permute-start(bf16[48,1920]{1,0:T(8,128)(2,1)S(1)} %get-tuple-element.5), channel_id=1, source_target_pairs={{0,4},{4,8},{8,12},{12,0},{1,5},{5,9},{9,13},{13,1},{2,6},{6,10},{... | collective-permute-start | bytes 552968 | tf_op jit(solution)/shard_map/ppermute | solution.py:18
  130.8 5.5 %collective-permute-start.13 = (bf16[48,896]{1,0:T(8,128)(2,1)S(1)}, bf16[48,896]{1,0:T(8,128)(2,1)S(1)}, u32[]{:S(2)}, u32[]{:S(2)}) collective-permute-start(bf16[48,896]{1,0:T(8,128)(2,1)S(1)} %fusion.27), channel_id=1, source_target_pairs={{0,12},{4,0},{8,4},{12,8},{1,13},{5,1},{9,5},{13,9},{2,14},{6,2},{... | collective-permute-start | bytes 258056 | tf_op jit(solution)/shard_map/ppermute | solution.py:18
  131.6 6.6 %collective-permute-start.12 = (bf16[48,896]{1,0:T(8,128)(2,1)S(1)}, bf16[48,896]{1,0:T(8,128)(2,1)S(1)}, u32[]{:S(2)}, u32[]{:S(2)}) collective-permute-start(bf16[48,896]{1,0:T(8,128)(2,1)S(1)} %fusion.27), channel_id=1, source_target_pairs={{0,8},{4,12},{8,0},{12,4},{1,9},{5,13},{9,1},{13,5},{2,10},{6,14},... | collective-permute-start | bytes 258056 | tf_op jit(solution)/shard_map/ppermute | solution.py:18
  131.9 7.2 %collective-permute-start.11 = (bf16[48,896]{1,0:T(8,128)(2,1)S(1)}, bf16[48,896]{1,0:T(8,128)(2,1)S(1)}, u32[]{:S(2)}, u32[]{:S(2)}) collective-permute-start(bf16[48,896]{1,0:T(8,128)(2,1)S(1)} %fusion.27), channel_id=1, source_target_pairs={{0,4},{4,8},{8,12},{12,0},{1,5},{5,9},{9,13},{13,1},{2,6},{6,10},{... | collective-permute-start | bytes 258056 | tf_op jit(solution)/shard_map/ppermute | solution.py:18
  140.0 2.0 %collective-permute-start.14 = (bf16[4,48,896]{2,1,0:T(8,128)(2,1)}, bf16[4,48,896]{2,1,0:T(8,128)(2,1)}, u32[]{:S(2)}, u32[]{:S(2)}) collective-permute-start(bf16[4,48,896]{2,1,0:T(8,128)(2,1)} %pad_maximum_fusion.6), channel_id=1, source_target_pairs={{0,2},{2,0},{1,3},{3,1},{4,6},{6,4},{5,7},{7,5},{8,10},{10,8},{9,1... | collective-permute-start | bytes 1032200 | tf_op jit(solution)/shard_map/ppermute | solution.py:40
  143.1 1.5 copy-start.14
  146.9 19.4 %copy-start.10 = (f32[48,256]{1,0:T(8,128)S(1)}, f32[48,256]{1,0:T(8,128)}, u32[]{:S(2)}) copy-start(f32[48,256]{1,0:T(8,128)} %copy-done.9) | copy-start | bytes 147460
  146.9 20.0 %copy-start.7 = (f32[2,2,12,256]{3,2,1,0:T(8,128)S(1)}, f32[2,2,12,256]{3,2,1,0:T(8,128)}, u32[]{:S(2)}) copy-start(f32[2,2,12,256]{3,2,1,0:T(8,128)} %copy-done.6) | copy-start | bytes 147460
  147.8 9.6 %collective-permute-start.17 = (bf16[96,1024]{1,0:T(8,128)(2,1)}, bf16[96,1024]{1,0:T(8,128)(2,1)}, u32[]{:S(2)}, u32[]{:S(2)}) collective-permute-start(bf16[96,1024]{1,0:T(8,128)(2,1)} %get-tuple-element.3), channel_id=1, source_target_pairs={{0,128},{1,129},{128,0},{129,1},{2,130},{3,131},{130,2},{131,3},{4... | collective-permute-start | bytes 589832 | tf_op jit(solution)/shard_map/ppermute | solution.py:18
  148.5 12.2 %collective-permute-start.16 = (bf16[96,1024]{1,0:T(8,128)(2,1)}, bf16[96,1024]{1,0:T(8,128)(2,1)}, u32[]{:S(2)}, u32[]{:S(2)}) collective-permute-start(bf16[96,1024]{1,0:T(8,128)(2,1)} %get-tuple-element.4), channel_id=1, source_target_pairs={{0,129},{1,0},{128,1},{129,128},{2,131},{3,2},{130,3},{131,130},{4... | collective-permute-start | bytes 589832 | tf_op jit(solution)/shard_map/ppermute | solution.py:18
  150.8 9.9 %collective-permute-start.15 = (bf16[96,1024]{1,0:T(8,128)(2,1)S(1)}, bf16[96,1024]{1,0:T(8,128)(2,1)}, u32[]{:S(2)}, u32[]{:S(2)}) collective-permute-start(bf16[96,1024]{1,0:T(8,128)(2,1)S(1)} %get-tuple-element.2), channel_id=1, source_target_pairs={{0,1},{1,128},{128,129},{129,0},{2,3},{3,130},{130,131},{131,2},{4... | collective-permute-start | bytes 589832 | tf_op jit(solution)/shard_map/ppermute | solution.py:18
  162.9 15.7 %all-to-all-start.3 = ((bf16[8,12,1024]{2,1,0:T(8,128)(2,1)}), bf16[8,12,1024]{2,1,0:T(8,128)(2,1)S(1)}, u32[]{:S(2)}, u32[]{:S(2)}) async-start(bf16[8,12,1024]{2,1,0:T(8,128)(2,1)} %reshape.145), calls=%async_computation.3 | async-start | bytes 524288 | tf_op jit(solution)/shard_map/all_to_all | solution.py:141
  (3 other events, 3.4 us)

commit v2 on v1

--- a/solution.py
+++ b/solution.py
@@ -1,6 +1,8 @@
 import jax
 import jax.numpy as jnp
 from jax import lax
+from jax.experimental import pallas as pl
+from jax.experimental.pallas import tpu as pltpu
 from jax.sharding import Mesh, PartitionSpec as P
 
 HEADS = 64
@@ -75,6 +77,143 @@
     return (mixture / total[..., None]).astype(BF).reshape(row_count, -1)
 
 
+VM = pl.BlockSpec(memory_space=pltpu.VMEM)
+SM = pl.BlockSpec(memory_space=pltpu.SMEM)
+N_CUTS = ((0, 256), (256, 256), (512, 256), (768, 128))
+
+
+def call(body, outs, ins, scratch=(), flops=0):
+    moved = sum(a.size * a.dtype.itemsize for a in ins)
+    return pl.pallas_call(
+        body,
+        out_shape=outs,
+        in_specs=[SM] + [VM] * (len(ins) - 1),
+        out_specs=jax.tree.map(lambda _: VM, outs),
+        scratch_shapes=list(scratch),
+        compiler_params=pltpu.CompilerParams(vmem_limit_bytes=40 * 1024 * 1024),
+        cost_estimate=pl.CostEstimate(flops=flops, bytes_accessed=moved, transcendentals=0),
+    )(*ins)
+
+
+def sds(shape, dtype):
+    return jax.ShapeDtypeStruct(shape, dtype)
+
+
+def proj_body(at, p0, p1, p2, p3, w, out):
+    for k, p in enumerate((p0, p1, p2, p3)):
+        src = lax.rem(at[0] + 4 - k, 4)
+        xh, xl = lax.div(src, 2), lax.rem(src, 2)
+        part = jnp.dot(p[...], w[...], preferred_element_type=F4)
+        for j in range(4):
+            out[xh * 4 + j, xl] = part[24 * j : 24 * j + 24].astype(BF)
+
+
+def proj(at, pieces, weight):
+    out = call(proj_body, sds((8, 2, 24, 256), BF), [at, *pieces, weight], flops=2 * 384 * 1024 * 256)
+    return out.reshape(8, 48, 256)
+
+
+def up_body(half, at, p0, p1, p2, p3, gain, wg, wu, out, rows, squares):
+    z1 = at[2] if half == 0 else 1 - at[2]
+    squares[...] = jnp.zeros_like(squares)
+    for k, p in enumerate((p0, p1, p2, p3)):
+        src = lax.rem(at[0] + 4 - k, 4)
+        xh, xl = lax.div(src, 2), lax.rem(src, 2)
+        for z2 in range(2):
+            for z0 in range(2):
+                part = p[z2 * 4 + z1 * 2 + z0].astype(F4)
+                col = pl.multiple_of(z0 * 512 + xl * 256, 256)
+                row = pl.multiple_of(xh * 96 + z2 * 48, 48)
+                sq = part * part
+                squares[pl.ds(row, 48), :] += sq[:, :128] + sq[:, 128:]
+                rows[pl.ds(row, 48), pl.ds(col, 256)] = (part * gain[:, pl.ds(col, 256)]).astype(BF)
+    total = jnp.sum(squares[...], axis=1, keepdims=True)
+    high = total.astype(BF).astype(F4)
+    lanes = lax.broadcasted_iota(jnp.int32, (192, 128), 1)
+    tail = jnp.where(lanes == 0, high, jnp.where(lanes == 1, total - high, 0.0))
+    left = rows[...]
+    for base, w in ((0, wg), (896, wu)):
+        for at_col, size in N_CUTS:
+            part = jnp.dot(left, w[:, at_col : at_col + size], preferred_element_type=F4)
+            part = part.astype(out.dtype).reshape(4, 48, size)
+            out[:, :, base + at_col : base + at_col + size] = part
+    out[:, :, 1792:] = tail.astype(out.dtype).reshape(4, 48, 128)
+
+
+def up_half(half, dtype, at, pieces, gain, wg, wu):
+    return call(
+        lambda *refs: up_body(half, *refs),
+        sds((4, 48, 1920), dtype),
+        [at, *pieces, gain, wg, wu],
+        [pltpu.VMEM((192, 1024), BF), pltpu.VMEM((192, 128), F4)],
+        flops=2 * 192 * 1024 * 1792,
+    )
+
+
+def pair_body(at, mine, theirs, own, s1, s2, s3):
+    y = at[1]
+    own[...] = mine[y] + theirs[y].astype(F4)
+    for k, ref in ((1, s1), (2, s2), (3, s3)):
+        to = lax.rem(y + k, 4)
+        ref[...] = (mine[to] + theirs[to].astype(F4)).astype(BF)
+
+
+def pair_sums(at, mine, theirs):
+    outs = [sds((48, 1920), F4)] + [sds((48, 1920), BF)] * 3
+    return call(pair_body, outs, [at, mine, theirs])
+
+
+def hidden_body(at, own, r1, r2, r3, out):
+    add = lambda lo, hi: (
+        own[:, lo:hi] + r1[:, lo:hi].astype(F4) + r2[:, lo:hi].astype(F4) + r3[:, lo:hi].astype(F4)
+    )
+    mean_square = jnp.sum(add(1792, 1920), axis=1, keepdims=True) / D
+    inv = lax.rsqrt(mean_square + 1e-05)
+    gate = add(0, 896) * inv
+    up = add(896, 1792) * inv
+    out[...] = (gate / (1.0 + jnp.exp(-gate)) * up).astype(BF)
+
+
+def order_body(at, p0, p1, p2, p3, out):
+    for k, p in enumerate((p0, p1, p2, p3)):
+        out[lax.rem(at[1] + 4 - k, 4)] = p[...]
+
+
+def down_body(at, mine, theirs, w, own, s1, s2, s3, acc):
+    for rows, z1 in ((mine, at[2]), (theirs, 1 - at[2])):
+        left = rows[...].reshape(192, 896)
+        for n in range(4):
+            part = jnp.dot(left, w[:, 256 * n : 256 * n + 256], preferred_element_type=F4)
+            for b in range(4):
+                for xl in range(2):
+                    r = b * 48 + xl * 24
+                    acc[(b // 2) * 2 + xl, (b % 2) * 2 + z1, :, 256 * n : 256 * n + 256] = part[r : r + 24]
+    own[...] = acc[at[0]]
+    for k, ref in ((1, s1), (2, s2), (3, s3)):
+        ref[...] = acc[lax.rem(at[0] + k, 4)].astype(BF)
+
+
+def down(at, mine, theirs, weight):
+    outs = [sds((4, 24, 1024), F4)] + [sds((4, 24, 1024), BF)] * 3
+    return call(
+        down_body,
+        outs,
+        [at, mine, theirs, weight],
+        [pltpu.VMEM((4, 4, 24, 1024), F4)],
+        flops=2 * 384 * 896 * 1024,
+    )
+
+
+def around(array, axis):
+    got = {k: shift(array, axis, 4, k) for k in (2, 1, 3)}
+    return [got[1], got[2], got[3]]
+
+
+def sent(one, two, three, axis):
+    got = {k: shift(a, axis, 4, k) for k, a in ((2, two), (1, one), (3, three))}
+    return [got[1], got[2], got[3]]
+
+
 def local(
     queries,
     new_keys,
@@ -92,52 +231,31 @@
     x = lax.axis_index("xh") * 2 + lax.axis_index("xl")
     y = lax.axis_index("y")
     c = lax.axis_index("c")
-    head = y * 2 + c
+    at = jnp.stack([x, y, c, c]).astype(jnp.int32)
     res = residual.reshape(2, 2, 12, 256).swapaxes(0, 1).reshape(48, 256).astype(F4)
-    gain = lax.dynamic_slice_in_dim(norm_gain, head * 1024, 1024, 0)
+    gain = lax.dynamic_slice_in_dim(norm_gain, (y * 2 + c) * 1024, 1024, 0).reshape(1, 1024)
 
     attn = attention(queries, new_keys, new_values, key_cache, value_cache, lengths)
     along_z = copies_by_a2a(attn, "z", 8).reshape(96, 1024)
-    rows = gather4(along_z, X, x)
-    projected = jnp.dot(rows.reshape(384, 1024), out_weight, preferred_element_type=F4)
-    pieces = projected.astype(BF).reshape(2, 2, 4, 24, 256).swapaxes(1, 2).reshape(8, 48, 256)
+    pieces = proj(at, [along_z, *around(along_z, X)], out_weight)
     pieces = lax.all_to_all(pieces, HEAD, 0, 0, tiled=True)
     state = (res + jnp.sum(pieces.astype(F4), axis=0)).astype(BF)
     hidden_state = state.reshape(2, 2, 12, 256).swapaxes(0, 1).reshape(48, 256)
 
     moved = lax.ppermute(state, ALL, transpose_perm())
     along_z = copies_by_a2a(moved, "z", 8)
-    along_z = along_z.reshape(4, 2, 48, 256).swapaxes(1, 2).reshape(192, 512)
-    full = gather4(along_z, X, x).reshape(2, 2, 192, 2, 256)
-    full = full.transpose(0, 2, 3, 1, 4).reshape(384, 1024)
-    full_f = full.astype(F4)
-    squares = jnp.sum(full_f * full_f, axis=1, keepdims=True)
-    scaled = (full_f * gain).astype(BF)
-    gate = jnp.dot(scaled, gate_weight, preferred_element_type=F4)
-    up = jnp.dot(scaled, up_weight, preferred_element_type=F4)
-    sq_hi = squares.astype(BF)
-    sq_lo = (squares - sq_hi.astype(F4)).astype(BF)
-    lanes = lax.broadcasted_iota(jnp.int32, (1, 128), 1)
-    sq = jnp.where(lanes == 0, sq_hi.astype(F4), jnp.where(lanes == 1, sq_lo.astype(F4), 0.0))
-    both = jnp.concatenate([gate, up, sq], axis=1)
-    both = both.reshape(4, 2, 48, 1920)
-    other = lax.dynamic_index_in_dim(both, 1 - c, 1, False).astype(BF)
-    mine = lax.dynamic_index_in_dim(both, c, 1, False)
-    pair_sum = mine + swapped(other, "c").astype(F4)
-    share = summed4(pair_sum, "y", y)
-    mean_square = jnp.sum(share[:, 1792:], axis=1, keepdims=True) / D
-    inv = lax.rsqrt(mean_square + 1e-05)
-    gate = share[:, :896] * inv
-    up = share[:, 896:1792] * inv
-    hidden = (jax.nn.silu(gate) * up).astype(BF)
-    hidden = gather4(hidden, "y", y)
-    theirs = swapped(hidden, "c")
-    both = jnp.stack([jnp.where(c == 0, hidden, theirs), jnp.where(c == 0, theirs, hidden)], axis=1)
-    hidden = both.reshape(384, 896)
-
-    part = jnp.dot(hidden, down_weight, preferred_element_type=F4)
-    part = part.reshape(2, 4, 2, 24, 1024).swapaxes(1, 2).reshape(4, 96, 1024)
-    part = summed4(part, X, x).astype(BF).reshape(8, 12, 1024)
+    pieces = [along_z, *around(along_z, X)]
+    other = up_half(1, BF, at, pieces, gain, gate_weight, up_weight)
+    theirs = swapped(other, "c")
+    mine = up_half(0, F4, at, pieces, gain, gate_weight, up_weight)
+    own, *shares = pair_sums(at, mine, theirs)
+    hidden = call(hidden_body, sds((48, 896), BF), [at, own, *sent(*shares, "y")])
+    hidden = call(order_body, sds((4, 48, 896), BF), [at, hidden, *around(hidden, "y")])
+    own, *shares = down(at, hidden, swapped(hidden, "c"), down_weight)
+    part = own
+    for got in sent(*shares, X):
+        part = part + got.astype(F4)
+    part = part.astype(BF).reshape(8, 12, 1024)
     part = lax.all_to_all(part, "z", 0, 0, tiled=True)
     ffn_out = jnp.sum(part.astype(F4), axis=0).astype(BF)
     return (hidden_state, ffn_out)

time: 182 us -> 157 us (0.86); the launches traced: 179 us -> 157 us
  local copies, waits for them, and re-layouts: 26.8 us -> 9.32 us
  Pallas kernels: 0 us -> 10 us
  other arithmetic: 13.9 us -> 3.96 us
  matrix products: 7.8 us -> 2.39 us
  starting transfers between devices: 26.8 us -> 29.3 us
  waiting for transfers between devices: 65.6 us -> 63.4 us
    convert_element_type x6 -> x0, local copies, waits for them, and re-layouts: 12.8 us -> none  [the longest x3 10.2 us: local(): full_f = full.astype(F4)]
    pallas_call x0 -> x7, Pallas kernels: none -> 10 us  [call(): pl.pallas_call(body, out_shape=outs, in_specs=[SM] + [VM] * (len(ins) - 1...]
    dot_general x4 -> x0, matrix products: 5.41 us -> none  [the longest x1 3.09 us: local(): up = jnp.dot(scaled, up_weight, preferred_element_type=F4)]
    another operation x8 -> x1, other arithmetic: 4.76 us -> 0.08 us  [local(): at = jnp.stack([x, y, c, c]).astype(jnp.int32)]
    unnamed x34 -> x23, local copies, waits for them, and re-layouts: 8.39 us -> 4.86 us
    add x2 -> x0, other arithmetic: 2.99 us -> none  [the longest x1 1.73 us: local(): pair_sum = mine + swapped(other, 'c').astype(F4)]
    ppermute x2, waiting for transfers between devices: 4.55 us -> 1.69 us  [swapped(): return lax.ppermute(array, axis, [(0, 1), (1, 0)])]
    convert_element_type x4 -> x1, other arithmetic: 2.81 us -> 0.1 us  [local(): part = part.astype(BF).reshape(8, 12, 1024)]
  transfers between devices with their start and end apart: 20 -> 20, of which waited for: 17 -> 17; matrix products, arithmetic and copies ran while one was open for 2% -> 2% of each run, Pallas kernels for 0% -> 1%
where the time goes in v2:
time: 157 us
  waiting for transfers between devices  63.4 us (40%)
  blocking collectives  37.3 us (24%)
  starting transfers between devices  29.3 us (19%)
  Pallas kernels  10 us (6%)
  local copies, waits for them, and re-layouts  9.32 us (6%)
  other arithmetic  3.96 us (3%)
  matrix products  2.39 us (2%)
    ppermute x15, waiting for transfers between devices, shift(): lax.ppermute(array, axis, [(i, (i + step) % size) for i in range(size)])  39.5 us
    all_to_all x2, blocking collectives, copies_by_a2a(): return lax.all_to_all(copies, axis, 0, 0, tiled=True)  37.3 us
    ppermute x15, starting transfers between devices, shift(): lax.ppermute(array, axis, [(i, (i + step) % size) for i in range(size)])  18 us
    pallas_call x7, Pallas kernels, call(): pl.pallas_call(body, out_shape=outs, in_specs=[SM] + [VM] * (len(ins) - 1...  10 us
    all_to_all x1, waiting for transfers between devices, local(): part = lax.all_to_all(part, 'z', 0, 0, tiled=True)  9.83 us
    ppermute x1, waiting for transfers between devices, local(): moved = lax.ppermute(state, ALL, transpose_perm())  6.32 us
    all_to_all x1, waiting for transfers between devices, local(): pieces = lax.all_to_all(pieces, HEAD, 0, 0, tiled=True)  6.06 us
    unnamed x23, local copies, waits for them, and re-layouts  4.86 us
  transfers between devices with their start and end apart: 20, of which 17 were waited for; matrix products, arithmetic and copies ran while one was open for 2% of the time, Pallas kernels for 1%

profile of v2, /device:TPU:6, one launch (start us, length us, event | category | flops | bytes accessed | tf_op | source)
XLA Modules:
  0.0 156.6 jit_solution(7641533382742282394)
XLA Ops:
  1.5 1.2 iota_compare_fusion
  4.2 1.0 fusion.17
  6.1 20.2 %all_to_all.20 = bf16[8,12,1024]{2,1,0:T(8,128)(2,1)} all-to-all(bf16[8,12,1024]{2,1,0:T(8,128)(2,1)S(1)} %broadcast_in_dim.25), channel_id=1, replica_groups=mesh['xh'=2,'z'=8,'y'=4,'c'=2,'xl'=2] {'z'}, dimensions={0} | all-to-all | bytes 393216 | tf_op jit(solution)/shard_map/all_to_all | solution.py:25
  28.3 1.1 collective-permute-start.1
  29.4 2.1 %collective-permute-start = (bf16[96,1024]{1,0:T(8,128)(2,1)S(1)}, bf16[96,1024]{1,0:T(8,128)(2,1)}, u32[]{:S(2)}, u32[]{:S(2)}) collective-permute-start(bf16[96,1024]{1,0:T(8,128)(2,1)S(1)} %reshape.59.p0), channel_id=1, source_target_pairs={{0,1},{1,128},{128,129},{129,0},{2,3},{3,130},{130,131},{131,2},{4... | collective-permute-start | bytes 589832 | tf_op jit(solution)/shard_map/ppermute | solution.py:20
  31.6 6.2 %collective-permute-done.2.p3 = bf16[96,1024]{1,0:T(8,128)(2,1)S(1)} collective-permute-done((bf16[96,1024]{1,0:T(8,128)(2,1)S(1)}, bf16[96,1024]{1,0:T(8,128)(2,1)S(1)}, u32[]{:S(2)}, u32[]{:S(2)}) %collective-permute-start.2) | collective-permute-done | bytes 196640 | tf_op jit(solution)/shard_map/ppermute | solution.py:20
  38.5 1.0 copy-done.3
  39.5 2.2 %shard_map.131 = bf16[8,2,24,256]{3,2,1,0:T(8,128)(2,1)} custom-call(s32[4]{0:T(128)S(1)} %pad_add_fusion.at.refs_0_, bf16[96,1024]{1,0:T(8,128)(2,1)S(1)} %reshape.59.p0, bf16[96,1024]{1,0:T(8,128)(2,1)} %collective-permute-done.p1, bf16[96,1024]{1,0:T(8,128)(2,1)} %collective-permute-done.1.p2, bf16[96,1024]{1,0:T(8,128)(2,1)S(1)} %collective-permute-done.2.p3, ...), custom_call_target="tpu_custom_call" | custom-call | flops 201326592 | bytes 1310736 | tf_op jit(solution)/shard_map/pallas_call | solution.py:87
  41.7 4.5 %all-to-all-start.1 = ((bf16[8,48,256]{2,1,0:T(8,128)(2,1)}), bf16[8,48,256]{2,1,0:T(8,128)(2,1)S(1)}, u32[]{:S(2)}, u32[]{:S(2)}) async-start(bf16[8,48,256]{2,1,0:T(8,128)(2,1)} %bitcast.6), calls=%async_computation.1 | async-start | bytes 393216 | tf_op jit(solution)/shard_map/all_to_all | solution.py:241
  47.0 6.1 %all-to-all-done.1 = bf16[8,48,256]{2,1,0:T(8,128)(2,1)S(1)} async-done(((bf16[8,48,256]{2,1,0:T(8,128)(2,1)}), bf16[8,48,256]{2,1,0:T(8,128)(2,1)S(1)}, u32[]{:S(2)}, u32[]{:S(2)}) %all-to-all-start.1) | async-done | bytes 196640 | tf_op jit(solution)/shard_map/all_to_all | solution.py:241
  53.1 3.3 %collective-permute-start.3 = (bf16[48,256]{1,0:T(8,128)(2,1)S(1)}, bf16[48,256]{1,0:T(8,128)(2,1)S(1)}, u32[]{:S(2)}, u32[]{:S(2)}) collective-permute-start(bf16[48,256]{1,0:T(8,128)(2,1)S(1)} %add_convert_fusion.1), channel_id=1, source_target_pairs={{0,0},{1,1},{2,32},{3,33},{4,64},{5,65},{6,96},{7,97},{8,128},{9,1... | collective-permute-start | bytes 73736 | tf_op jit(solution)/shard_map/ppermute | solution.py:245
  56.4 6.3 %collective-permute-done.3 = bf16[48,256]{1,0:T(8,128)(2,1)S(1)} collective-permute-done((bf16[48,256]{1,0:T(8,128)(2,1)S(1)}, bf16[48,256]{1,0:T(8,128)(2,1)S(1)}, u32[]{:S(2)}, u32[]{:S(2)}) %collective-permute-start.3) | collective-permute-done | bytes 24608 | tf_op jit(solution)/shard_map/ppermute | solution.py:245
  62.7 17.1 %all_to_all.21.refs_1_ = bf16[8,48,256]{2,1,0:T(8,128)(2,1)S(1)} all-to-all(bf16[8,48,256]{2,1,0:T(8,128)(2,1)S(1)} %broadcast_in_dim.26), channel_id=1, replica_groups=mesh['xh'=2,'z'=8,'y'=4,'c'=2,'xl'=2] {'z'}, dimensions={0} | all-to-all | bytes 393216 | tf_op jit(solution)/shard_map/all_to_all | solution.py:25
  80.6 2.7 %collective-permute-start.4 = (bf16[8,48,256]{2,1,0:T(8,128)(2,1)S(1)}, bf16[8,48,256]{2,1,0:T(8,128)(2,1)}, u32[]{:S(2)}, u32[]{:S(2)}) collective-permute-start(bf16[8,48,256]{2,1,0:T(8,128)(2,1)S(1)} %all_to_all.21.refs_1_), channel_id=1, source_target_pairs={{0,1},{1,128},{128,129},{129,0},{2,3},{3,130},{130,131},{131,2},{4... | collective-permute-start | bytes 589832 | tf_op jit(solution)/shard_map/ppermute | solution.py:20
  84.0 5.2 %collective-permute-done.6.refs_4_ = bf16[8,48,256]{2,1,0:T(8,128)(2,1)S(1)} collective-permute-done((bf16[8,48,256]{2,1,0:T(8,128)(2,1)S(1)}, bf16[8,48,256]{2,1,0:T(8,128)(2,1)S(1)}, u32[]{:S(2)}, u32[]{:S(2)}) %collective-permute-start.6) | collective-permute-done | bytes 196640 | tf_op jit(solution)/shard_map/ppermute | solution.py:20
  89.8 1.5 copy-done.1
  91.3 1.5 copy-done.2
  92.8 2.1 %shard_map.133 = bf16[4,48,1920]{2,1,0:T(8,128)(2,1)S(1)} custom-call(s32[4]{0:T(128)S(1)} %pad_add_fusion.at.refs_0_, bf16[8,48,256]{2,1,0:T(8,128)(2,1)S(1)} %all_to_all.21.refs_1_, bf16[8,48,256]{2,1,0:T(8,128)(2,1)} %collective-permute-done.4.refs_2_, bf16[8,48,256]{2,1,0:T(8,128)(2,1)} %collective-permute-done.5.refs_3_, ...), custom_call_target="tpu_custom_call" | custom-call | flops 704643072 | bytes 4460560 | tf_op jit(solution)/shard_map/pallas_call | solution.py:87
  95.1 2.1 %shard_map.132.mine = f32[4,48,1920]{2,1,0:T(8,128)S(1)} custom-call(s32[4]{0:T(128)S(1)} %pad_add_fusion.at.refs_0_, bf16[8,48,256]{2,1,0:T(8,128)(2,1)S(1)} %all_to_all.21.refs_1_, bf16[8,48,256]{2,1,0:T(8,128)(2,1)} %collective-permute-done.4.refs_2_, bf16[8,48,256]{2,1,0:T(8,128)(2,1)} %collective-permute-done.5.refs_3_, ...), custom_call_target="tpu_custom_call" | custom-call | flops 704643072 | bytes 4460560 | tf_op jit(solution)/shard_map/pallas_call | solution.py:87
  98.0 2.2 %collective-permute-start.9 = (bf16[48,1920]{1,0:T(8,128)(2,1)S(1)}, bf16[48,1920]{1,0:T(8,128)(2,1)S(1)}, u32[]{:S(2)}, u32[]{:S(2)}) collective-permute-start(bf16[48,1920]{1,0:T(8,128)(2,1)S(1)} %get-tuple-element.12), channel_id=1, source_target_pairs={{0,8},{4,12},{8,0},{12,4},{1,9},{5,13},{9,1},{13,5},{2,10},{6,14},... | collective-permute-start | bytes 552968 | tf_op jit(solution)/shard_map/ppermute | solution.py:20
  100.2 1.1 collective-permute-start.10
  101.3 8.9 %collective-permute-done.8.r1 = bf16[48,1920]{1,0:T(8,128)(2,1)S(1)} collective-permute-done((bf16[48,1920]{1,0:T(8,128)(2,1)S(1)}, bf16[48,1920]{1,0:T(8,128)(2,1)S(1)}, u32[]{:S(2)}, u32[]{:S(2)}) %collective-permute-start.8) | collective-permute-done | bytes 184352 | tf_op jit(solution)/shard_map/ppermute | solution.py:20
  111.5 2.6 %collective-permute-start.13 = (bf16[48,896]{1,0:T(8,128)(2,1)S(1)}, bf16[48,896]{1,0:T(8,128)(2,1)S(1)}, u32[]{:S(2)}, u32[]{:S(2)}) collective-permute-start(bf16[48,896]{1,0:T(8,128)(2,1)S(1)} %shard_map.135.p0), channel_id=1, source_target_pairs={{0,12},{4,0},{8,4},{12,8},{1,13},{5,1},{9,5},{13,9},{2,14},{6,2},{... | collective-permute-start | bytes 258056 | tf_op jit(solution)/shard_map/ppermute | solution.py:20
  115.1 2.6 %collective-permute-done.13.p3 = bf16[48,896]{1,0:T(8,128)(2,1)S(1)} collective-permute-done((bf16[48,896]{1,0:T(8,128)(2,1)S(1)}, bf16[48,896]{1,0:T(8,128)(2,1)S(1)}, u32[]{:S(2)}, u32[]{:S(2)}) %collective-permute-start.13) | collective-permute-done | bytes 86048 | tf_op jit(solution)/shard_map/ppermute | solution.py:20
  117.7 2.8 %collective-permute-done.12.p2 = bf16[48,896]{1,0:T(8,128)(2,1)S(1)} collective-permute-done((bf16[48,896]{1,0:T(8,128)(2,1)S(1)}, bf16[48,896]{1,0:T(8,128)(2,1)S(1)}, u32[]{:S(2)}, u32[]{:S(2)}) %collective-permute-start.12) | collective-permute-done | bytes 86048 | tf_op jit(solution)/shard_map/ppermute | solution.py:20
  121.8 1.6 %collective-permute-done.14.theirs = bf16[4,48,896]{2,1,0:T(8,128)(2,1)S(1)} collective-permute-done((bf16[4,48,896]{2,1,0:T(8,128)(2,1)S(1)}, bf16[4,48,896]{2,1,0:T(8,128)(2,1)S(1)}, u32[]{:S(2)}, u32[]{:S(2)}) %collective-permute-start.14) | collective-permute-done | bytes 344096 | tf_op jit(solution)/shard_map/ppermute | solution.py:42
  123.4 1.6 %shard_map.137 = (f32[4,24,1024]{2,1,0:T(8,128)S(1)}, bf16[4,24,1024]{2,1,0:T(8,128)(2,1)S(1)}, bf16[4,24,1024]{2,1,0:T(8,128)(2,1)S(1)}, bf16[4,24,1024]{2,1,0:T(8,128)(2,1)S(1)}) custom-call(s32[4]{0:T(128)S(1)} %pad_add_fusion.at.refs_0_, bf16[4,48,896]{2,1,0:T(8,128)(2,1)S(1)} %shard_map.136.mine, ...), custom_call_target="tpu_custom_call" | custom-call | flops 704643072 | bytes 2523152 | tf_op jit(solution)/shard_map/pallas_call | solution.py:87
  125.1 2.6 %collective-permute-start.15 = (bf16[4,24,1024]{2,1,0:T(8,128)(2,1)S(1)}, bf16[4,24,1024]{2,1,0:T(8,128)(2,1)S(1)}, u32[]{:S(2)}, u32[]{:S(2)}) collective-permute-start(bf16[4,24,1024]{2,1,0:T(8,128)(2,1)S(1)} %get-tuple-element.15), channel_id=1, source_target_pairs={{0,1},{1,128},{128,129},{129,0},{2,3},{3,130},{130,131},{131,2},{4... | collective-permute-start | bytes 589832 | tf_op jit(solution)/shard_map/ppermute | solution.py:20
  128.6 7.7 %collective-permute-done.15 = bf16[4,24,1024]{2,1,0:T(8,128)(2,1)S(1)} collective-permute-done((bf16[4,24,1024]{2,1,0:T(8,128)(2,1)S(1)}, bf16[4,24,1024]{2,1,0:T(8,128)(2,1)S(1)}, u32[]{:S(2)}, u32[]{:S(2)}) %collective-permute-start.15) | collective-permute-done | bytes 196640 | tf_op jit(solution)/shard_map/ppermute | solution.py:20
  137.0 2.8 %collective-permute-done.17 = bf16[4,24,1024]{2,1,0:T(8,128)(2,1)S(1)} collective-permute-done((bf16[4,24,1024]{2,1,0:T(8,128)(2,1)S(1)}, bf16[4,24,1024]{2,1,0:T(8,128)(2,1)S(1)}, u32[]{:S(2)}, u32[]{:S(2)}) %collective-permute-start.17) | collective-permute-done | bytes 196640 | tf_op jit(solution)/shard_map/ppermute | solution.py:20
  140.6 3.4 %all-to-all-start.3 = ((bf16[8,12,1024]{2,1,0:T(8,128)(2,1)}), bf16[8,12,1024]{2,1,0:T(8,128)(2,1)S(1)}, u32[]{:S(2)}, u32[]{:S(2)}) async-start(bf16[8,12,1024]{2,1,0:T(8,128)(2,1)} %reshape.63), calls=%async_computation.3 | async-start | bytes 524288 | tf_op jit(solution)/shard_map/all_to_all | solution.py:259
  146.1 9.8 %all-to-all-done.3 = bf16[8,12,1024]{2,1,0:T(8,128)(2,1)S(1)} async-done(((bf16[8,12,1024]{2,1,0:T(8,128)(2,1)}), bf16[8,12,1024]{2,1,0:T(8,128)(2,1)S(1)}, u32[]{:S(2)}, u32[]{:S(2)}) %all-to-all-start.3) | async-done | bytes 196640 | tf_op jit(solution)/shard_map/all_to_all | solution.py:259
  (64 shorter events, 18.6 us)
Async XLA Ops:
  0.6 3.6 %copy-start = (bf16[12,1024,128]{2,1,0:T(8,128)(2,1)S(1)}, bf16[12,1024,128]{2,1,0:T(8,128)(2,1)}, u32[]{:S(2)}) copy-start(bf16[12,1024,128]{2,1,0:T(8,128)(2,1)} %param.15) | copy-start | bytes 9437188
  0.6 4.8 %copy-start.5 = (bf16[12,1024,128]{2,1,0:T(8,128)(2,1)S(1)}, bf16[12,1024,128]{2,1,0:T(8,128)(2,1)}, u32[]{:S(2)}) copy-start(bf16[12,1024,128]{2,1,0:T(8,128)(2,1)} %param.16) | copy-start | bytes 9437188
  27.4 10.4 %collective-permute-start.2 = (bf16[96,1024]{1,0:T(8,128)(2,1)S(1)}, bf16[96,1024]{1,0:T(8,128)(2,1)S(1)}, u32[]{:S(2)}, u32[]{:S(2)}) collective-permute-start(bf16[96,1024]{1,0:T(8,128)(2,1)S(1)} %reshape.59.p0), channel_id=1, source_target_pairs={{0,129},{1,0},{128,1},{129,128},{2,131},{3,2},{130,3},{131,130},{4... | collective-permute-start | bytes 589832 | tf_op jit(solution)/shard_map/ppermute | solution.py:20
  28.3 9.5 %collective-permute-start.1 = (bf16[96,1024]{1,0:T(8,128)(2,1)S(1)}, bf16[96,1024]{1,0:T(8,128)(2,1)}, u32[]{:S(2)}, u32[]{:S(2)}) collective-permute-start(bf16[96,1024]{1,0:T(8,128)(2,1)S(1)} %reshape.59.p0), channel_id=1, source_target_pairs={{0,128},{1,129},{128,0},{129,1},{2,130},{3,131},{130,2},{131,3},{4... | collective-permute-start | bytes 589832 | tf_op jit(solution)/shard_map/ppermute | solution.py:20
  29.4 9.1 %collective-permute-start = (bf16[96,1024]{1,0:T(8,128)(2,1)S(1)}, bf16[96,1024]{1,0:T(8,128)(2,1)}, u32[]{:S(2)}, u32[]{:S(2)}) collective-permute-start(bf16[96,1024]{1,0:T(8,128)(2,1)S(1)} %reshape.59.p0), channel_id=1, source_target_pairs={{0,1},{1,128},{128,129},{129,0},{2,3},{3,130},{130,131},{131,2},{4... | collective-permute-start | bytes 589832 | tf_op jit(solution)/shard_map/ppermute | solution.py:20
  38.5 1.0 copy-start.3
  41.7 11.3 %all-to-all-start.1 = ((bf16[8,48,256]{2,1,0:T(8,128)(2,1)}), bf16[8,48,256]{2,1,0:T(8,128)(2,1)S(1)}, u32[]{:S(2)}, u32[]{:S(2)}) async-start(bf16[8,48,256]{2,1,0:T(8,128)(2,1)} %bitcast.6), calls=%async_computation.1 | async-start | bytes 393216 | tf_op jit(solution)/shard_map/all_to_all | solution.py:241
  46.9 15.8 %copy-start.6 = (f32[2,2,12,256]{3,2,1,0:T(8,128)}, f32[2,2,12,256]{3,2,1,0:T(8,128)S(1)}, u32[]{:S(2)}) copy-start(f32[2,2,12,256]{3,2,1,0:T(8,128)S(1)} %reshape.65) | copy-start | bytes 147460
  53.1 3.3 %copy-start.8 = (f32[48,256]{1,0:T(8,128)}, f32[48,256]{1,0:T(8,128)S(1)}, u32[]{:S(2)}) copy-start(f32[48,256]{1,0:T(8,128)S(1)} %convert_reduce_fusion) | copy-start | bytes 147460
  53.1 9.6 %collective-permute-start.3 = (bf16[48,256]{1,0:T(8,128)(2,1)S(1)}, bf16[48,256]{1,0:T(8,128)(2,1)S(1)}, u32[]{:S(2)}, u32[]{:S(2)}) collective-permute-start(bf16[48,256]{1,0:T(8,128)(2,1)S(1)} %add_convert_fusion.1), channel_id=1, source_target_pairs={{0,0},{1,1},{2,32},{3,33},{4,64},{5,65},{6,96},{7,97},{8,128},{9,1... | collective-permute-start | bytes 73736 | tf_op jit(solution)/shard_map/ppermute | solution.py:245
  79.8 9.3 %collective-permute-start.6 = (bf16[8,48,256]{2,1,0:T(8,128)(2,1)S(1)}, bf16[8,48,256]{2,1,0:T(8,128)(2,1)S(1)}, u32[]{:S(2)}, u32[]{:S(2)}) collective-permute-start(bf16[8,48,256]{2,1,0:T(8,128)(2,1)S(1)} %all_to_all.21.refs_1_), channel_id=1, source_target_pairs={{0,129},{1,0},{128,1},{129,128},{2,131},{3,2},{130,3},{131,130},{4... | collective-permute-start | bytes 589832 | tf_op jit(solution)/shard_map/ppermute | solution.py:20
  80.6 8.5 %collective-permute-start.5 = (bf16[8,48,256]{2,1,0:T(8,128)(2,1)S(1)}, bf16[8,48,256]{2,1,0:T(8,128)(2,1)}, u32[]{:S(2)}, u32[]{:S(2)}) collective-permute-start(bf16[8,48,256]{2,1,0:T(8,128)(2,1)S(1)} %all_to_all.21.refs_1_), channel_id=1, source_target_pairs={{0,128},{1,129},{128,0},{129,1},{2,130},{3,131},{130,2},{131,3},{4... | collective-permute-start | bytes 589832 | tf_op jit(solution)/shard_map/ppermute | solution.py:20
  80.6 9.2 %collective-permute-start.4 = (bf16[8,48,256]{2,1,0:T(8,128)(2,1)S(1)}, bf16[8,48,256]{2,1,0:T(8,128)(2,1)}, u32[]{:S(2)}, u32[]{:S(2)}) collective-permute-start(bf16[8,48,256]{2,1,0:T(8,128)(2,1)S(1)} %all_to_all.21.refs_1_), channel_id=1, source_target_pairs={{0,1},{1,128},{128,129},{129,0},{2,3},{3,130},{130,131},{131,2},{4... | collective-permute-start | bytes 589832 | tf_op jit(solution)/shard_map/ppermute | solution.py:20
  89.8 1.5 copy-start.1
  91.3 1.5 copy-start.2
  95.0 2.3 %collective-permute-start.7 = (bf16[4,48,1920]{2,1,0:T(8,128)(2,1)S(1)}, bf16[4,48,1920]{2,1,0:T(8,128)(2,1)S(1)}, u32[]{:S(2)}, u32[]{:S(2)}) collective-permute-start(bf16[4,48,1920]{2,1,0:T(8,128)(2,1)S(1)} %shard_map.133), channel_id=1, source_target_pairs={{0,2},{2,0},{1,3},{3,1},{4,6},{6,4},{5,7},{7,5},{8,10},{10,8},{9,1... | collective-permute-start | bytes 2211848 | tf_op jit(solution)/shard_map/ppermute | solution.py:42
  97.2 26.2 %copy-start.4 = (bf16[896,1024]{1,0:T(8,128)(2,1)S(1)}, bf16[896,1024]{1,0:T(8,128)(2,1)}, u32[]{:S(2)}) copy-start(bf16[896,1024]{1,0:T(8,128)(2,1)} %w.3) | copy-start | bytes 5505028
  98.0 12.2 %collective-permute-start.8 = (bf16[48,1920]{1,0:T(8,128)(2,1)S(1)}, bf16[48,1920]{1,0:T(8,128)(2,1)S(1)}, u32[]{:S(2)}, u32[]{:S(2)}) collective-permute-start(bf16[48,1920]{1,0:T(8,128)(2,1)S(1)} %get-tuple-element.11), channel_id=1, source_target_pairs={{0,4},{4,8},{8,12},{12,0},{1,5},{5,9},{9,13},{13,1},{2,6},{6,10},{... | collective-permute-start | bytes 552968 | tf_op jit(solution)/shard_map/ppermute | solution.py:20
  98.0 12.1 %collective-permute-start.9 = (bf16[48,1920]{1,0:T(8,128)(2,1)S(1)}, bf16[48,1920]{1,0:T(8,128)(2,1)S(1)}, u32[]{:S(2)}, u32[]{:S(2)}) collective-permute-start(bf16[48,1920]{1,0:T(8,128)(2,1)S(1)} %get-tuple-element.12), channel_id=1, source_target_pairs={{0,8},{4,12},{8,0},{12,4},{1,9},{5,13},{9,1},{13,5},{2,10},{6,14},... | collective-permute-start | bytes 552968 | tf_op jit(solution)/shard_map/ppermute | solution.py:20
  100.2 10.6 %collective-permute-start.10 = (bf16[48,1920]{1,0:T(8,128)(2,1)S(1)}, bf16[48,1920]{1,0:T(8,128)(2,1)S(1)}, u32[]{:S(2)}, u32[]{:S(2)}) collective-permute-start(bf16[48,1920]{1,0:T(8,128)(2,1)S(1)} %get-tuple-element.13), channel_id=1, source_target_pairs={{0,12},{4,0},{8,4},{12,8},{1,13},{5,1},{9,5},{13,9},{2,14},{6,2},{... | collective-permute-start | bytes 552968 | tf_op jit(solution)/shard_map/ppermute | solution.py:20
  110.8 33.2 %copy-start.9 = (f32[48,256]{1,0:T(8,128)S(1)}, f32[48,256]{1,0:T(8,128)}, u32[]{:S(2)}) copy-start(f32[48,256]{1,0:T(8,128)} %copy-done.8) | copy-start | bytes 147460
  110.8 33.8 %copy-start.7 = (f32[2,2,12,256]{3,2,1,0:T(8,128)S(1)}, f32[2,2,12,256]{3,2,1,0:T(8,128)}, u32[]{:S(2)}) copy-start(f32[2,2,12,256]{3,2,1,0:T(8,128)} %copy-done.6) | copy-start | bytes 147460
  111.5 6.2 %collective-permute-start.13 = (bf16[48,896]{1,0:T(8,128)(2,1)S(1)}, bf16[48,896]{1,0:T(8,128)(2,1)S(1)}, u32[]{:S(2)}, u32[]{:S(2)}) collective-permute-start(bf16[48,896]{1,0:T(8,128)(2,1)S(1)} %shard_map.135.p0), channel_id=1, source_target_pairs={{0,12},{4,0},{8,4},{12,8},{1,13},{5,1},{9,5},{13,9},{2,14},{6,2},{... | collective-permute-start | bytes 258056 | tf_op jit(solution)/shard_map/ppermute | solution.py:20
  114.1 6.4 %collective-permute-start.12 = (bf16[48,896]{1,0:T(8,128)(2,1)S(1)}, bf16[48,896]{1,0:T(8,128)(2,1)S(1)}, u32[]{:S(2)}, u32[]{:S(2)}) collective-permute-start(bf16[48,896]{1,0:T(8,128)(2,1)S(1)} %shard_map.135.p0), channel_id=1, source_target_pairs={{0,8},{4,12},{8,0},{12,4},{1,9},{5,13},{9,1},{13,5},{2,10},{6,14},... | collective-permute-start | bytes 258056 | tf_op jit(solution)/shard_map/ppermute | solution.py:20
  114.1 7.0 %collective-permute-start.11 = (bf16[48,896]{1,0:T(8,128)(2,1)S(1)}, bf16[48,896]{1,0:T(8,128)(2,1)S(1)}, u32[]{:S(2)}, u32[]{:S(2)}) collective-permute-start(bf16[48,896]{1,0:T(8,128)(2,1)S(1)} %shard_map.135.p0), channel_id=1, source_target_pairs={{0,4},{4,8},{8,12},{12,0},{1,5},{5,9},{9,13},{13,1},{2,6},{6,10},{... | collective-permute-start | bytes 258056 | tf_op jit(solution)/shard_map/ppermute | solution.py:20
  121.7 1.7 %collective-permute-start.14 = (bf16[4,48,896]{2,1,0:T(8,128)(2,1)S(1)}, bf16[4,48,896]{2,1,0:T(8,128)(2,1)S(1)}, u32[]{:S(2)}, u32[]{:S(2)}) collective-permute-start(bf16[4,48,896]{2,1,0:T(8,128)(2,1)S(1)} %shard_map.136.mine), channel_id=1, source_target_pairs={{0,2},{2,0},{1,3},{3,1},{4,6},{6,4},{5,7},{7,5},{8,10},{10,8},{9,1... | collective-permute-start | bytes 1032200 | tf_op jit(solution)/shard_map/ppermute | solution.py:42
  125.1 11.3 %collective-permute-start.15 = (bf16[4,24,1024]{2,1,0:T(8,128)(2,1)S(1)}, bf16[4,24,1024]{2,1,0:T(8,128)(2,1)S(1)}, u32[]{:S(2)}, u32[]{:S(2)}) collective-permute-start(bf16[4,24,1024]{2,1,0:T(8,128)(2,1)S(1)} %get-tuple-element.15), channel_id=1, source_target_pairs={{0,1},{1,128},{128,129},{129,0},{2,3},{3,130},{130,131},{131,2},{4... | collective-permute-start | bytes 589832 | tf_op jit(solution)/shard_map/ppermute | solution.py:20
  127.7 9.3 %collective-permute-start.16 = (bf16[4,24,1024]{2,1,0:T(8,128)(2,1)S(1)}, bf16[4,24,1024]{2,1,0:T(8,128)(2,1)S(1)}, u32[]{:S(2)}, u32[]{:S(2)}) collective-permute-start(bf16[4,24,1024]{2,1,0:T(8,128)(2,1)S(1)} %get-tuple-element.16), channel_id=1, source_target_pairs={{0,128},{1,129},{128,0},{129,1},{2,130},{3,131},{130,2},{131,3},{4... | collective-permute-start | bytes 589832 | tf_op jit(solution)/shard_map/ppermute | solution.py:20
  127.7 12.1 %collective-permute-start.17 = (bf16[4,24,1024]{2,1,0:T(8,128)(2,1)S(1)}, bf16[4,24,1024]{2,1,0:T(8,128)(2,1)S(1)}, u32[]{:S(2)}, u32[]{:S(2)}) collective-permute-start(bf16[4,24,1024]{2,1,0:T(8,128)(2,1)S(1)} %get-tuple-element.17), channel_id=1, source_target_pairs={{0,129},{1,0},{128,1},{129,128},{2,131},{3,2},{130,3},{131,130},{4... | collective-permute-start | bytes 589832 | tf_op jit(solution)/shard_map/ppermute | solution.py:20
  140.6 15.4 %all-to-all-start.3 = ((bf16[8,12,1024]{2,1,0:T(8,128)(2,1)}), bf16[8,12,1024]{2,1,0:T(8,128)(2,1)S(1)}, u32[]{:S(2)}, u32[]{:S(2)}) async-start(bf16[8,12,1024]{2,1,0:T(8,128)(2,1)} %reshape.63), calls=%async_computation.3 | async-start | bytes 524288 | tf_op jit(solution)/shard_map/all_to_all | solution.py:259

commit v3 on v2

--- a/solution.py
+++ b/solution.py
@@ -42,7 +42,7 @@
     return lax.ppermute(array, axis, [(0, 1), (1, 0)])
 
 
-def transpose_perm():
+def device_pairs(place):
     pairs = []
     for xh in range(2):
         for z in range(8):
@@ -50,11 +50,21 @@
                 for c in range(2):
                     for xl in range(2):
                         src = (((xh * 8 + z) * 4 + y) * 2 + c) * 2 + xl
-                        z2, z1, z0 = z >> 2, (z >> 1) & 1, z & 1
-                        nxh, nz = y >> 1, ((y & 1) << 2) | (c << 1) | z0
-                        ny, nc = xh * 2 + z2, z1
-                        pairs.append((src, (((nxh * 8 + nz) * 4 + ny) * 2 + nc) * 2 + xl))
+                        nxh, nz, ny, nc, nxl = place(xh, z, y, c, xl)
+                        pairs.append((src, (((nxh * 8 + nz) * 4 + ny) * 2 + nc) * 2 + nxl))
     return pairs
+
+
+def to_features(xh, z, y, c, xl):
+    return xh, ((y & 1) << 2) | (c << 1) | (z & 1), (y & 2) | (z >> 2), (z >> 1) & 1, xl
+
+
+def swap_same(xh, z, y, c, xl):
+    return y >> 1, z, (xh << 1) | (y & 1), c, xl
+
+
+def swap_cross(xh, z, y, c, xl):
+    return y >> 1, z, (xh << 1) | (y & 1), c, 1 - xl
 
 
 def attention(queries, new_keys, new_values, key_cache, value_cache, lengths):
@@ -99,39 +109,63 @@
     return jax.ShapeDtypeStruct(shape, dtype)
 
 
-def proj_body(at, p0, p1, p2, p3, w, out):
-    for k, p in enumerate((p0, p1, p2, p3)):
+def proj_body(at, rows, w0, w1, w2, w3, out, held, sems):
+    copies = [pltpu.make_async_copy(w, held.at[k], sems.at[k]) for k, w in enumerate((w0, w1, w2, w3))]
+    for copy in copies:
+        copy.start()
+    left = rows[...]
+    for k, copy in enumerate(copies):
         src = lax.rem(at[0] + 4 - k, 4)
         xh, xl = lax.div(src, 2), lax.rem(src, 2)
-        part = jnp.dot(p[...], w[...], preferred_element_type=F4)
+        copy.wait()
+        part = jnp.dot(left, held[k], preferred_element_type=F4)
         for j in range(4):
             out[xh * 4 + j, xl] = part[24 * j : 24 * j + 24].astype(BF)
 
 
-def proj(at, pieces, weight):
-    out = call(proj_body, sds((8, 2, 24, 256), BF), [at, *pieces, weight], flops=2 * 384 * 1024 * 256)
-    return out.reshape(8, 48, 256)
-
-
-def up_body(half, at, p0, p1, p2, p3, gain, wg, wu, out, rows, squares):
+def proj(at, rows, weights):
+    moved = 4 * 1024 * 256 * 2
+    return pl.pallas_call(
+        proj_body,
+        out_shape=sds((8, 2, 24, 256), BF),
+        in_specs=[SM, VM] + [pl.BlockSpec(memory_space=pl.ANY)] * 4,
+        out_specs=VM,
+        scratch_shapes=[pltpu.VMEM((4, 1024, 256), BF), pltpu.SemaphoreType.DMA((4,))],
+        cost_estimate=pl.CostEstimate(flops=2 * 96 * 1024 * 1024, bytes_accessed=moved, transcendentals=0),
+    )(at, rows, *weights)
+
+
+def first_body(at, p0, wg, wu, out):
+    part = p0[...].astype(F4)
+    part = part * part
+    out[...] = part[:, :, :128] + part[:, :, 128:256] + part[:, :, 256:384] + part[:, :, 384:]
+
+
+def up_body(half, at, sq0, p0, p1, p2, p3, gain, wg, wu, out, rows, squares):
     z1 = at[2] if half == 0 else 1 - at[2]
-    squares[...] = jnp.zeros_like(squares)
     for k, p in enumerate((p0, p1, p2, p3)):
         src = lax.rem(at[0] + 4 - k, 4)
         xh, xl = lax.div(src, 2), lax.rem(src, 2)
         for z2 in range(2):
+            row = pl.multiple_of(xh * 96 + z2 * 48 + xl * 24, 8)
+            sq = None
             for z0 in range(2):
-                part = p[z2 * 4 + z1 * 2 + z0].astype(F4)
-                col = pl.multiple_of(z0 * 512 + xl * 256, 256)
-                row = pl.multiple_of(xh * 96 + z2 * 48, 48)
-                sq = part * part
-                squares[pl.ds(row, 48), :] += sq[:, :128] + sq[:, 128:]
-                rows[pl.ds(row, 48), pl.ds(col, 256)] = (part * gain[:, pl.ds(col, 256)]).astype(BF)
+                place = z2 * 4 + z1 * 2 + z0
+                part = p[place].astype(F4)
+                cols = slice(z0 * 512, z0 * 512 + 512)
+                rows[pl.ds(row, 24), cols] = part * gain[:, cols]
+                if k == 0:
+                    one = sq0[place]
+                else:
+                    part = part * part
+                    one = part[:, :128] + part[:, 128:256] + part[:, 256:384] + part[:, 384:]
+                sq = one if sq is None else sq + one
+            squares[pl.ds(row, 24), :] = sq
     total = jnp.sum(squares[...], axis=1, keepdims=True)
     high = total.astype(BF).astype(F4)
     lanes = lax.broadcasted_iota(jnp.int32, (192, 128), 1)
     tail = jnp.where(lanes == 0, high, jnp.where(lanes == 1, total - high, 0.0))
-    left = rows[...]
+    left = rows[...].astype(BF)
     for base, w in ((0, wg), (896, wu)):
         for at_col, size in N_CUTS:
             part = jnp.dot(left, w[:, at_col : at_col + size], preferred_element_type=F4)
@@ -140,12 +174,12 @@
     out[:, :, 1792:] = tail.astype(out.dtype).reshape(4, 48, 128)
 
 
-def up_half(half, dtype, at, pieces, gain, wg, wu):
+def up_half(half, dtype, at, sq0, pieces, gain, wg, wu):
     return call(
         lambda *refs: up_body(half, *refs),
         sds((4, 48, 1920), dtype),
-        [at, *pieces, gain, wg, wu],
-        [pltpu.VMEM((192, 1024), BF), pltpu.VMEM((192, 128), F4)],
+        [at, sq0, *pieces, gain, wg, wu],
+        [pltpu.VMEM((192, 1024), F4), pltpu.VMEM((192, 128), F4)],
         flops=2 * 192 * 1024 * 1792,
     )
 
@@ -232,22 +266,39 @@
     y = lax.axis_index("y")
     c = lax.axis_index("c")
     at = jnp.stack([x, y, c, c]).astype(jnp.int32)
-    res = residual.reshape(2, 2, 12, 256).swapaxes(0, 1).reshape(48, 256).astype(F4)
+    xl = lax.axis_index("xl")
     gain = lax.dynamic_slice_in_dim(norm_gain, (y * 2 + c) * 1024, 1024, 0).reshape(1, 1024)
+    weights = [out_weight, *around(out_weight, X)]
 
     attn = attention(queries, new_keys, new_values, key_cache, value_cache, lengths)
-    along_z = copies_by_a2a(attn, "z", 8).reshape(96, 1024)
-    pieces = proj(at, [along_z, *around(along_z, X)], out_weight)
-    pieces = lax.all_to_all(pieces, HEAD, 0, 0, tiled=True)
-    state = (res + jnp.sum(pieces.astype(F4), axis=0)).astype(BF)
-    hidden_state = state.reshape(2, 2, 12, 256).swapaxes(0, 1).reshape(48, 256)
-
-    moved = lax.ppermute(state, ALL, transpose_perm())
+    rows = copies_by_a2a(attn, "z", 8).reshape(96, 1024)
+    res = residual.reshape(2, 2, 12, 256).swapaxes(0, 1)
+    res, rows = lax.optimization_barrier((res, rows))
+    res_same = lax.dynamic_index_in_dim(res, xl, 0, False).reshape(24, 256)
+    res_cross = lax.dynamic_index_in_dim(res, 1 - xl, 0, False).reshape(24, 256)
+    res_same = lax.ppermute(res_same, ALL, device_pairs(swap_same))
+    res_cross = lax.ppermute(res_cross, ALL, device_pairs(swap_cross))
+    first = jnp.where(xl == 0, res_same, res_cross).astype(F4)
+    second = jnp.where(xl == 0, res_cross, res_same).astype(F4)
+    pieces = lax.all_to_all(proj(at, rows, weights), HEAD, 0, 0, tiled=True)
+    state = jnp.sum(pieces.astype(F4), axis=0) + jnp.stack([first, second])
+    state = state.astype(BF)
+
+    moved = state.swapaxes(0, 1).reshape(24, 512)
+    moved = lax.ppermute(moved, ALL, device_pairs(to_features))
+    out_same = lax.dynamic_index_in_dim(state, xl, 0, False)
+    out_cross = lax.dynamic_index_in_dim(state, 1 - xl, 0, False)
+    out_same = lax.ppermute(out_same, ALL, device_pairs(swap_same))
+    out_cross = lax.ppermute(out_cross, ALL, device_pairs(swap_cross))
+    hidden_state = jnp.stack([jnp.where(xl == 0, out_same, out_cross), jnp.where(xl == 0, out_cross, out_same)])
+    hidden_state = hidden_state.reshape(2, 2, 12, 256).swapaxes(0, 1).reshape(48, 256)
+
     along_z = copies_by_a2a(moved, "z", 8)
     pieces = [along_z, *around(along_z, X)]
-    other = up_half(1, BF, at, pieces, gain, gate_weight, up_weight)
+    sq0 = call(first_body, sds((8, 24, 128), F4), [at, along_z, gate_weight, up_weight])
+    other = up_half(1, BF, at, sq0, pieces, gain, gate_weight, up_weight)
     theirs = swapped(other, "c")
-    mine = up_half(0, F4, at, pieces, gain, gate_weight, up_weight)
+    mine = up_half(0, F4, at, sq0, pieces, gain, gate_weight, up_weight)
     own, *shares = pair_sums(at, mine, theirs)
     hidden = call(hidden_body, sds((48, 896), BF), [at, own, *sent(*shares, "y")])
     hidden = call(order_body, sds((4, 48, 896), BF), [at, hidden, *around(hidden, "y")])

time: 157 us -> 151 us (0.962)
  starting transfers between devices: 29.3 us -> 55.5 us
  blocking collectives: 37.3 us -> 21.2 us
  waiting for transfers between devices: 63.4 us -> 47.6 us
  Pallas kernels: 10 us -> 12.2 us
  local copies, waits for them, and re-layouts: 9.32 us -> 7.43 us
    ppermute x15, waiting for transfers between devices: 39.5 us -> 17 us  [shift(): lax.ppermute(array, axis, [(i, (i + step) % size) for i in range(size)])]
    all_to_all x2 -> x1, blocking collectives: 37.3 us -> 21.2 us  [copies_by_a2a(): return lax.all_to_all(copies, axis, 0, 0, tiled=True)]
    ppermute x1 -> x5, starting transfers between devices: 3.29 us -> 17 us  [the longest x1 5.67 us: local(): res_cross = lax.ppermute(res_cross, ALL, device_pairs(swap_cross))]
    all_to_all x1 -> x2, waiting for transfers between devices: 6.06 us -> 17.1 us  [the longest x1 10.7 us: copies_by_a2a(): return lax.all_to_all(copies, axis, 0, 0, tiled=True)]
    all_to_all x1 -> x2, starting transfers between devices: 4.47 us -> 11.9 us  [the longest x1 8.47 us: copies_by_a2a(): return lax.all_to_all(copies, axis, 0, 0, tiled=True)]
    ppermute x1 -> x5, waiting for transfers between devices: 6.32 us -> 0.33 us  [the longest x1 0.32 us: local(): res_same = lax.ppermute(res_same, ALL, device_pairs(swap_same))]
    ppermute x15, starting transfers between devices: 18 us -> 23.1 us  [shift(): lax.ppermute(array, axis, [(i, (i + step) % size) for i in range(size)])]
    pallas_call x0 -> x1, Pallas kernels: none -> 3.79 us  [proj(): pl.pallas_call(proj_body, out_shape=sds((8, 2, 24, 256), BF), in_specs=[S...]
  transfers between devices with their start and end apart: 20 -> 25, of which waited for: 17 -> 12; matrix products, arithmetic and copies ran while one was open for 2% -> 6% of each run, Pallas kernels for 1% -> 4%
where the time goes in v3:
time: 151 us
  starting transfers between devices  55.5 us (37%)
  waiting for transfers between devices  47.6 us (32%)
  blocking collectives  21.2 us (14%)
  Pallas kernels  12.2 us (8%)
  local copies, waits for them, and re-layouts  7.43 us (5%)
  other arithmetic  3.09 us (2%)
  matrix products  2.39 us (2%)
    ppermute x15, starting transfers between devices, shift(): lax.ppermute(array, axis, [(i, (i + step) % size) for i in range(size)])  23.1 us
    all_to_all x1, blocking collectives, copies_by_a2a(): return lax.all_to_all(copies, axis, 0, 0, tiled=True)  21.2 us
    ppermute x15, waiting for transfers between devices, shift(): lax.ppermute(array, axis, [(i, (i + step) % size) for i in range(size)])  17 us
    all_to_all x1, waiting for transfers between devices, local(): part = lax.all_to_all(part, 'z', 0, 0, tiled=True)  11.5 us
    all_to_all x1, waiting for transfers between devices, copies_by_a2a(): return lax.all_to_all(copies, axis, 0, 0, tiled=True)  10.7 us
    all_to_all x1, starting transfers between devices, copies_by_a2a(): return lax.all_to_all(copies, axis, 0, 0, tiled=True)  8.47 us
    pallas_call x7, Pallas kernels, call(): pl.pallas_call(body, out_shape=outs, in_specs=[SM] + [VM] * (len(ins) - 1...  8.45 us
    all_to_all x1, waiting for transfers between devices, local(): pieces = lax.all_to_all(proj(at, rows, weights), HEAD, 0, 0, tiled=True)  6.42 us
  transfers between devices with their start and end apart: 25, of which 12 were waited for; matrix products, arithmetic and copies ran while one was open for 6% of the time, Pallas kernels for 4%

profile of v3, /device:TPU:6, one launch (start us, length us, event | category | flops | bytes accessed | tf_op | source)
XLA Modules:
  0.0 150.6 jit_solution(4358187066485915351)
XLA Ops:
  0.7 1.5 collective-permute-start.1
  2.1 2.1 %collective-permute-start = (bf16[1024,256]{1,0:T(8,128)(2,1)}, bf16[1024,256]{1,0:T(8,128)(2,1)}, u32[]{:S(2)}, u32[]{:S(2)}) collective-permute-start(bf16[1024,256]{1,0:T(8,128)(2,1)} %w0.1), channel_id=1, source_target_pairs={{0,1},{1,128},{128,129},{129,0},{2,3},{3,130},{130,131},{131,2},{4... | collective-permute-start | bytes 1572872 | tf_op jit(solution)/shard_map/ppermute | solution.py:20
  9.9 8.5 %all-to-all-start = ((bf16[8,12,1024]{2,1,0:T(8,128)(2,1)}), bf16[8,12,1024]{2,1,0:T(8,128)(2,1)S(1)}, u32[]{:S(2)}, u32[]{:S(2)}) async-start(bf16[8,12,1024]{2,1,0:T(8,128)(2,1)} %broadcast_in_dim.25), calls=%async_computation | async-start | bytes 524288 | tf_op jit(solution)/shard_map/all_to_all | solution.py:25
  19.0 10.7 %all-to-all-done = bf16[8,12,1024]{2,1,0:T(8,128)(2,1)S(1)} async-done(((bf16[8,12,1024]{2,1,0:T(8,128)(2,1)}), bf16[8,12,1024]{2,1,0:T(8,128)(2,1)S(1)}, u32[]{:S(2)}, u32[]{:S(2)}) %all-to-all-start) | async-done | bytes 196640 | tf_op jit(solution)/shard_map/all_to_all | solution.py:25
  30.4 5.7 %collective-permute-start.4 = (bf16[24,256]{1,0:T(8,128)(2,1)S(1)}, bf16[24,256]{1,0:T(8,128)(2,1)S(1)}, u32[]{:S(2)}, u32[]{:S(2)}) collective-permute-start(bf16[24,256]{1,0:T(8,128)(2,1)S(1)} %reshape.68), channel_id=1, source_target_pairs={{0,1},{1,0},{2,3},{3,2},{4,5},{5,4},{6,7},{7,6},{8,129},{9,128},{1... | collective-permute-start | bytes 36872 | tf_op jit(solution)/shard_map/ppermute | solution.py:280
  36.1 1.9 %collective-permute-start.3 = (bf16[24,256]{1,0:T(8,128)(2,1)S(1)}, bf16[24,256]{1,0:T(8,128)(2,1)S(1)}, u32[]{:S(2)}, u32[]{:S(2)}) collective-permute-start(bf16[24,256]{1,0:T(8,128)(2,1)S(1)} %reshape.67), channel_id=1, source_target_pairs={{0,0},{1,1},{2,2},{3,3},{4,4},{5,5},{6,6},{7,7},{8,128},{9,129},{1... | collective-permute-start | bytes 36872 | tf_op jit(solution)/shard_map/ppermute | solution.py:279
  38.0 3.8 %shard_map.131 = bf16[8,2,24,256]{3,2,1,0:T(8,128)(2,1)} custom-call(s32[4]{0:T(128)} %pad_add_fusion.at.refs_0_, bf16[96,1024]{1,0:T(8,128)(2,1)} %reshape.66.rows, bf16[1024,256]{1,0:T(8,128)(2,1)} %w0.1, bf16[1024,256]{1,0:T(8,128)(2,1)} %collective-permute-done.w1, bf16[1024,256]{1,0:T(8,128)(2,1)} %collective-permute-done.1.w2, ...), custom_call_target="tpu_custom_call" | custom-call | flops 201326592 | bytes 2097152 | tf_op jit(solution)/shard_map/pallas_call | solution.py:128
  41.8 3.4 %all-to-all-start.1 = ((bf16[8,2,24,256]{3,2,1,0:T(8,128)(2,1)}), bf16[8,2,24,256]{3,2,1,0:T(8,128)(2,1)S(1)}, u32[]{:S(2)}, u32[]{:S(2)}) async-start(bf16[8,2,24,256]{3,2,1,0:T(8,128)(2,1)} %shard_map.131), calls=%async_computation.1 | async-start | bytes 393216 | tf_op jit(solution)/shard_map/all_to_all | solution.py:283
  45.6 6.4 %all-to-all-done.1 = bf16[8,2,24,256]{3,2,1,0:T(8,128)(2,1)S(1)} async-done(((bf16[8,2,24,256]{3,2,1,0:T(8,128)(2,1)}), bf16[8,2,24,256]{3,2,1,0:T(8,128)(2,1)S(1)}, u32[]{:S(2)}, u32[]{:S(2)}) %all-to-all-start.1) | async-done | bytes 196640 | tf_op jit(solution)/shard_map/all_to_all | solution.py:283
  52.8 21.2 %all_to_all.20.p0.refs_2_ = bf16[8,24,512]{2,1,0:T(8,128)(2,1)S(1)} all-to-all(bf16[8,24,512]{2,1,0:T(8,128)(2,1)S(1)} %broadcast_in_dim.26), channel_id=1, replica_groups=mesh['xh'=2,'z'=8,'y'=4,'c'=2,'xl'=2] {'z'}, dimensions={0} | all-to-all | bytes 393216 | tf_op jit(solution)/shard_map/all_to_all | solution.py:25
  74.9 3.5 %collective-permute-start.9 = (bf16[8,24,512]{2,1,0:T(8,128)(2,1)S(1)}, bf16[8,24,512]{2,1,0:T(8,128)(2,1)}, u32[]{:S(2)}, u32[]{:S(2)}) collective-permute-start(bf16[8,24,512]{2,1,0:T(8,128)(2,1)S(1)} %all_to_all.20.p0.refs_2_), channel_id=1, source_target_pairs={{0,128},{1,129},{128,0},{129,1},{2,130},{3,131},{130,2},{131,3},{4... | collective-permute-start | bytes 589832 | tf_op jit(solution)/shard_map/ppermute | solution.py:20
  78.5 2.6 %collective-permute-start.8 = (bf16[8,24,512]{2,1,0:T(8,128)(2,1)S(1)}, bf16[8,24,512]{2,1,0:T(8,128)(2,1)}, u32[]{:S(2)}, u32[]{:S(2)}) collective-permute-start(bf16[8,24,512]{2,1,0:T(8,128)(2,1)S(1)} %all_to_all.20.p0.refs_2_), channel_id=1, source_target_pairs={{0,1},{1,128},{128,129},{129,0},{2,3},{3,130},{130,131},{131,2},{4... | collective-permute-start | bytes 589832 | tf_op jit(solution)/shard_map/ppermute | solution.py:20
  81.8 1.5 copy-done.1
  83.3 1.5 copy-done.2
  85.4 2.1 %shard_map.134 = bf16[4,48,1920]{2,1,0:T(8,128)(2,1)S(1)} custom-call(s32[4]{0:T(128)S(1)} %copy-done.3, f32[8,24,128]{2,1,0:T(8,128)S(1)} %shard_map.132.refs_1_, bf16[8,24,512]{2,1,0:T(8,128)(2,1)S(1)} %all_to_all.20.p0.refs_2_, bf16[8,24,512]{2,1,0:T(8,128)(2,1)} %collective-permute-done.8.refs_3_, bf16[8,24,512]{2,1,0:T(8,128)(2,1)} %collective-permute-done.9.refs_4_, ...), custom_call_target="tpu_custom_call" | custom-call | flops 704643072 | bytes 4558864 | tf_op jit(solution)/shard_map/pallas_call | solution.py:97
  87.7 2.1 %shard_map.133.mine = f32[4,48,1920]{2,1,0:T(8,128)S(1)} custom-call(s32[4]{0:T(128)S(1)} %copy-done.3, f32[8,24,128]{2,1,0:T(8,128)S(1)} %shard_map.132.refs_1_, bf16[8,24,512]{2,1,0:T(8,128)(2,1)S(1)} %all_to_all.20.p0.refs_2_, bf16[8,24,512]{2,1,0:T(8,128)(2,1)} %collective-permute-done.8.refs_3_, bf16[8,24,512]{2,1,0:T(8,128)(2,1)} %collective-permute-done.9.refs_4_, ...), custom_call_target="tpu_custom_call" | custom-call | flops 704643072 | bytes 4558864 | tf_op jit(solution)/shard_map/pallas_call | solution.py:97
  90.6 1.4 collective-permute-start.12
  92.0 2.1 %collective-permute-start.13 = (bf16[48,1920]{1,0:T(8,128)(2,1)S(1)}, bf16[48,1920]{1,0:T(8,128)(2,1)S(1)}, u32[]{:S(2)}, u32[]{:S(2)}) collective-permute-start(bf16[48,1920]{1,0:T(8,128)(2,1)S(1)} %get-tuple-element.16), channel_id=1, source_target_pairs={{0,8},{4,12},{8,0},{12,4},{1,9},{5,13},{9,1},{13,5},{2,10},{6,14},... | collective-permute-start | bytes 552968 | tf_op jit(solution)/shard_map/ppermute | solution.py:20
  94.7 4.4 %collective-permute-done.12.r1 = bf16[48,1920]{1,0:T(8,128)(2,1)S(1)} collective-permute-done((bf16[48,1920]{1,0:T(8,128)(2,1)S(1)}, bf16[48,1920]{1,0:T(8,128)(2,1)S(1)}, u32[]{:S(2)}, u32[]{:S(2)}) %collective-permute-start.12) | collective-permute-done | bytes 184352 | tf_op jit(solution)/shard_map/ppermute | solution.py:20
  99.1 3.8 %collective-permute-done.13.r2 = bf16[48,1920]{1,0:T(8,128)(2,1)S(1)} collective-permute-done((bf16[48,1920]{1,0:T(8,128)(2,1)S(1)}, bf16[48,1920]{1,0:T(8,128)(2,1)S(1)}, u32[]{:S(2)}, u32[]{:S(2)}) %collective-permute-start.13) | collective-permute-done | bytes 184352 | tf_op jit(solution)/shard_map/ppermute | solution.py:20
  104.1 2.7 %collective-permute-start.17 = (bf16[48,896]{1,0:T(8,128)(2,1)S(1)}, bf16[48,896]{1,0:T(8,128)(2,1)S(1)}, u32[]{:S(2)}, u32[]{:S(2)}) collective-permute-start(bf16[48,896]{1,0:T(8,128)(2,1)S(1)} %shard_map.136.p0), channel_id=1, source_target_pairs={{0,12},{4,0},{8,4},{12,8},{1,13},{5,1},{9,5},{13,9},{2,14},{6,2},{... | collective-permute-start | bytes 258056 | tf_op jit(solution)/shard_map/ppermute | solution.py:20
  107.8 2.9 %collective-permute-done.17.p3 = bf16[48,896]{1,0:T(8,128)(2,1)S(1)} collective-permute-done((bf16[48,896]{1,0:T(8,128)(2,1)S(1)}, bf16[48,896]{1,0:T(8,128)(2,1)S(1)}, u32[]{:S(2)}, u32[]{:S(2)}) %collective-permute-start.17) | collective-permute-done | bytes 86048 | tf_op jit(solution)/shard_map/ppermute | solution.py:20
  110.7 2.8 %collective-permute-done.16.p2 = bf16[48,896]{1,0:T(8,128)(2,1)S(1)} collective-permute-done((bf16[48,896]{1,0:T(8,128)(2,1)S(1)}, bf16[48,896]{1,0:T(8,128)(2,1)S(1)}, u32[]{:S(2)}, u32[]{:S(2)}) %collective-permute-start.16) | collective-permute-done | bytes 86048 | tf_op jit(solution)/shard_map/ppermute | solution.py:20
  115.0 1.6 %collective-permute-done.18.theirs = bf16[4,48,896]{2,1,0:T(8,128)(2,1)S(1)} collective-permute-done((bf16[4,48,896]{2,1,0:T(8,128)(2,1)S(1)}, bf16[4,48,896]{2,1,0:T(8,128)(2,1)S(1)}, u32[]{:S(2)}, u32[]{:S(2)}) %collective-permute-start.18) | collective-permute-done | bytes 344096 | tf_op jit(solution)/shard_map/ppermute | solution.py:42
  116.7 1.6 %shard_map.138 = (f32[4,24,1024]{2,1,0:T(8,128)S(1)}, bf16[4,24,1024]{2,1,0:T(8,128)(2,1)S(1)}, bf16[4,24,1024]{2,1,0:T(8,128)(2,1)S(1)}, bf16[4,24,1024]{2,1,0:T(8,128)(2,1)S(1)}) custom-call(s32[4]{0:T(128)S(1)} %copy-done.3, bf16[4,48,896]{2,1,0:T(8,128)(2,1)S(1)} %shard_map.137.mine, bf16[4,48,896]{2,1,0:T(8,128)(2,1)S(1)} %collective-permute-done.18.theirs, ...), custom_call_target="tpu_custom_call" | custom-call | flops 704643072 | bytes 2523152 | tf_op jit(solution)/shard_map/pallas_call | solution.py:97
  118.3 2.8 %collective-permute-start.19 = (bf16[4,24,1024]{2,1,0:T(8,128)(2,1)S(1)}, bf16[4,24,1024]{2,1,0:T(8,128)(2,1)S(1)}, u32[]{:S(2)}, u32[]{:S(2)}) collective-permute-start(bf16[4,24,1024]{2,1,0:T(8,128)(2,1)S(1)} %get-tuple-element.19), channel_id=1, source_target_pairs={{0,1},{1,128},{128,129},{129,0},{2,3},{3,130},{130,131},{131,2},{4... | collective-permute-start | bytes 589832 | tf_op jit(solution)/shard_map/ppermute | solution.py:20
  121.5 1.3 collective-permute-start.21
  122.9 4.0 %collective-permute-start.5 = (bf16[24,256]{1,0:T(8,128)(2,1)S(1)}, bf16[24,256]{1,0:T(8,128)(2,1)S(1)}, u32[]{:S(2)}, u32[]{:S(2)}) collective-permute-start(bf16[24,256]{1,0:T(8,128)(2,1)S(1)} %get-tuple-element.26), channel_id=1, source_target_pairs={{0,0},{1,1},{2,2},{3,3},{4,4},{5,5},{6,6},{7,7},{8,128},{9,129},{1... | collective-permute-start | bytes 36872 | tf_op jit(solution)/shard_map/ppermute | solution.py:291
  126.9 4.8 %collective-permute-start.6 = (bf16[24,256]{1,0:T(8,128)(2,1)S(1)}, bf16[24,256]{1,0:T(8,128)(2,1)S(1)}, u32[]{:S(2)}, u32[]{:S(2)}) collective-permute-start(bf16[24,256]{1,0:T(8,128)(2,1)S(1)} %get-tuple-element.27), channel_id=1, source_target_pairs={{0,1},{1,0},{2,3},{3,2},{4,5},{5,4},{6,7},{7,6},{8,129},{9,128},{1... | collective-permute-start | bytes 36872 | tf_op jit(solution)/shard_map/ppermute | solution.py:292
  131.7 1.8 %collective-permute-done.21 = bf16[4,24,1024]{2,1,0:T(8,128)(2,1)S(1)} collective-permute-done((bf16[4,24,1024]{2,1,0:T(8,128)(2,1)S(1)}, bf16[4,24,1024]{2,1,0:T(8,128)(2,1)S(1)}, u32[]{:S(2)}, u32[]{:S(2)}) %collective-permute-start.21) | collective-permute-done | bytes 196640 | tf_op jit(solution)/shard_map/ppermute | solution.py:20
  134.3 3.4 %all-to-all-start.3 = ((bf16[8,12,1024]{2,1,0:T(8,128)(2,1)}), bf16[8,12,1024]{2,1,0:T(8,128)(2,1)S(1)}, u32[]{:S(2)}, u32[]{:S(2)}) async-start(bf16[8,12,1024]{2,1,0:T(8,128)(2,1)} %reshape.72), calls=%async_computation.3 | async-start | bytes 524288 | tf_op jit(solution)/shard_map/all_to_all | solution.py:310
  138.4 11.5 %all-to-all-done.3 = bf16[8,12,1024]{2,1,0:T(8,128)(2,1)S(1)} async-done(((bf16[8,12,1024]{2,1,0:T(8,128)(2,1)}), bf16[8,12,1024]{2,1,0:T(8,128)(2,1)S(1)}, u32[]{:S(2)}, u32[]{:S(2)}) %all-to-all-start.3) | async-done | bytes 196640 | tf_op jit(solution)/shard_map/all_to_all | solution.py:310
  (84 shorter events, 18.0 us)
Async XLA Ops:
  0.6 7.9 %copy-start.5 = (bf16[12,1024,128]{2,1,0:T(8,128)(2,1)S(1)}, bf16[12,1024,128]{2,1,0:T(8,128)(2,1)}, u32[]{:S(2)}) copy-start(bf16[12,1024,128]{2,1,0:T(8,128)(2,1)} %param.16) | copy-start | bytes 9437188
  0.7 37.3 %collective-permute-start.1 = (bf16[1024,256]{1,0:T(8,128)(2,1)}, bf16[1024,256]{1,0:T(8,128)(2,1)}, u32[]{:S(2)}, u32[]{:S(2)}) collective-permute-start(bf16[1024,256]{1,0:T(8,128)(2,1)} %w0.1), channel_id=1, source_target_pairs={{0,128},{1,129},{128,0},{129,1},{2,130},{3,131},{130,2},{131,3},{4... | collective-permute-start | bytes 1572872 | tf_op jit(solution)/shard_map/ppermute | solution.py:20
  2.1 35.9 %collective-permute-start = (bf16[1024,256]{1,0:T(8,128)(2,1)}, bf16[1024,256]{1,0:T(8,128)(2,1)}, u32[]{:S(2)}, u32[]{:S(2)}) collective-permute-start(bf16[1024,256]{1,0:T(8,128)(2,1)} %w0.1), channel_id=1, source_target_pairs={{0,1},{1,128},{128,129},{129,0},{2,3},{3,130},{130,131},{131,2},{4... | collective-permute-start | bytes 1572872 | tf_op jit(solution)/shard_map/ppermute | solution.py:20
  4.2 33.8 %collective-permute-start.2 = (bf16[1024,256]{1,0:T(8,128)(2,1)}, bf16[1024,256]{1,0:T(8,128)(2,1)}, u32[]{:S(2)}, u32[]{:S(2)}) collective-permute-start(bf16[1024,256]{1,0:T(8,128)(2,1)} %w0.1), channel_id=1, source_target_pairs={{0,129},{1,0},{128,1},{129,128},{2,131},{3,2},{130,3},{131,130},{4... | collective-permute-start | bytes 1572872 | tf_op jit(solution)/shard_map/ppermute | solution.py:20
  8.3 10.1 %copy-start.10 = (bf16[48,256]{1,0:T(8,128)(2,1)S(1)}, bf16[48,256]{1,0:T(8,128)(2,1)}, u32[]{:S(2)}) copy-start(bf16[48,256]{1,0:T(8,128)(2,1)} %param.18) | copy-start | bytes 73732
  9.9 19.8 %all-to-all-start = ((bf16[8,12,1024]{2,1,0:T(8,128)(2,1)}), bf16[8,12,1024]{2,1,0:T(8,128)(2,1)S(1)}, u32[]{:S(2)}, u32[]{:S(2)}) async-start(bf16[8,12,1024]{2,1,0:T(8,128)(2,1)} %broadcast_in_dim.25), calls=%async_computation | async-start | bytes 524288 | tf_op jit(solution)/shard_map/all_to_all | solution.py:25
  19.0 62.8 %copy-start.3 = (s32[4]{0:T(128)S(1)}, s32[4]{0:T(128)}, u32[]{:S(2)}) copy-start(s32[4]{0:T(128)} %pad_add_fusion.at.refs_0_) | copy-start | bytes 52
  30.4 14.8 %collective-permute-start.4 = (bf16[24,256]{1,0:T(8,128)(2,1)S(1)}, bf16[24,256]{1,0:T(8,128)(2,1)S(1)}, u32[]{:S(2)}, u32[]{:S(2)}) collective-permute-start(bf16[24,256]{1,0:T(8,128)(2,1)S(1)} %reshape.68), channel_id=1, source_target_pairs={{0,1},{1,0},{2,3},{3,2},{4,5},{5,4},{6,7},{7,6},{8,129},{9,128},{1... | collective-permute-start | bytes 36872 | tf_op jit(solution)/shard_map/ppermute | solution.py:280
  36.1 9.5 %collective-permute-start.3 = (bf16[24,256]{1,0:T(8,128)(2,1)S(1)}, bf16[24,256]{1,0:T(8,128)(2,1)S(1)}, u32[]{:S(2)}, u32[]{:S(2)}) collective-permute-start(bf16[24,256]{1,0:T(8,128)(2,1)S(1)} %reshape.67), channel_id=1, source_target_pairs={{0,0},{1,1},{2,2},{3,3},{4,4},{5,5},{6,6},{7,7},{8,128},{9,129},{1... | collective-permute-start | bytes 36872 | tf_op jit(solution)/shard_map/ppermute | solution.py:279
  41.8 10.2 %all-to-all-start.1 = ((bf16[8,2,24,256]{3,2,1,0:T(8,128)(2,1)}), bf16[8,2,24,256]{3,2,1,0:T(8,128)(2,1)S(1)}, u32[]{:S(2)}, u32[]{:S(2)}) async-start(bf16[8,2,24,256]{3,2,1,0:T(8,128)(2,1)} %shard_map.131), calls=%async_computation.1 | async-start | bytes 393216 | tf_op jit(solution)/shard_map/all_to_all | solution.py:283
  45.6 7.2 %copy-start.8 = (bf16[1,24,256]{2,1,0:T(8,128)(2,1)}, bf16[1,24,256]{2,1,0:T(8,128)(2,1)S(1)}, u32[]{:S(2)}) copy-start(bf16[1,24,256]{2,1,0:T(8,128)(2,1)S(1)} %get-tuple-element.29) | copy-start | bytes 36868
  52.1 0.7 collective-permute-start.7
  74.0 11.4 %collective-permute-start.10 = (bf16[8,24,512]{2,1,0:T(8,128)(2,1)S(1)}, bf16[8,24,512]{2,1,0:T(8,128)(2,1)S(1)}, u32[]{:S(2)}, u32[]{:S(2)}) collective-permute-start(bf16[8,24,512]{2,1,0:T(8,128)(2,1)S(1)} %all_to_all.20.p0.refs_2_), channel_id=1, source_target_pairs={{0,129},{1,0},{128,1},{129,128},{2,131},{3,2},{130,3},{131,130},{4... | collective-permute-start | bytes 589832 | tf_op jit(solution)/shard_map/ppermute | solution.py:20
  74.9 10.5 %collective-permute-start.9 = (bf16[8,24,512]{2,1,0:T(8,128)(2,1)S(1)}, bf16[8,24,512]{2,1,0:T(8,128)(2,1)}, u32[]{:S(2)}, u32[]{:S(2)}) collective-permute-start(bf16[8,24,512]{2,1,0:T(8,128)(2,1)S(1)} %all_to_all.20.p0.refs_2_), channel_id=1, source_target_pairs={{0,128},{1,129},{128,0},{129,1},{2,130},{3,131},{130,2},{131,3},{4... | collective-permute-start | bytes 589832 | tf_op jit(solution)/shard_map/ppermute | solution.py:20
  78.5 6.9 %collective-permute-start.8 = (bf16[8,24,512]{2,1,0:T(8,128)(2,1)S(1)}, bf16[8,24,512]{2,1,0:T(8,128)(2,1)}, u32[]{:S(2)}, u32[]{:S(2)}) collective-permute-start(bf16[8,24,512]{2,1,0:T(8,128)(2,1)S(1)} %all_to_all.20.p0.refs_2_), channel_id=1, source_target_pairs={{0,1},{1,128},{128,129},{129,0},{2,3},{3,130},{130,131},{131,2},{4... | collective-permute-start | bytes 589832 | tf_op jit(solution)/shard_map/ppermute | solution.py:20
  87.6 2.3 %collective-permute-start.11 = (bf16[4,48,1920]{2,1,0:T(8,128)(2,1)S(1)}, bf16[4,48,1920]{2,1,0:T(8,128)(2,1)S(1)}, u32[]{:S(2)}, u32[]{:S(2)}) collective-permute-start(bf16[4,48,1920]{2,1,0:T(8,128)(2,1)S(1)} %shard_map.134), channel_id=1, source_target_pairs={{0,2},{2,0},{1,3},{3,1},{4,6},{6,4},{5,7},{7,5},{8,10},{10,8},{9,1... | collective-permute-start | bytes 2211848 | tf_op jit(solution)/shard_map/ppermute | solution.py:42
  89.8 26.9 %copy-start.4 = (bf16[896,1024]{1,0:T(8,128)(2,1)S(1)}, bf16[896,1024]{1,0:T(8,128)(2,1)}, u32[]{:S(2)}) copy-start(bf16[896,1024]{1,0:T(8,128)(2,1)} %w.1) | copy-start | bytes 5505028
  89.8 33.0 %copy-start.7 = (f32[2,24,256]{2,1,0:T(8,128)S(1)}, f32[2,24,256]{2,1,0:T(8,128)}, u32[]{:S(2)}) copy-start(f32[2,24,256]{2,1,0:T(8,128)} %copy-done.6) | copy-start | bytes 147460
  89.8 33.0 %copy-start.9 = (bf16[1,24,256]{2,1,0:T(8,128)(2,1)S(1)}, bf16[1,24,256]{2,1,0:T(8,128)(2,1)}, u32[]{:S(2)}) copy-start(bf16[1,24,256]{2,1,0:T(8,128)(2,1)} %copy-done.8) | copy-start | bytes 36868
  90.6 8.6 %collective-permute-start.12 = (bf16[48,1920]{1,0:T(8,128)(2,1)S(1)}, bf16[48,1920]{1,0:T(8,128)(2,1)S(1)}, u32[]{:S(2)}, u32[]{:S(2)}) collective-permute-start(bf16[48,1920]{1,0:T(8,128)(2,1)S(1)} %get-tuple-element.15), channel_id=1, source_target_pairs={{0,4},{4,8},{8,12},{12,0},{1,5},{5,9},{9,13},{13,1},{2,6},{6,10},{... | collective-permute-start | bytes 552968 | tf_op jit(solution)/shard_map/ppermute | solution.py:20
  92.0 11.0 %collective-permute-start.13 = (bf16[48,1920]{1,0:T(8,128)(2,1)S(1)}, bf16[48,1920]{1,0:T(8,128)(2,1)S(1)}, u32[]{:S(2)}, u32[]{:S(2)}) collective-permute-start(bf16[48,1920]{1,0:T(8,128)(2,1)S(1)} %get-tuple-element.16), channel_id=1, source_target_pairs={{0,8},{4,12},{8,0},{12,4},{1,9},{5,13},{9,1},{13,5},{2,10},{6,14},... | collective-permute-start | bytes 552968 | tf_op jit(solution)/shard_map/ppermute | solution.py:20
  94.0 9.4 %collective-permute-start.14 = (bf16[48,1920]{1,0:T(8,128)(2,1)S(1)}, bf16[48,1920]{1,0:T(8,128)(2,1)S(1)}, u32[]{:S(2)}, u32[]{:S(2)}) collective-permute-start(bf16[48,1920]{1,0:T(8,128)(2,1)S(1)} %get-tuple-element.17), channel_id=1, source_target_pairs={{0,12},{4,0},{8,4},{12,8},{1,13},{5,1},{9,5},{13,9},{2,14},{6,2},{... | collective-permute-start | bytes 552968 | tf_op jit(solution)/shard_map/ppermute | solution.py:20
  104.1 6.6 %collective-permute-start.17 = (bf16[48,896]{1,0:T(8,128)(2,1)S(1)}, bf16[48,896]{1,0:T(8,128)(2,1)S(1)}, u32[]{:S(2)}, u32[]{:S(2)}) collective-permute-start(bf16[48,896]{1,0:T(8,128)(2,1)S(1)} %shard_map.136.p0), channel_id=1, source_target_pairs={{0,12},{4,0},{8,4},{12,8},{1,13},{5,1},{9,5},{13,9},{2,14},{6,2},{... | collective-permute-start | bytes 258056 | tf_op jit(solution)/shard_map/ppermute | solution.py:20
  106.9 6.7 %collective-permute-start.16 = (bf16[48,896]{1,0:T(8,128)(2,1)S(1)}, bf16[48,896]{1,0:T(8,128)(2,1)S(1)}, u32[]{:S(2)}, u32[]{:S(2)}) collective-permute-start(bf16[48,896]{1,0:T(8,128)(2,1)S(1)} %shard_map.136.p0), channel_id=1, source_target_pairs={{0,8},{4,12},{8,0},{12,4},{1,9},{5,13},{9,1},{13,5},{2,10},{6,14},... | collective-permute-start | bytes 258056 | tf_op jit(solution)/shard_map/ppermute | solution.py:20
  107.4 6.9 %collective-permute-start.15 = (bf16[48,896]{1,0:T(8,128)(2,1)S(1)}, bf16[48,896]{1,0:T(8,128)(2,1)S(1)}, u32[]{:S(2)}, u32[]{:S(2)}) collective-permute-start(bf16[48,896]{1,0:T(8,128)(2,1)S(1)} %shard_map.136.p0), channel_id=1, source_target_pairs={{0,4},{4,8},{8,12},{12,0},{1,5},{5,9},{9,13},{13,1},{2,6},{6,10},{... | collective-permute-start | bytes 258056 | tf_op jit(solution)/shard_map/ppermute | solution.py:20
  114.9 1.7 %collective-permute-start.18 = (bf16[4,48,896]{2,1,0:T(8,128)(2,1)S(1)}, bf16[4,48,896]{2,1,0:T(8,128)(2,1)S(1)}, u32[]{:S(2)}, u32[]{:S(2)}) collective-permute-start(bf16[4,48,896]{2,1,0:T(8,128)(2,1)S(1)} %shard_map.137.mine), channel_id=1, source_target_pairs={{0,2},{2,0},{1,3},{3,1},{4,6},{6,4},{5,7},{7,5},{8,10},{10,8},{9,1... | collective-permute-start | bytes 1032200 | tf_op jit(solution)/shard_map/ppermute | solution.py:42
  118.3 13.4 %collective-permute-start.19 = (bf16[4,24,1024]{2,1,0:T(8,128)(2,1)S(1)}, bf16[4,24,1024]{2,1,0:T(8,128)(2,1)S(1)}, u32[]{:S(2)}, u32[]{:S(2)}) collective-permute-start(bf16[4,24,1024]{2,1,0:T(8,128)(2,1)S(1)} %get-tuple-element.19), channel_id=1, source_target_pairs={{0,1},{1,128},{128,129},{129,0},{2,3},{3,130},{130,131},{131,2},{4... | collective-permute-start | bytes 589832 | tf_op jit(solution)/shard_map/ppermute | solution.py:20
  121.1 10.6 %collective-permute-start.20 = (bf16[4,24,1024]{2,1,0:T(8,128)(2,1)S(1)}, bf16[4,24,1024]{2,1,0:T(8,128)(2,1)S(1)}, u32[]{:S(2)}, u32[]{:S(2)}) collective-permute-start(bf16[4,24,1024]{2,1,0:T(8,128)(2,1)S(1)} %get-tuple-element.20), channel_id=1, source_target_pairs={{0,128},{1,129},{128,0},{129,1},{2,130},{3,131},{130,2},{131,3},{4... | collective-permute-start | bytes 589832 | tf_op jit(solution)/shard_map/ppermute | solution.py:20
  121.5 11.9 %collective-permute-start.21 = (bf16[4,24,1024]{2,1,0:T(8,128)(2,1)S(1)}, bf16[4,24,1024]{2,1,0:T(8,128)(2,1)S(1)}, u32[]{:S(2)}, u32[]{:S(2)}) collective-permute-start(bf16[4,24,1024]{2,1,0:T(8,128)(2,1)S(1)} %get-tuple-element.21), channel_id=1, source_target_pairs={{0,129},{1,0},{128,1},{129,128},{2,131},{3,2},{130,3},{131,130},{4... | collective-permute-start | bytes 589832 | tf_op jit(solution)/shard_map/ppermute | solution.py:20
  122.9 14.8 %collective-permute-start.5 = (bf16[24,256]{1,0:T(8,128)(2,1)S(1)}, bf16[24,256]{1,0:T(8,128)(2,1)S(1)}, u32[]{:S(2)}, u32[]{:S(2)}) collective-permute-start(bf16[24,256]{1,0:T(8,128)(2,1)S(1)} %get-tuple-element.26), channel_id=1, source_target_pairs={{0,0},{1,1},{2,2},{3,3},{4,4},{5,5},{6,6},{7,7},{8,128},{9,129},{1... | collective-permute-start | bytes 36872 | tf_op jit(solution)/shard_map/ppermute | solution.py:291
  126.9 10.8 %collective-permute-start.6 = (bf16[24,256]{1,0:T(8,128)(2,1)S(1)}, bf16[24,256]{1,0:T(8,128)(2,1)S(1)}, u32[]{:S(2)}, u32[]{:S(2)}) collective-permute-start(bf16[24,256]{1,0:T(8,128)(2,1)S(1)} %get-tuple-element.27), channel_id=1, source_target_pairs={{0,1},{1,0},{2,3},{3,2},{4,5},{5,4},{6,7},{7,6},{8,129},{9,128},{1... | collective-permute-start | bytes 36872 | tf_op jit(solution)/shard_map/ppermute | solution.py:292
  134.3 15.7 %all-to-all-start.3 = ((bf16[8,12,1024]{2,1,0:T(8,128)(2,1)}), bf16[8,12,1024]{2,1,0:T(8,128)(2,1)S(1)}, u32[]{:S(2)}, u32[]{:S(2)}) async-start(bf16[8,12,1024]{2,1,0:T(8,128)(2,1)} %reshape.72), calls=%async_computation.3 | async-start | bytes 524288 | tf_op jit(solution)/shard_map/all_to_all | solution.py:310
  (4 other events, 10.3 us)

commit v4 on v3

--- a/solution.py
+++ b/solution.py
@@ -67,28 +67,77 @@
     return y >> 1, z, (xh << 1) | (y & 1), c, 1 - xl
 
 
-def attention(queries, new_keys, new_values, key_cache, value_cache, lengths):
-    row_count = queries.shape[0]
-    slot_count = key_cache.shape[1]
-    group_size = HEADS // KV_HEADS
-    scale = HEAD_DIM ** (-0.5)
-    q = queries.reshape(row_count, group_size, HEAD_DIM)
-    scores = jnp.einsum("rgd,rcd->rgc", q, key_cache, preferred_element_type=F4) * scale
-    slot_ids = lax.broadcasted_iota(jnp.int32, (row_count, 1, slot_count), 2)
-    scores = jnp.where(slot_ids < lengths[:, None, None], scores, -jnp.inf)
-    own_score = jnp.einsum("rgd,rd->rg", q, new_keys, preferred_element_type=F4) * scale
-    top = jnp.maximum(jnp.max(scores, axis=2), own_score)
-    weights = jnp.exp(scores - top[..., None])
-    own_weight = jnp.exp(own_score - top)
-    total = jnp.sum(weights, axis=2) + own_weight
-    own_low = own_weight.astype(BF).astype(F4)
-    mixture = jnp.einsum("rgc,rcd->rgd", weights.astype(BF), value_cache, preferred_element_type=F4)
-    mixture = mixture + own_low[..., None] * new_values.astype(F4)[:, None, :]
-    return (mixture / total[..., None]).astype(BF).reshape(row_count, -1)
-
-
 VM = pl.BlockSpec(memory_space=pltpu.VMEM)
 SM = pl.BlockSpec(memory_space=pltpu.SMEM)
+CHUNKS = 2
+
+
+def attention_body(lengths, q, kn, vn, k_hbm, v_hbm, out, keys, values, mixed, sems):
+    row_count, slots = keys.shape[0], keys.shape[1]
+    step = row_count // CHUNKS
+    copies = []
+    for n in range(CHUNKS):
+        cut = pl.ds(n * step, step)
+        copies.append(pltpu.make_async_copy(k_hbm.at[cut], keys.at[cut], sems.at[0, n]))
+        copies.append(pltpu.make_async_copy(v_hbm.at[cut], values.at[cut], sems.at[1, n]))
+    for copy in copies:
+        copy.start()
+    group = HEADS // KV_HEADS
+    scale = HEAD_DIM ** (-0.5)
+    slot_ids = lax.broadcasted_iota(jnp.int32, (group, slots), 1)
+    heads = [q[:, HEAD_DIM * g : HEAD_DIM * (g + 1)].astype(F4) for g in range(group)]
+    new_keys = kn[...].astype(F4)
+    new_values = vn[...].astype(F4)
+    for n in range(CHUNKS):
+        rows = range(n * step, n * step + step)
+        qs = [jnp.concatenate([h[r : r + 1] for h in heads], axis=0) for r in rows]
+        copies[2 * n].wait()
+        ws, tots, owns = [], [], []
+        for r, qr in zip(rows, qs):
+            s = lax.dot_general(
+                qr.astype(BF), keys[r], (((1,), (1,)), ((), ())), preferred_element_type=F4
+            )
+            s = jnp.where(slot_ids < lengths[r], s * scale, -jnp.inf)
+            own = jnp.sum(qr * new_keys[r : r + 1], axis=1, keepdims=True) * scale
+            top = jnp.maximum(jnp.max(s, axis=1, keepdims=True), own)
+            w = jnp.exp(s - top)
+            own = jnp.exp(own - top)
+            tots.append(jnp.sum(w, axis=1, keepdims=True) + own)
+            ws.append(w.astype(BF))
+            owns.append(own.astype(BF).astype(F4))
+        copies[2 * n + 1].wait()
+        for r, w, tot, own in zip(rows, ws, tots, owns):
+            mix = jnp.dot(w, values[r], preferred_element_type=F4) + own * new_values[r : r + 1]
+            mix = mix / tot
+            for g in range(group):
+                mixed[r : r + 1, HEAD_DIM * g : HEAD_DIM * (g + 1)] = mix[g : g + 1]
+    attn = mixed[...].astype(BF)
+    for j in range(out.shape[0]):
+        out[j] = attn
+
+
+def attention(queries, new_keys, new_values, key_cache, value_cache, lengths, copies):
+    rows, slots, dim = key_cache.shape
+    width = queries.shape[1]
+    anywhere = pl.BlockSpec(memory_space=pl.ANY)
+    return pl.pallas_call(
+        attention_body,
+        out_shape=jax.ShapeDtypeStruct((copies, rows, width), BF),
+        in_specs=[SM, VM, VM, VM, anywhere, anywhere],
+        out_specs=VM,
+        scratch_shapes=[
+            pltpu.VMEM((rows, slots, dim), BF),
+            pltpu.VMEM((rows, slots, dim), BF),
+            pltpu.VMEM((rows, width), F4),
+            pltpu.SemaphoreType.DMA((2, CHUNKS)),
+        ],
+        compiler_params=pltpu.CompilerParams(vmem_limit_bytes=60 * 1024 * 1024),
+        cost_estimate=pl.CostEstimate(
+            flops=4 * rows * width * slots, bytes_accessed=4 * rows * slots * dim, transcendentals=0
+        ),
+    )(lengths, queries, new_keys, new_values, key_cache, value_cache)
+
+
 N_CUTS = ((0, 256), (256, 256), (512, 256), (768, 128))
 
 
@@ -109,30 +158,17 @@
     return jax.ShapeDtypeStruct(shape, dtype)
 
 
-def proj_body(at, rows, w0, w1, w2, w3, out, held, sems):
-    copies = [pltpu.make_async_copy(w, held.at[k], sems.at[k]) for k, w in enumerate((w0, w1, w2, w3))]
-    for copy in copies:
-        copy.start()
-    left = rows[...]
-    for k, copy in enumerate(copies):
+def proj_body(at, rows, w0, w1, w2, w3, out):
+    for k, w in enumerate((w0, w1, w2, w3)):
         src = lax.rem(at[0] + 4 - k, 4)
         xh, xl = lax.div(src, 2), lax.rem(src, 2)
-        copy.wait()
-        part = jnp.dot(left, held[k], preferred_element_type=F4)
+        part = jnp.dot(rows[...], w[...], preferred_element_type=F4)
         for j in range(4):
             out[xh * 4 + j, xl] = part[24 * j : 24 * j + 24].astype(BF)
 
 
 def proj(at, rows, weights):
-    moved = 4 * 1024 * 256 * 2
-    return pl.pallas_call(
-        proj_body,
-        out_shape=sds((8, 2, 24, 256), BF),
-        in_specs=[SM, VM] + [pl.BlockSpec(memory_space=pl.ANY)] * 4,
-        out_specs=VM,
-        scratch_shapes=[pltpu.VMEM((4, 1024, 256), BF), pltpu.SemaphoreType.DMA((4,))],
-        cost_estimate=pl.CostEstimate(flops=2 * 96 * 1024 * 1024, bytes_accessed=moved, transcendentals=0),
-    )(at, rows, *weights)
+    return call(proj_body, sds((8, 2, 24, 256), BF), [at, rows, *weights], flops=2 * 96 * 1024 * 1024)
 
 
 def first_body(at, p0, wg, wu, out):
@@ -270,10 +306,10 @@
     gain = lax.dynamic_slice_in_dim(norm_gain, (y * 2 + c) * 1024, 1024, 0).reshape(1, 1024)
     weights = [out_weight, *around(out_weight, X)]
 
-    attn = attention(queries, new_keys, new_values, key_cache, value_cache, lengths)
-    rows = copies_by_a2a(attn, "z", 8).reshape(96, 1024)
+    attn = attention(queries, new_keys, new_values, key_cache, value_cache, lengths, 8)
+    rows = lax.all_to_all(attn, "z", 0, 0, tiled=True).reshape(96, 1024)
     res = residual.reshape(2, 2, 12, 256).swapaxes(0, 1)
-    res, rows = lax.optimization_barrier((res, rows))
+    res, _ = lax.optimization_barrier((res, attn))
     res_same = lax.dynamic_index_in_dim(res, xl, 0, False).reshape(24, 256)
     res_cross = lax.dynamic_index_in_dim(res, 1 - xl, 0, False).reshape(24, 256)
     res_same = lax.ppermute(res_same, ALL, device_pairs(swap_same))

time: 151 us -> 144 us (0.954)
  blocking collectives: 21.2 us -> 26.3 us
  waiting for transfers between devices: 47.6 us -> 43.2 us
  local copies, waits for them, and re-layouts: 7.43 us -> 3.69 us
  Pallas kernels: 12.2 us -> 14.9 us
  starting transfers between devices: 55.5 us -> 52.9 us
  matrix products: 2.39 us -> 0 us
  other arithmetic: 3.09 us -> 0.91 us
    all_to_all x1, waiting for transfers between devices: 10.7 us -> 3.27 us  [local(): rows = lax.all_to_all(attn, 'z', 0, 0, tiled=True).reshape(96, 1024)]
    all_to_all x1, blocking collectives: 21.2 us -> 26.3 us  [copies_by_a2a(): return lax.all_to_all(copies, axis, 0, 0, tiled=True)]
    ppermute x15, starting transfers between devices: 23.1 us -> 18.2 us  [shift(): lax.ppermute(array, axis, [(i, (i + step) % size) for i in range(size)])]
    ppermute x15, waiting for transfers between devices: 17 us -> 19.8 us  [shift(): lax.ppermute(array, axis, [(i, (i + step) % size) for i in range(size)])]
    dot_general x3 -> x0, matrix products: 2.39 us -> none  [the longest x1 1 us: attention(): jnp.einsum('rgd,rcd->rgc', q, key_cache, preferred_element_type=F4) * scale]
    unnamed x25 -> x10, local copies, waits for them, and re-layouts: 3.83 us -> 1.52 us
    pallas_call x7 -> x8, Pallas kernels: 8.45 us -> 9.95 us  [call(): pl.pallas_call(body, out_shape=outs, in_specs=[SM] + [VM] * (len(ins) - 1...]
  transfers between devices with their start and end apart: 25 -> 25, of which waited for: 12 -> 13; matrix products, arithmetic and copies ran while one was open for 6% -> 2% of each run, Pallas kernels for 4% -> 7%
where the time goes in v4:
time: 144 us; the launch traced here: 143 us
  starting transfers between devices  52.9 us (37%)
  waiting for transfers between devices  43.2 us (30%)
  blocking collectives  26.3 us (18%)
  Pallas kernels  14.9 us (10%)
  local copies, waits for them, and re-layouts  3.69 us (3%)
    all_to_all x1, blocking collectives, copies_by_a2a(): return lax.all_to_all(copies, axis, 0, 0, tiled=True)  26.3 us
    ppermute x15, waiting for transfers between devices, shift(): lax.ppermute(array, axis, [(i, (i + step) % size) for i in range(size)])  19.8 us
    ppermute x15, starting transfers between devices, shift(): lax.ppermute(array, axis, [(i, (i + step) % size) for i in range(size)])  18.2 us
    all_to_all x1, waiting for transfers between devices, local(): part = lax.all_to_all(part, 'z', 0, 0, tiled=True)  11.2 us
    pallas_call x8, Pallas kernels, call(): pl.pallas_call(body, out_shape=outs, in_specs=[SM] + [VM] * (len(ins) - 1...  9.95 us
    all_to_all x1, starting transfers between devices, local(): rows = lax.all_to_all(attn, 'z', 0, 0, tiled=True).reshape(96, 1024)  8.48 us
    all_to_all x1, waiting for transfers between devices, local(): pieces = lax.all_to_all(proj(at, rows, weights), HEAD, 0, 0, tiled=True)  6.81 us
    ppermute x1, starting transfers between devices, local(): res_cross = lax.ppermute(res_cross, ALL, device_pairs(swap_cross))  5.95 us
  transfers between devices with their start and end apart: 25, of which 13 were waited for; matrix products, arithmetic and copies ran while one was open for 2% of the time, Pallas kernels for 7%

profile of v4, /device:TPU:6, one launch (start us, length us, event | category | flops | bytes accessed | tf_op | source)
XLA Modules:
  0.0 142.9 jit_solution(13461271155418796286)
XLA Ops:
  0.7 1.5 %collective-permute-start.1 = (bf16[1024,256]{1,0:T(8,128)(2,1)}, bf16[1024,256]{1,0:T(8,128)(2,1)S(1)}, u32[]{:S(2)}, u32[]{:S(2)}) collective-permute-start(bf16[1024,256]{1,0:T(8,128)(2,1)} %w0.1), channel_id=1, source_target_pairs={{0,128},{1,129},{128,0},{129,1},{2,130},{3,131},{130,2},{131,3},{4... | collective-permute-start | bytes 1572872 | tf_op jit(solution)/shard_map/ppermute | solution.py:20
  2.1 2.1 %collective-permute-start = (bf16[1024,256]{1,0:T(8,128)(2,1)}, bf16[1024,256]{1,0:T(8,128)(2,1)}, u32[]{:S(2)}, u32[]{:S(2)}) collective-permute-start(bf16[1024,256]{1,0:T(8,128)(2,1)} %w0.1), channel_id=1, source_target_pairs={{0,1},{1,128},{128,129},{129,0},{2,3},{3,130},{130,131},{131,2},{4... | collective-permute-start | bytes 1572872 | tf_op jit(solution)/shard_map/ppermute | solution.py:20
  4.2 5.0 %shard_map.131 = bf16[8,12,1024]{2,1,0:T(8,128)(2,1)} custom-call(s32[12]{0:T(128)} %lengths.1, bf16[12,1024]{1,0:T(8,128)(2,1)} %q.1, bf16[12,128]{1,0:T(8,128)(2,1)} %kn.1, bf16[12,128]{1,0:T(8,128)(2,1)} %vn.1, bf16[12,1024,128]{2,1,0:T(8,128)(2,1)} %k_hbm.1, bf16[12,1024,128]{2,1,0:T(8,128)(2,1)} %v_hbm.1), custom_call_target="tpu_custom_call" | custom-call | flops 50331648 | bytes 6291456 | tf_op jit(solution)/shard_map/pallas_call | solution.py:123
  9.3 8.5 %all-to-all-start = ((bf16[8,12,1024]{2,1,0:T(8,128)(2,1)}), bf16[8,12,1024]{2,1,0:T(8,128)(2,1)S(1)}, u32[]{:S(2)}, u32[]{:S(2)}) async-start(bf16[8,12,1024]{2,1,0:T(8,128)(2,1)} %shard_map.131), calls=%async_computation | async-start | bytes 524288 | tf_op jit(solution)/shard_map/all_to_all | solution.py:310
  17.8 6.0 %collective-permute-start.4 = (bf16[24,256]{1,0:T(8,128)(2,1)S(1)}, bf16[24,256]{1,0:T(8,128)(2,1)S(1)}, u32[]{:S(2)}, u32[]{:S(2)}) collective-permute-start(bf16[24,256]{1,0:T(8,128)(2,1)S(1)} %reshape.38), channel_id=1, source_target_pairs={{0,1},{1,0},{2,3},{3,2},{4,5},{5,4},{6,7},{7,6},{8,129},{9,128},{1... | collective-permute-start | bytes 36872 | tf_op jit(solution)/shard_map/ppermute | solution.py:316
  23.8 1.9 %collective-permute-start.3 = (bf16[24,256]{1,0:T(8,128)(2,1)S(1)}, bf16[24,256]{1,0:T(8,128)(2,1)S(1)}, u32[]{:S(2)}, u32[]{:S(2)}) collective-permute-start(bf16[24,256]{1,0:T(8,128)(2,1)S(1)} %reshape.37), channel_id=1, source_target_pairs={{0,0},{1,1},{2,2},{3,3},{4,4},{5,5},{6,6},{7,7},{8,128},{9,129},{1... | collective-permute-start | bytes 36872 | tf_op jit(solution)/shard_map/ppermute | solution.py:315
  25.8 3.3 %all-to-all-done = bf16[8,12,1024]{2,1,0:T(8,128)(2,1)S(1)} async-done(((bf16[8,12,1024]{2,1,0:T(8,128)(2,1)}), bf16[8,12,1024]{2,1,0:T(8,128)(2,1)S(1)}, u32[]{:S(2)}, u32[]{:S(2)}) %all-to-all-start) | async-done | bytes 196640 | tf_op jit(solution)/shard_map/all_to_all | solution.py:310
  29.2 2.5 %shard_map.132 = bf16[8,2,24,256]{3,2,1,0:T(8,128)(2,1)} custom-call(s32[4]{0:T(128)S(1)} %pad_add_fusion.at.refs_0_, bf16[96,1024]{1,0:T(8,128)(2,1)S(1)} %reshape.35.rows, bf16[1024,256]{1,0:T(8,128)(2,1)S(1)} %copy-done.2, bf16[1024,256]{1,0:T(8,128)(2,1)} %collective-permute-done.w1, bf16[1024,256]{1,0:T(8,128)(2,1)S(1)} %collective-permute-done.1.w2, ...), custom_call_target="tpu_custom_call" | custom-call | flops 201326592 | bytes 2293776 | tf_op jit(solution)/shard_map/pallas_call | solution.py:146
  31.6 4.5 %all-to-all-start.1 = ((bf16[8,2,24,256]{3,2,1,0:T(8,128)(2,1)}), bf16[8,2,24,256]{3,2,1,0:T(8,128)(2,1)S(1)}, u32[]{:S(2)}, u32[]{:S(2)}) async-start(bf16[8,2,24,256]{3,2,1,0:T(8,128)(2,1)} %shard_map.132), calls=%async_computation.1 | async-start | bytes 393216 | tf_op jit(solution)/shard_map/all_to_all | solution.py:319
  36.1 6.8 %all-to-all-done.1 = bf16[8,2,24,256]{3,2,1,0:T(8,128)(2,1)S(1)} async-done(((bf16[8,2,24,256]{3,2,1,0:T(8,128)(2,1)}), bf16[8,2,24,256]{3,2,1,0:T(8,128)(2,1)S(1)}, u32[]{:S(2)}, u32[]{:S(2)}) %all-to-all-start.1) | async-done | bytes 196640 | tf_op jit(solution)/shard_map/all_to_all | solution.py:319
  43.7 26.3 %all_to_all.20.p0.refs_2_ = bf16[8,24,512]{2,1,0:T(8,128)(2,1)S(1)} all-to-all(bf16[8,24,512]{2,1,0:T(8,128)(2,1)S(1)} %broadcast_in_dim.3), channel_id=1, replica_groups=mesh['xh'=2,'z'=8,'y'=4,'c'=2,'xl'=2] {'z'}, dimensions={0} | all-to-all | bytes 393216 | tf_op jit(solution)/shard_map/all_to_all | solution.py:25
  70.0 1.9 %collective-permute-start.9 = (bf16[8,24,512]{2,1,0:T(8,128)(2,1)S(1)}, bf16[8,24,512]{2,1,0:T(8,128)(2,1)S(1)}, u32[]{:S(2)}, u32[]{:S(2)}) collective-permute-start(bf16[8,24,512]{2,1,0:T(8,128)(2,1)S(1)} %all_to_all.20.p0.refs_2_), channel_id=1, source_target_pairs={{0,128},{1,129},{128,0},{129,1},{2,130},{3,131},{130,2},{131,3},{4... | collective-permute-start | bytes 589832 | tf_op jit(solution)/shard_map/ppermute | solution.py:20
  72.0 2.0 %collective-permute-start.8 = (bf16[8,24,512]{2,1,0:T(8,128)(2,1)S(1)}, bf16[8,24,512]{2,1,0:T(8,128)(2,1)S(1)}, u32[]{:S(2)}, u32[]{:S(2)}) collective-permute-start(bf16[8,24,512]{2,1,0:T(8,128)(2,1)S(1)} %all_to_all.20.p0.refs_2_), channel_id=1, source_target_pairs={{0,1},{1,128},{128,129},{129,0},{2,3},{3,130},{130,131},{131,2},{4... | collective-permute-start | bytes 589832 | tf_op jit(solution)/shard_map/ppermute | solution.py:20
  74.7 1.5 %copy-done.1 = bf16[1024,896]{1,0:T(8,128)(2,1)S(1)} copy-done((bf16[1024,896]{1,0:T(8,128)(2,1)S(1)}, bf16[1024,896]{1,0:T(8,128)(2,1)}, u32[]{:S(2)}) %copy-start.1) | copy-done | bytes 1835032
  76.8 2.2 %collective-permute-done.10.refs_5_ = bf16[8,24,512]{2,1,0:T(8,128)(2,1)S(1)} collective-permute-done((bf16[8,24,512]{2,1,0:T(8,128)(2,1)S(1)}, bf16[8,24,512]{2,1,0:T(8,128)(2,1)S(1)}, u32[]{:S(2)}, u32[]{:S(2)}) %collective-permute-start.10) | collective-permute-done | bytes 196640 | tf_op jit(solution)/shard_map/ppermute | solution.py:20
  79.0 0.9 collective-permute-done.8.refs_3_
  79.9 1.6 %shard_map.135 = bf16[4,48,1920]{2,1,0:T(8,128)(2,1)S(1)} custom-call(s32[4]{0:T(128)S(1)} %pad_add_fusion.at.refs_0_, f32[8,24,128]{2,1,0:T(8,128)S(1)} %shard_map.133.refs_1_, bf16[8,24,512]{2,1,0:T(8,128)(2,1)S(1)} %all_to_all.20.p0.refs_2_, bf16[8,24,512]{2,1,0:T(8,128)(2,1)S(1)} %collective-permute-done.8.refs_3_, ...), custom_call_target="tpu_custom_call" | custom-call | flops 704643072 | bytes 4558864 | tf_op jit(solution)/shard_map/pallas_call | solution.py:146
  81.6 1.6 %shard_map.134.mine = f32[4,48,1920]{2,1,0:T(8,128)S(1)} custom-call(s32[4]{0:T(128)S(1)} %pad_add_fusion.at.refs_0_, f32[8,24,128]{2,1,0:T(8,128)S(1)} %shard_map.133.refs_1_, bf16[8,24,512]{2,1,0:T(8,128)(2,1)S(1)} %all_to_all.20.p0.refs_2_, bf16[8,24,512]{2,1,0:T(8,128)(2,1)S(1)} %collective-permute-done.8.refs_3_, ...), custom_call_target="tpu_custom_call" | custom-call | flops 704643072 | bytes 4558864 | tf_op jit(solution)/shard_map/pallas_call | solution.py:146
  85.4 2.4 %collective-permute-start.14 = (bf16[48,1920]{1,0:T(8,128)(2,1)S(1)}, bf16[48,1920]{1,0:T(8,128)(2,1)S(1)}, u32[]{:S(2)}, u32[]{:S(2)}) collective-permute-start(bf16[48,1920]{1,0:T(8,128)(2,1)S(1)} %get-tuple-element.15), channel_id=1, source_target_pairs={{0,12},{4,0},{8,4},{12,8},{1,13},{5,1},{9,5},{13,9},{2,14},{6,2},{... | collective-permute-start | bytes 552968 | tf_op jit(solution)/shard_map/ppermute | solution.py:20
  87.8 8.6 %collective-permute-done.12.r1 = bf16[48,1920]{1,0:T(8,128)(2,1)S(1)} collective-permute-done((bf16[48,1920]{1,0:T(8,128)(2,1)S(1)}, bf16[48,1920]{1,0:T(8,128)(2,1)S(1)}, u32[]{:S(2)}, u32[]{:S(2)}) %collective-permute-start.12) | collective-permute-done | bytes 184352 | tf_op jit(solution)/shard_map/ppermute | solution.py:20
  97.8 2.6 %collective-permute-start.17 = (bf16[48,896]{1,0:T(8,128)(2,1)S(1)}, bf16[48,896]{1,0:T(8,128)(2,1)S(1)}, u32[]{:S(2)}, u32[]{:S(2)}) collective-permute-start(bf16[48,896]{1,0:T(8,128)(2,1)S(1)} %shard_map.137.p0), channel_id=1, source_target_pairs={{0,12},{4,0},{8,4},{12,8},{1,13},{5,1},{9,5},{13,9},{2,14},{6,2},{... | collective-permute-start | bytes 258056 | tf_op jit(solution)/shard_map/ppermute | solution.py:20
  100.4 1.0 collective-permute-start.15
  101.3 2.6 %collective-permute-done.17.p3 = bf16[48,896]{1,0:T(8,128)(2,1)S(1)} collective-permute-done((bf16[48,896]{1,0:T(8,128)(2,1)S(1)}, bf16[48,896]{1,0:T(8,128)(2,1)S(1)}, u32[]{:S(2)}, u32[]{:S(2)}) %collective-permute-start.17) | collective-permute-done | bytes 86048 | tf_op jit(solution)/shard_map/ppermute | solution.py:20
  103.9 2.8 %collective-permute-done.16.p2 = bf16[48,896]{1,0:T(8,128)(2,1)S(1)} collective-permute-done((bf16[48,896]{1,0:T(8,128)(2,1)S(1)}, bf16[48,896]{1,0:T(8,128)(2,1)S(1)}, u32[]{:S(2)}, u32[]{:S(2)}) %collective-permute-start.16) | collective-permute-done | bytes 86048 | tf_op jit(solution)/shard_map/ppermute | solution.py:20
  108.0 1.6 %collective-permute-done.18.theirs = bf16[4,48,896]{2,1,0:T(8,128)(2,1)S(1)} collective-permute-done((bf16[4,48,896]{2,1,0:T(8,128)(2,1)S(1)}, bf16[4,48,896]{2,1,0:T(8,128)(2,1)S(1)}, u32[]{:S(2)}, u32[]{:S(2)}) %collective-permute-start.18) | collective-permute-done | bytes 344096 | tf_op jit(solution)/shard_map/ppermute | solution.py:42
  109.6 1.6 %shard_map.139 = (f32[4,24,1024]{2,1,0:T(8,128)S(1)}, bf16[4,24,1024]{2,1,0:T(8,128)(2,1)S(1)}, bf16[4,24,1024]{2,1,0:T(8,128)(2,1)S(1)}, bf16[4,24,1024]{2,1,0:T(8,128)(2,1)S(1)}) custom-call(s32[4]{0:T(128)S(1)} %pad_add_fusion.at.refs_0_, bf16[4,48,896]{2,1,0:T(8,128)(2,1)S(1)} %shard_map.138.mine, ...), custom_call_target="tpu_custom_call" | custom-call | flops 704643072 | bytes 2523152 | tf_op jit(solution)/shard_map/pallas_call | solution.py:146
  111.2 2.7 %collective-permute-start.19 = (bf16[4,24,1024]{2,1,0:T(8,128)(2,1)S(1)}, bf16[4,24,1024]{2,1,0:T(8,128)(2,1)S(1)}, u32[]{:S(2)}, u32[]{:S(2)}) collective-permute-start(bf16[4,24,1024]{2,1,0:T(8,128)(2,1)S(1)} %get-tuple-element.17), channel_id=1, source_target_pairs={{0,1},{1,128},{128,129},{129,0},{2,3},{3,130},{130,131},{131,2},{4... | collective-permute-start | bytes 589832 | tf_op jit(solution)/shard_map/ppermute | solution.py:20
  115.0 5.0 %collective-permute-start.5 = (bf16[24,256]{1,0:T(8,128)(2,1)S(1)}, bf16[24,256]{1,0:T(8,128)(2,1)S(1)}, u32[]{:S(2)}, u32[]{:S(2)}) collective-permute-start(bf16[24,256]{1,0:T(8,128)(2,1)S(1)} %get-tuple-element.24), channel_id=1, source_target_pairs={{0,0},{1,1},{2,2},{3,3},{4,4},{5,5},{6,6},{7,7},{8,128},{9,129},{1... | collective-permute-start | bytes 36872 | tf_op jit(solution)/shard_map/ppermute | solution.py:327
  120.0 4.6 %collective-permute-start.6 = (bf16[24,256]{1,0:T(8,128)(2,1)S(1)}, bf16[24,256]{1,0:T(8,128)(2,1)S(1)}, u32[]{:S(2)}, u32[]{:S(2)}) collective-permute-start(bf16[24,256]{1,0:T(8,128)(2,1)S(1)} %get-tuple-element.25), channel_id=1, source_target_pairs={{0,1},{1,0},{2,3},{3,2},{4,5},{5,4},{6,7},{7,6},{8,129},{9,128},{1... | collective-permute-start | bytes 36872 | tf_op jit(solution)/shard_map/ppermute | solution.py:328
  124.6 1.5 %collective-permute-done.21 = bf16[4,24,1024]{2,1,0:T(8,128)(2,1)S(1)} collective-permute-done((bf16[4,24,1024]{2,1,0:T(8,128)(2,1)S(1)}, bf16[4,24,1024]{2,1,0:T(8,128)(2,1)S(1)}, u32[]{:S(2)}, u32[]{:S(2)}) %collective-permute-start.21) | collective-permute-done | bytes 196640 | tf_op jit(solution)/shard_map/ppermute | solution.py:20
  126.9 3.4 %all-to-all-start.3 = ((bf16[8,12,1024]{2,1,0:T(8,128)(2,1)}), bf16[8,12,1024]{2,1,0:T(8,128)(2,1)S(1)}, u32[]{:S(2)}, u32[]{:S(2)}) async-start(bf16[8,12,1024]{2,1,0:T(8,128)(2,1)} %reshape.42), calls=%async_computation.3 | async-start | bytes 524288 | tf_op jit(solution)/shard_map/all_to_all | solution.py:346
  131.0 11.2 %all-to-all-done.3 = bf16[8,12,1024]{2,1,0:T(8,128)(2,1)S(1)} async-done(((bf16[8,12,1024]{2,1,0:T(8,128)(2,1)}), bf16[8,12,1024]{2,1,0:T(8,128)(2,1)S(1)}, u32[]{:S(2)}, u32[]{:S(2)}) %all-to-all-start.3) | async-done | bytes 196640 | tf_op jit(solution)/shard_map/all_to_all | solution.py:346
  (61 shorter events, 10.2 us)
Async XLA Ops:
  0.6 28.5 %copy-start.2 = (bf16[1024,256]{1,0:T(8,128)(2,1)S(1)}, bf16[1024,256]{1,0:T(8,128)(2,1)}, u32[]{:S(2)}) copy-start(bf16[1024,256]{1,0:T(8,128)(2,1)} %w0.1) | copy-start | bytes 1572868
  0.6 17.1 %copy-start.4 = (bf16[48,256]{1,0:T(8,128)(2,1)S(1)}, bf16[48,256]{1,0:T(8,128)(2,1)}, u32[]{:S(2)}) copy-start(bf16[48,256]{1,0:T(8,128)(2,1)} %param.18) | copy-start | bytes 73732
  0.7 28.5 %collective-permute-start.1 = (bf16[1024,256]{1,0:T(8,128)(2,1)}, bf16[1024,256]{1,0:T(8,128)(2,1)S(1)}, u32[]{:S(2)}, u32[]{:S(2)}) collective-permute-start(bf16[1024,256]{1,0:T(8,128)(2,1)} %w0.1), channel_id=1, source_target_pairs={{0,128},{1,129},{128,0},{129,1},{2,130},{3,131},{130,2},{131,3},{4... | collective-permute-start | bytes 1572872 | tf_op jit(solution)/shard_map/ppermute | solution.py:20
  2.1 27.0 %collective-permute-start = (bf16[1024,256]{1,0:T(8,128)(2,1)}, bf16[1024,256]{1,0:T(8,128)(2,1)}, u32[]{:S(2)}, u32[]{:S(2)}) collective-permute-start(bf16[1024,256]{1,0:T(8,128)(2,1)} %w0.1), channel_id=1, source_target_pairs={{0,1},{1,128},{128,129},{129,0},{2,3},{3,130},{130,131},{131,2},{4... | collective-permute-start | bytes 1572872 | tf_op jit(solution)/shard_map/ppermute | solution.py:20
  4.2 24.9 %collective-permute-start.2 = (bf16[1024,256]{1,0:T(8,128)(2,1)}, bf16[1024,256]{1,0:T(8,128)(2,1)}, u32[]{:S(2)}, u32[]{:S(2)}) collective-permute-start(bf16[1024,256]{1,0:T(8,128)(2,1)} %w0.1), channel_id=1, source_target_pairs={{0,129},{1,0},{128,1},{129,128},{2,131},{3,2},{130,3},{131,130},{4... | collective-permute-start | bytes 1572872 | tf_op jit(solution)/shard_map/ppermute | solution.py:20
  9.3 19.8 %all-to-all-start = ((bf16[8,12,1024]{2,1,0:T(8,128)(2,1)}), bf16[8,12,1024]{2,1,0:T(8,128)(2,1)S(1)}, u32[]{:S(2)}, u32[]{:S(2)}) async-start(bf16[8,12,1024]{2,1,0:T(8,128)(2,1)} %shard_map.131), calls=%async_computation | async-start | bytes 524288 | tf_op jit(solution)/shard_map/all_to_all | solution.py:310
  17.8 18.3 %collective-permute-start.4 = (bf16[24,256]{1,0:T(8,128)(2,1)S(1)}, bf16[24,256]{1,0:T(8,128)(2,1)S(1)}, u32[]{:S(2)}, u32[]{:S(2)}) collective-permute-start(bf16[24,256]{1,0:T(8,128)(2,1)S(1)} %reshape.38), channel_id=1, source_target_pairs={{0,1},{1,0},{2,3},{3,2},{4,5},{5,4},{6,7},{7,6},{8,129},{9,128},{1... | collective-permute-start | bytes 36872 | tf_op jit(solution)/shard_map/ppermute | solution.py:316
  23.8 12.4 %collective-permute-start.3 = (bf16[24,256]{1,0:T(8,128)(2,1)S(1)}, bf16[24,256]{1,0:T(8,128)(2,1)S(1)}, u32[]{:S(2)}, u32[]{:S(2)}) collective-permute-start(bf16[24,256]{1,0:T(8,128)(2,1)S(1)} %reshape.37), channel_id=1, source_target_pairs={{0,0},{1,1},{2,2},{3,3},{4,4},{5,5},{6,6},{7,7},{8,128},{9,129},{1... | collective-permute-start | bytes 36872 | tf_op jit(solution)/shard_map/ppermute | solution.py:315
  29.1 45.6 %copy-start = (bf16[1024,896]{1,0:T(8,128)(2,1)S(1)}, bf16[1024,896]{1,0:T(8,128)(2,1)}, u32[]{:S(2)}) copy-start(bf16[1024,896]{1,0:T(8,128)(2,1)} %refs_7_.3) | copy-start | bytes 5505028
  31.6 11.3 %all-to-all-start.1 = ((bf16[8,2,24,256]{3,2,1,0:T(8,128)(2,1)}), bf16[8,2,24,256]{3,2,1,0:T(8,128)(2,1)S(1)}, u32[]{:S(2)}, u32[]{:S(2)}) async-start(bf16[8,2,24,256]{3,2,1,0:T(8,128)(2,1)} %shard_map.132), calls=%async_computation.1 | async-start | bytes 393216 | tf_op jit(solution)/shard_map/all_to_all | solution.py:319
  43.0 0.7 collective-permute-start.7
  70.0 9.0 %collective-permute-start.10 = (bf16[8,24,512]{2,1,0:T(8,128)(2,1)S(1)}, bf16[8,24,512]{2,1,0:T(8,128)(2,1)S(1)}, u32[]{:S(2)}, u32[]{:S(2)}) collective-permute-start(bf16[8,24,512]{2,1,0:T(8,128)(2,1)S(1)} %all_to_all.20.p0.refs_2_), channel_id=1, source_target_pairs={{0,129},{1,0},{128,1},{129,128},{2,131},{3,2},{130,3},{131,130},{4... | collective-permute-start | bytes 589832 | tf_op jit(solution)/shard_map/ppermute | solution.py:20
  70.0 9.0 %collective-permute-start.9 = (bf16[8,24,512]{2,1,0:T(8,128)(2,1)S(1)}, bf16[8,24,512]{2,1,0:T(8,128)(2,1)S(1)}, u32[]{:S(2)}, u32[]{:S(2)}) collective-permute-start(bf16[8,24,512]{2,1,0:T(8,128)(2,1)S(1)} %all_to_all.20.p0.refs_2_), channel_id=1, source_target_pairs={{0,128},{1,129},{128,0},{129,1},{2,130},{3,131},{130,2},{131,3},{4... | collective-permute-start | bytes 589832 | tf_op jit(solution)/shard_map/ppermute | solution.py:20
  72.0 7.9 %collective-permute-start.8 = (bf16[8,24,512]{2,1,0:T(8,128)(2,1)S(1)}, bf16[8,24,512]{2,1,0:T(8,128)(2,1)S(1)}, u32[]{:S(2)}, u32[]{:S(2)}) collective-permute-start(bf16[8,24,512]{2,1,0:T(8,128)(2,1)S(1)} %all_to_all.20.p0.refs_2_), channel_id=1, source_target_pairs={{0,1},{1,128},{128,129},{129,0},{2,3},{3,130},{130,131},{131,2},{4... | collective-permute-start | bytes 589832 | tf_op jit(solution)/shard_map/ppermute | solution.py:20
  74.7 1.5 %copy-start.1 = (bf16[1024,896]{1,0:T(8,128)(2,1)S(1)}, bf16[1024,896]{1,0:T(8,128)(2,1)}, u32[]{:S(2)}) copy-start(bf16[1024,896]{1,0:T(8,128)(2,1)} %refs_8_.3) | copy-start | bytes 5505028
  81.5 2.3 %collective-permute-start.11 = (bf16[4,48,1920]{2,1,0:T(8,128)(2,1)S(1)}, bf16[4,48,1920]{2,1,0:T(8,128)(2,1)S(1)}, u32[]{:S(2)}, u32[]{:S(2)}) collective-permute-start(bf16[4,48,1920]{2,1,0:T(8,128)(2,1)S(1)} %shard_map.135), channel_id=1, source_target_pairs={{0,2},{2,0},{1,3},{3,1},{4,6},{6,4},{5,7},{7,5},{8,10},{10,8},{9,1... | collective-permute-start | bytes 2211848 | tf_op jit(solution)/shard_map/ppermute | solution.py:42
  83.3 26.4 %copy-start.3 = (bf16[896,1024]{1,0:T(8,128)(2,1)S(1)}, bf16[896,1024]{1,0:T(8,128)(2,1)}, u32[]{:S(2)}) copy-start(bf16[896,1024]{1,0:T(8,128)(2,1)} %w.1) | copy-start | bytes 5505028
  84.5 11.9 %collective-permute-start.12 = (bf16[48,1920]{1,0:T(8,128)(2,1)S(1)}, bf16[48,1920]{1,0:T(8,128)(2,1)S(1)}, u32[]{:S(2)}, u32[]{:S(2)}) collective-permute-start(bf16[48,1920]{1,0:T(8,128)(2,1)S(1)} %get-tuple-element.13), channel_id=1, source_target_pairs={{0,4},{4,8},{8,12},{12,0},{1,5},{5,9},{9,13},{13,1},{2,6},{6,10},{... | collective-permute-start | bytes 552968 | tf_op jit(solution)/shard_map/ppermute | solution.py:20
  84.6 11.8 %collective-permute-start.13 = (bf16[48,1920]{1,0:T(8,128)(2,1)S(1)}, bf16[48,1920]{1,0:T(8,128)(2,1)S(1)}, u32[]{:S(2)}, u32[]{:S(2)}) collective-permute-start(bf16[48,1920]{1,0:T(8,128)(2,1)S(1)} %get-tuple-element.14), channel_id=1, source_target_pairs={{0,8},{4,12},{8,0},{12,4},{1,9},{5,13},{9,1},{13,5},{2,10},{6,14},... | collective-permute-start | bytes 552968 | tf_op jit(solution)/shard_map/ppermute | solution.py:20
  85.4 11.6 %collective-permute-start.14 = (bf16[48,1920]{1,0:T(8,128)(2,1)S(1)}, bf16[48,1920]{1,0:T(8,128)(2,1)S(1)}, u32[]{:S(2)}, u32[]{:S(2)}) collective-permute-start(bf16[48,1920]{1,0:T(8,128)(2,1)S(1)} %get-tuple-element.15), channel_id=1, source_target_pairs={{0,12},{4,0},{8,4},{12,8},{1,13},{5,1},{9,5},{13,9},{2,14},{6,2},{... | collective-permute-start | bytes 552968 | tf_op jit(solution)/shard_map/ppermute | solution.py:20
  97.8 6.1 %collective-permute-start.17 = (bf16[48,896]{1,0:T(8,128)(2,1)S(1)}, bf16[48,896]{1,0:T(8,128)(2,1)S(1)}, u32[]{:S(2)}, u32[]{:S(2)}) collective-permute-start(bf16[48,896]{1,0:T(8,128)(2,1)S(1)} %shard_map.137.p0), channel_id=1, source_target_pairs={{0,12},{4,0},{8,4},{12,8},{1,13},{5,1},{9,5},{13,9},{2,14},{6,2},{... | collective-permute-start | bytes 258056 | tf_op jit(solution)/shard_map/ppermute | solution.py:20
  100.4 6.4 %collective-permute-start.16 = (bf16[48,896]{1,0:T(8,128)(2,1)S(1)}, bf16[48,896]{1,0:T(8,128)(2,1)S(1)}, u32[]{:S(2)}, u32[]{:S(2)}) collective-permute-start(bf16[48,896]{1,0:T(8,128)(2,1)S(1)} %shard_map.137.p0), channel_id=1, source_target_pairs={{0,8},{4,12},{8,0},{12,4},{1,9},{5,13},{9,1},{13,5},{2,10},{6,14},... | collective-permute-start | bytes 258056 | tf_op jit(solution)/shard_map/ppermute | solution.py:20
  100.4 6.9 %collective-permute-start.15 = (bf16[48,896]{1,0:T(8,128)(2,1)S(1)}, bf16[48,896]{1,0:T(8,128)(2,1)S(1)}, u32[]{:S(2)}, u32[]{:S(2)}) collective-permute-start(bf16[48,896]{1,0:T(8,128)(2,1)S(1)} %shard_map.137.p0), channel_id=1, source_target_pairs={{0,4},{4,8},{8,12},{12,0},{1,5},{5,9},{9,13},{13,1},{2,6},{6,10},{... | collective-permute-start | bytes 258056 | tf_op jit(solution)/shard_map/ppermute | solution.py:20
  107.9 1.7 %collective-permute-start.18 = (bf16[4,48,896]{2,1,0:T(8,128)(2,1)S(1)}, bf16[4,48,896]{2,1,0:T(8,128)(2,1)S(1)}, u32[]{:S(2)}, u32[]{:S(2)}) collective-permute-start(bf16[4,48,896]{2,1,0:T(8,128)(2,1)S(1)} %shard_map.138.mine), channel_id=1, source_target_pairs={{0,2},{2,0},{1,3},{3,1},{4,6},{6,4},{5,7},{7,5},{8,10},{10,8},{9,1... | collective-permute-start | bytes 1032200 | tf_op jit(solution)/shard_map/ppermute | solution.py:42
  111.2 13.3 %collective-permute-start.19 = (bf16[4,24,1024]{2,1,0:T(8,128)(2,1)S(1)}, bf16[4,24,1024]{2,1,0:T(8,128)(2,1)S(1)}, u32[]{:S(2)}, u32[]{:S(2)}) collective-permute-start(bf16[4,24,1024]{2,1,0:T(8,128)(2,1)S(1)} %get-tuple-element.17), channel_id=1, source_target_pairs={{0,1},{1,128},{128,129},{129,0},{2,3},{3,130},{130,131},{131,2},{4... | collective-permute-start | bytes 589832 | tf_op jit(solution)/shard_map/ppermute | solution.py:20
  114.0 10.6 %collective-permute-start.20 = (bf16[4,24,1024]{2,1,0:T(8,128)(2,1)S(1)}, bf16[4,24,1024]{2,1,0:T(8,128)(2,1)S(1)}, u32[]{:S(2)}, u32[]{:S(2)}) collective-permute-start(bf16[4,24,1024]{2,1,0:T(8,128)(2,1)S(1)} %get-tuple-element.18), channel_id=1, source_target_pairs={{0,128},{1,129},{128,0},{129,1},{2,130},{3,131},{130,2},{131,3},{4... | collective-permute-start | bytes 589832 | tf_op jit(solution)/shard_map/ppermute | solution.py:20
  114.2 11.9 %collective-permute-start.21 = (bf16[4,24,1024]{2,1,0:T(8,128)(2,1)S(1)}, bf16[4,24,1024]{2,1,0:T(8,128)(2,1)S(1)}, u32[]{:S(2)}, u32[]{:S(2)}) collective-permute-start(bf16[4,24,1024]{2,1,0:T(8,128)(2,1)S(1)} %get-tuple-element.19), channel_id=1, source_target_pairs={{0,129},{1,0},{128,1},{129,128},{2,131},{3,2},{130,3},{131,130},{4... | collective-permute-start | bytes 589832 | tf_op jit(solution)/shard_map/ppermute | solution.py:20
  115.0 15.4 %collective-permute-start.5 = (bf16[24,256]{1,0:T(8,128)(2,1)S(1)}, bf16[24,256]{1,0:T(8,128)(2,1)S(1)}, u32[]{:S(2)}, u32[]{:S(2)}) collective-permute-start(bf16[24,256]{1,0:T(8,128)(2,1)S(1)} %get-tuple-element.24), channel_id=1, source_target_pairs={{0,0},{1,1},{2,2},{3,3},{4,4},{5,5},{6,6},{7,7},{8,128},{9,129},{1... | collective-permute-start | bytes 36872 | tf_op jit(solution)/shard_map/ppermute | solution.py:327
  120.0 10.4 %collective-permute-start.6 = (bf16[24,256]{1,0:T(8,128)(2,1)S(1)}, bf16[24,256]{1,0:T(8,128)(2,1)S(1)}, u32[]{:S(2)}, u32[]{:S(2)}) collective-permute-start(bf16[24,256]{1,0:T(8,128)(2,1)S(1)} %get-tuple-element.25), channel_id=1, source_target_pairs={{0,1},{1,0},{2,3},{3,2},{4,5},{5,4},{6,7},{7,6},{8,129},{9,128},{1... | collective-permute-start | bytes 36872 | tf_op jit(solution)/shard_map/ppermute | solution.py:328
  126.9 15.3 %all-to-all-start.3 = ((bf16[8,12,1024]{2,1,0:T(8,128)(2,1)}), bf16[8,12,1024]{2,1,0:T(8,128)(2,1)S(1)}, u32[]{:S(2)}, u32[]{:S(2)}) async-start(bf16[8,12,1024]{2,1,0:T(8,128)(2,1)} %reshape.42), calls=%async_computation.3 | async-start | bytes 524288 | tf_op jit(solution)/shard_map/all_to_all | solution.py:346

commit v5 on v4

--- a/solution.py
+++ b/solution.py
@@ -249,29 +249,43 @@
         out[lax.rem(at[1] + 4 - k, 4)] = p[...]
 
 
-def down_body(at, mine, theirs, w, own, s1, s2, s3, acc):
-    for rows, z1 in ((mine, at[2]), (theirs, 1 - at[2])):
-        left = rows[...].reshape(192, 896)
-        for n in range(4):
-            part = jnp.dot(left, w[:, 256 * n : 256 * n + 256], preferred_element_type=F4)
-            for b in range(4):
-                for xl in range(2):
-                    r = b * 48 + xl * 24
-                    acc[(b // 2) * 2 + xl, (b % 2) * 2 + z1, :, 256 * n : 256 * n + 256] = part[r : r + 24]
-    own[...] = acc[at[0]]
-    for k, ref in ((1, s1), (2, s2), (3, s3)):
-        ref[...] = acc[lax.rem(at[0] + k, 4)].astype(BF)
-
-
-def down(at, mine, theirs, weight):
+def down_rows(rows, w, acc):
+    left = rows[...].reshape(192, 896)
+    for n in range(4):
+        part = jnp.dot(left, w[:, 256 * n : 256 * n + 256], preferred_element_type=F4)
+        for b in range(4):
+            for xl in range(2):
+                r = b * 48 + xl * 24
+                acc[(b // 2) * 2 + xl, b % 2, :, 256 * n : 256 * n + 256] = part[r : r + 24]
+
+
+def down_mine_body(at, mine, w, acc):
+    down_rows(mine, w, acc)
+
+
+def down_body(at, ready, theirs, w, own, s1, s2, s3, acc):
+    down_rows(theirs, w, acc)
+    for k, ref in enumerate((own, s1, s2, s3)):
+        to = lax.rem(at[0] + k, 4)
+        for z2 in range(2):
+            ref[z2 * 2 + at[2]] = ready[to, z2].astype(ref.dtype)
+            ref[z2 * 2 + 1 - at[2]] = acc[to, z2].astype(ref.dtype)
+
+
+def down(at, mine, weight):
     outs = [sds((4, 24, 1024), F4)] + [sds((4, 24, 1024), BF)] * 3
-    return call(
-        down_body,
-        outs,
-        [at, mine, theirs, weight],
-        [pltpu.VMEM((4, 4, 24, 1024), F4)],
-        flops=2 * 384 * 896 * 1024,
-    )
+    acc = (4, 2, 24, 1024)
+    theirs = swapped(mine, "c")
+    flops = 192 * 896 * 1024 * 2
+    ready = call(down_mine_body, sds(acc, F4), [at, mine, weight], flops=flops)
+    return call(down_body, outs, [at, ready, theirs, weight], [pltpu.VMEM(acc, F4)], flops=flops)
+
+
+def last_body(at, own, r1, r2, r3, out):
+    for j in range(4):
+        total = own[j] + r1[j].astype(F4) + r2[j].astype(F4) + r3[j].astype(F4)
+        out[2 * j] = total[:12].astype(BF)
+        out[2 * j + 1] = total[12:].astype(BF)
 
 
 def around(array, axis):
@@ -338,11 +352,8 @@
     own, *shares = pair_sums(at, mine, theirs)
     hidden = call(hidden_body, sds((48, 896), BF), [at, own, *sent(*shares, "y")])
     hidden = call(order_body, sds((4, 48, 896), BF), [at, hidden, *around(hidden, "y")])
-    own, *shares = down(at, hidden, swapped(hidden, "c"), down_weight)
-    part = own
-    for got in sent(*shares, X):
-        part = part + got.astype(F4)
-    part = part.astype(BF).reshape(8, 12, 1024)
+    own, *shares = down(at, hidden, down_weight)
+    part = call(last_body, sds((8, 12, 1024), BF), [at, own, *sent(*shares, X)])
     part = lax.all_to_all(part, "z", 0, 0, tiled=True)
     ffn_out = jnp.sum(part.astype(F4), axis=0).astype(BF)
     return (hidden_state, ffn_out)

time: 144 us -> 144 us (level)
  Pallas kernels: 14.9 us -> 17 us
    pallas_call x8 -> x10, Pallas kernels: 9.95 us -> 12 us  [call(): pl.pallas_call(body, out_shape=outs, in_specs=[SM] + [VM] * (len(ins) - 1...]
  transfers between devices with their start and end apart: 25 -> 25, of which waited for: 13 -> 13; matrix products, arithmetic and copies ran while one was open for 2% -> 1% of each run, Pallas kernels for 7% -> 8%
where the time goes in v5:
time: 144 us; the launch traced here: 143 us
  starting transfers between devices  52.8 us (37%)
  waiting for transfers between devices  42.1 us (29%)
  blocking collectives  26.3 us (18%)
  Pallas kernels  17 us (12%)
  local copies, waits for them, and re-layouts  2.96 us (2%)
    all_to_all x1, blocking collectives, copies_by_a2a(): return lax.all_to_all(copies, axis, 0, 0, tiled=True)  26.3 us
    ppermute x15, waiting for transfers between devices, shift(): lax.ppermute(array, axis, [(i, (i + step) % size) for i in range(size)])  19.8 us
    ppermute x15, starting transfers between devices, shift(): lax.ppermute(array, axis, [(i, (i + step) % size) for i in range(size)])  18.2 us
    pallas_call x10, Pallas kernels, call(): pl.pallas_call(body, out_shape=outs, in_specs=[SM] + [VM] * (len(ins) - 1...  12 us
    all_to_all x1, waiting for transfers between devices, local(): part = lax.all_to_all(part, 'z', 0, 0, tiled=True)  11.2 us
    all_to_all x1, starting transfers between devices, local(): rows = lax.all_to_all(attn, 'z', 0, 0, tiled=True).reshape(96, 1024)  8.48 us
    all_to_all x1, waiting for transfers between devices, local(): pieces = lax.all_to_all(proj(at, rows, weights), HEAD, 0, 0, tiled=True)  6.81 us
    ppermute x1, starting transfers between devices, local(): res_cross = lax.ppermute(res_cross, ALL, device_pairs(swap_cross))  5.95 us
  transfers between devices with their start and end apart: 25, of which 13 were waited for; matrix products, arithmetic and copies ran while one was open for 1% of the time, Pallas kernels for 8%

profile of v5, /device:TPU:6, one launch (start us, length us, event | category | flops | bytes accessed | tf_op | source)
XLA Modules:
  0.0 143.0 jit_solution(16349608772633391721)
XLA Ops:
  0.7 1.5 %collective-permute-start.1 = (bf16[1024,256]{1,0:T(8,128)(2,1)}, bf16[1024,256]{1,0:T(8,128)(2,1)S(1)}, u32[]{:S(2)}, u32[]{:S(2)}) collective-permute-start(bf16[1024,256]{1,0:T(8,128)(2,1)} %w0.1), channel_id=1, source_target_pairs={{0,128},{1,129},{128,0},{129,1},{2,130},{3,131},{130,2},{131,3},{4... | collective-permute-start | bytes 1572872 | tf_op jit(solution)/shard_map/ppermute | solution.py:20
  2.1 2.1 %collective-permute-start = (bf16[1024,256]{1,0:T(8,128)(2,1)}, bf16[1024,256]{1,0:T(8,128)(2,1)}, u32[]{:S(2)}, u32[]{:S(2)}) collective-permute-start(bf16[1024,256]{1,0:T(8,128)(2,1)} %w0.1), channel_id=1, source_target_pairs={{0,1},{1,128},{128,129},{129,0},{2,3},{3,130},{130,131},{131,2},{4... | collective-permute-start | bytes 1572872 | tf_op jit(solution)/shard_map/ppermute | solution.py:20
  4.2 5.0 %shard_map.131 = bf16[8,12,1024]{2,1,0:T(8,128)(2,1)} custom-call(s32[12]{0:T(128)} %lengths.1, bf16[12,1024]{1,0:T(8,128)(2,1)} %q.1, bf16[12,128]{1,0:T(8,128)(2,1)} %kn.1, bf16[12,128]{1,0:T(8,128)(2,1)} %vn.1, bf16[12,1024,128]{2,1,0:T(8,128)(2,1)} %k_hbm.1, bf16[12,1024,128]{2,1,0:T(8,128)(2,1)} %v_hbm.1), custom_call_target="tpu_custom_call" | custom-call | flops 50331648 | bytes 6291456 | tf_op jit(solution)/shard_map/pallas_call | solution.py:123
  9.3 8.5 %all-to-all-start = ((bf16[8,12,1024]{2,1,0:T(8,128)(2,1)}), bf16[8,12,1024]{2,1,0:T(8,128)(2,1)S(1)}, u32[]{:S(2)}, u32[]{:S(2)}) async-start(bf16[8,12,1024]{2,1,0:T(8,128)(2,1)} %shard_map.131), calls=%async_computation | async-start | bytes 524288 | tf_op jit(solution)/shard_map/all_to_all | solution.py:324
  17.8 6.0 %collective-permute-start.4 = (bf16[24,256]{1,0:T(8,128)(2,1)S(1)}, bf16[24,256]{1,0:T(8,128)(2,1)S(1)}, u32[]{:S(2)}, u32[]{:S(2)}) collective-permute-start(bf16[24,256]{1,0:T(8,128)(2,1)S(1)} %reshape.35), channel_id=1, source_target_pairs={{0,1},{1,0},{2,3},{3,2},{4,5},{5,4},{6,7},{7,6},{8,129},{9,128},{1... | collective-permute-start | bytes 36872 | tf_op jit(solution)/shard_map/ppermute | solution.py:330
  23.8 1.9 %collective-permute-start.3 = (bf16[24,256]{1,0:T(8,128)(2,1)S(1)}, bf16[24,256]{1,0:T(8,128)(2,1)S(1)}, u32[]{:S(2)}, u32[]{:S(2)}) collective-permute-start(bf16[24,256]{1,0:T(8,128)(2,1)S(1)} %reshape.34), channel_id=1, source_target_pairs={{0,0},{1,1},{2,2},{3,3},{4,4},{5,5},{6,6},{7,7},{8,128},{9,129},{1... | collective-permute-start | bytes 36872 | tf_op jit(solution)/shard_map/ppermute | solution.py:329
  25.8 3.3 %all-to-all-done = bf16[8,12,1024]{2,1,0:T(8,128)(2,1)S(1)} async-done(((bf16[8,12,1024]{2,1,0:T(8,128)(2,1)}), bf16[8,12,1024]{2,1,0:T(8,128)(2,1)S(1)}, u32[]{:S(2)}, u32[]{:S(2)}) %all-to-all-start) | async-done | bytes 196640 | tf_op jit(solution)/shard_map/all_to_all | solution.py:324
  29.2 2.5 %shard_map.132 = bf16[8,2,24,256]{3,2,1,0:T(8,128)(2,1)} custom-call(s32[4]{0:T(128)S(1)} %pad_add_fusion.at.refs_0_, bf16[96,1024]{1,0:T(8,128)(2,1)S(1)} %reshape.32.rows, bf16[1024,256]{1,0:T(8,128)(2,1)S(1)} %copy-done.3, bf16[1024,256]{1,0:T(8,128)(2,1)} %collective-permute-done.w1, bf16[1024,256]{1,0:T(8,128)(2,1)S(1)} %collective-permute-done.1.w2, ...), custom_call_target="tpu_custom_call" | custom-call | flops 201326592 | bytes 2293776 | tf_op jit(solution)/shard_map/pallas_call | solution.py:146
  31.6 4.5 %all-to-all-start.1 = ((bf16[8,2,24,256]{3,2,1,0:T(8,128)(2,1)}), bf16[8,2,24,256]{3,2,1,0:T(8,128)(2,1)S(1)}, u32[]{:S(2)}, u32[]{:S(2)}) async-start(bf16[8,2,24,256]{3,2,1,0:T(8,128)(2,1)} %shard_map.132), calls=%async_computation.1 | async-start | bytes 393216 | tf_op jit(solution)/shard_map/all_to_all | solution.py:333
  36.1 6.8 %all-to-all-done.1 = bf16[8,2,24,256]{3,2,1,0:T(8,128)(2,1)S(1)} async-done(((bf16[8,2,24,256]{3,2,1,0:T(8,128)(2,1)}), bf16[8,2,24,256]{3,2,1,0:T(8,128)(2,1)S(1)}, u32[]{:S(2)}, u32[]{:S(2)}) %all-to-all-start.1) | async-done | bytes 196640 | tf_op jit(solution)/shard_map/all_to_all | solution.py:333
  43.7 26.3 %all_to_all.20.p0.refs_2_ = bf16[8,24,512]{2,1,0:T(8,128)(2,1)S(1)} all-to-all(bf16[8,24,512]{2,1,0:T(8,128)(2,1)S(1)} %broadcast_in_dim.3), channel_id=1, replica_groups=mesh['xh'=2,'z'=8,'y'=4,'c'=2,'xl'=2] {'z'}, dimensions={0} | all-to-all | bytes 393216 | tf_op jit(solution)/shard_map/all_to_all | solution.py:25
  70.0 1.9 %collective-permute-start.9 = (bf16[8,24,512]{2,1,0:T(8,128)(2,1)S(1)}, bf16[8,24,512]{2,1,0:T(8,128)(2,1)S(1)}, u32[]{:S(2)}, u32[]{:S(2)}) collective-permute-start(bf16[8,24,512]{2,1,0:T(8,128)(2,1)S(1)} %all_to_all.20.p0.refs_2_), channel_id=1, source_target_pairs={{0,128},{1,129},{128,0},{129,1},{2,130},{3,131},{130,2},{131,3},{4... | collective-permute-start | bytes 589832 | tf_op jit(solution)/shard_map/ppermute | solution.py:20
  72.0 2.0 %collective-permute-start.8 = (bf16[8,24,512]{2,1,0:T(8,128)(2,1)S(1)}, bf16[8,24,512]{2,1,0:T(8,128)(2,1)S(1)}, u32[]{:S(2)}, u32[]{:S(2)}) collective-permute-start(bf16[8,24,512]{2,1,0:T(8,128)(2,1)S(1)} %all_to_all.20.p0.refs_2_), channel_id=1, source_target_pairs={{0,1},{1,128},{128,129},{129,0},{2,3},{3,130},{130,131},{131,2},{4... | collective-permute-start | bytes 589832 | tf_op jit(solution)/shard_map/ppermute | solution.py:20
  74.7 1.5 %copy-done.1 = bf16[1024,896]{1,0:T(8,128)(2,1)S(1)} copy-done((bf16[1024,896]{1,0:T(8,128)(2,1)S(1)}, bf16[1024,896]{1,0:T(8,128)(2,1)}, u32[]{:S(2)}) %copy-start.1) | copy-done | bytes 1835032
  76.8 2.2 %collective-permute-done.10.refs_5_ = bf16[8,24,512]{2,1,0:T(8,128)(2,1)S(1)} collective-permute-done((bf16[8,24,512]{2,1,0:T(8,128)(2,1)S(1)}, bf16[8,24,512]{2,1,0:T(8,128)(2,1)S(1)}, u32[]{:S(2)}, u32[]{:S(2)}) %collective-permute-start.10) | collective-permute-done | bytes 196640 | tf_op jit(solution)/shard_map/ppermute | solution.py:20
  79.9 1.6 %shard_map.135 = bf16[4,48,1920]{2,1,0:T(8,128)(2,1)S(1)} custom-call(s32[4]{0:T(128)S(1)} %pad_add_fusion.at.refs_0_, f32[8,24,128]{2,1,0:T(8,128)S(1)} %shard_map.133.refs_1_, bf16[8,24,512]{2,1,0:T(8,128)(2,1)S(1)} %all_to_all.20.p0.refs_2_, bf16[8,24,512]{2,1,0:T(8,128)(2,1)S(1)} %collective-permute-done.8.refs_3_, ...), custom_call_target="tpu_custom_call" | custom-call | flops 704643072 | bytes 4558864 | tf_op jit(solution)/shard_map/pallas_call | solution.py:146
  81.6 1.6 %shard_map.134.mine = f32[4,48,1920]{2,1,0:T(8,128)S(1)} custom-call(s32[4]{0:T(128)S(1)} %pad_add_fusion.at.refs_0_, f32[8,24,128]{2,1,0:T(8,128)S(1)} %shard_map.133.refs_1_, bf16[8,24,512]{2,1,0:T(8,128)(2,1)S(1)} %all_to_all.20.p0.refs_2_, bf16[8,24,512]{2,1,0:T(8,128)(2,1)S(1)} %collective-permute-done.8.refs_3_, ...), custom_call_target="tpu_custom_call" | custom-call | flops 704643072 | bytes 4558864 | tf_op jit(solution)/shard_map/pallas_call | solution.py:146
  85.4 2.4 %collective-permute-start.14 = (bf16[48,1920]{1,0:T(8,128)(2,1)S(1)}, bf16[48,1920]{1,0:T(8,128)(2,1)S(1)}, u32[]{:S(2)}, u32[]{:S(2)}) collective-permute-start(bf16[48,1920]{1,0:T(8,128)(2,1)S(1)} %get-tuple-element.15), channel_id=1, source_target_pairs={{0,12},{4,0},{8,4},{12,8},{1,13},{5,1},{9,5},{13,9},{2,14},{6,2},{... | collective-permute-start | bytes 552968 | tf_op jit(solution)/shard_map/ppermute | solution.py:20
  87.8 8.6 %collective-permute-done.12.r1 = bf16[48,1920]{1,0:T(8,128)(2,1)S(1)} collective-permute-done((bf16[48,1920]{1,0:T(8,128)(2,1)S(1)}, bf16[48,1920]{1,0:T(8,128)(2,1)S(1)}, u32[]{:S(2)}, u32[]{:S(2)}) %collective-permute-start.12) | collective-permute-done | bytes 184352 | tf_op jit(solution)/shard_map/ppermute | solution.py:20
  97.7 2.6 %collective-permute-start.17 = (bf16[48,896]{1,0:T(8,128)(2,1)S(1)}, bf16[48,896]{1,0:T(8,128)(2,1)S(1)}, u32[]{:S(2)}, u32[]{:S(2)}) collective-permute-start(bf16[48,896]{1,0:T(8,128)(2,1)S(1)} %shard_map.137.p0), channel_id=1, source_target_pairs={{0,12},{4,0},{8,4},{12,8},{1,13},{5,1},{9,5},{13,9},{2,14},{6,2},{... | collective-permute-start | bytes 258056 | tf_op jit(solution)/shard_map/ppermute | solution.py:20
  100.3 1.0 collective-permute-start.15
  101.3 2.6 %collective-permute-done.17.p3 = bf16[48,896]{1,0:T(8,128)(2,1)S(1)} collective-permute-done((bf16[48,896]{1,0:T(8,128)(2,1)S(1)}, bf16[48,896]{1,0:T(8,128)(2,1)S(1)}, u32[]{:S(2)}, u32[]{:S(2)}) %collective-permute-start.17) | collective-permute-done | bytes 86048 | tf_op jit(solution)/shard_map/ppermute | solution.py:20
  103.9 2.8 %collective-permute-done.16.p2 = bf16[48,896]{1,0:T(8,128)(2,1)S(1)} collective-permute-done((bf16[48,896]{1,0:T(8,128)(2,1)S(1)}, bf16[48,896]{1,0:T(8,128)(2,1)S(1)}, u32[]{:S(2)}, u32[]{:S(2)}) %collective-permute-start.16) | collective-permute-done | bytes 86048 | tf_op jit(solution)/shard_map/ppermute | solution.py:20
  108.0 1.1 shard_map.139.ready
  109.6 1.2 shard_map.140
  110.8 2.7 %collective-permute-start.19 = (bf16[4,24,1024]{2,1,0:T(8,128)(2,1)S(1)}, bf16[4,24,1024]{2,1,0:T(8,128)(2,1)S(1)}, u32[]{:S(2)}, u32[]{:S(2)}) collective-permute-start(bf16[4,24,1024]{2,1,0:T(8,128)(2,1)S(1)} %get-tuple-element.17), channel_id=1, source_target_pairs={{0,1},{1,128},{128,129},{129,0},{2,3},{3,130},{130,131},{131,2},{4... | collective-permute-start | bytes 589832 | tf_op jit(solution)/shard_map/ppermute | solution.py:20
  114.5 5.0 %collective-permute-start.5 = (bf16[24,256]{1,0:T(8,128)(2,1)S(1)}, bf16[24,256]{1,0:T(8,128)(2,1)S(1)}, u32[]{:S(2)}, u32[]{:S(2)}) collective-permute-start(bf16[24,256]{1,0:T(8,128)(2,1)S(1)} %get-tuple-element.24), channel_id=1, source_target_pairs={{0,0},{1,1},{2,2},{3,3},{4,4},{5,5},{6,6},{7,7},{8,128},{9,129},{1... | collective-permute-start | bytes 36872 | tf_op jit(solution)/shard_map/ppermute | solution.py:341
  119.6 4.6 %collective-permute-start.6 = (bf16[24,256]{1,0:T(8,128)(2,1)S(1)}, bf16[24,256]{1,0:T(8,128)(2,1)S(1)}, u32[]{:S(2)}, u32[]{:S(2)}) collective-permute-start(bf16[24,256]{1,0:T(8,128)(2,1)S(1)} %get-tuple-element.25), channel_id=1, source_target_pairs={{0,1},{1,0},{2,3},{3,2},{4,5},{5,4},{6,7},{7,6},{8,129},{9,128},{1... | collective-permute-start | bytes 36872 | tf_op jit(solution)/shard_map/ppermute | solution.py:342
  124.2 1.5 %collective-permute-done.21.r3 = bf16[4,24,1024]{2,1,0:T(8,128)(2,1)S(1)} collective-permute-done((bf16[4,24,1024]{2,1,0:T(8,128)(2,1)S(1)}, bf16[4,24,1024]{2,1,0:T(8,128)(2,1)S(1)}, u32[]{:S(2)}, u32[]{:S(2)}) %collective-permute-start.21) | collective-permute-done | bytes 196640 | tf_op jit(solution)/shard_map/ppermute | solution.py:20
  125.7 1.3 shard_map.141
  127.0 3.4 %all-to-all-start.3 = ((bf16[8,12,1024]{2,1,0:T(8,128)(2,1)}), bf16[8,12,1024]{2,1,0:T(8,128)(2,1)S(1)}, u32[]{:S(2)}, u32[]{:S(2)}) async-start(bf16[8,12,1024]{2,1,0:T(8,128)(2,1)} %shard_map.141), calls=%async_computation.3 | async-start | bytes 524288 | tf_op jit(solution)/shard_map/all_to_all | solution.py:357
  131.1 11.2 %all-to-all-done.3 = bf16[8,12,1024]{2,1,0:T(8,128)(2,1)S(1)} async-done(((bf16[8,12,1024]{2,1,0:T(8,128)(2,1)}), bf16[8,12,1024]{2,1,0:T(8,128)(2,1)S(1)}, u32[]{:S(2)}, u32[]{:S(2)}) %all-to-all-start.3) | async-done | bytes 196640 | tf_op jit(solution)/shard_map/all_to_all | solution.py:357
  (61 shorter events, 10.7 us)
Async XLA Ops:
  0.6 28.5 %copy-start.3 = (bf16[1024,256]{1,0:T(8,128)(2,1)S(1)}, bf16[1024,256]{1,0:T(8,128)(2,1)}, u32[]{:S(2)}) copy-start(bf16[1024,256]{1,0:T(8,128)(2,1)} %w0.1) | copy-start | bytes 1572868
  0.6 17.1 %copy-start.4 = (bf16[48,256]{1,0:T(8,128)(2,1)S(1)}, bf16[48,256]{1,0:T(8,128)(2,1)}, u32[]{:S(2)}) copy-start(bf16[48,256]{1,0:T(8,128)(2,1)} %param.18) | copy-start | bytes 73732
  0.7 28.5 %collective-permute-start.1 = (bf16[1024,256]{1,0:T(8,128)(2,1)}, bf16[1024,256]{1,0:T(8,128)(2,1)S(1)}, u32[]{:S(2)}, u32[]{:S(2)}) collective-permute-start(bf16[1024,256]{1,0:T(8,128)(2,1)} %w0.1), channel_id=1, source_target_pairs={{0,128},{1,129},{128,0},{129,1},{2,130},{3,131},{130,2},{131,3},{4... | collective-permute-start | bytes 1572872 | tf_op jit(solution)/shard_map/ppermute | solution.py:20
  2.1 27.0 %collective-permute-start = (bf16[1024,256]{1,0:T(8,128)(2,1)}, bf16[1024,256]{1,0:T(8,128)(2,1)}, u32[]{:S(2)}, u32[]{:S(2)}) collective-permute-start(bf16[1024,256]{1,0:T(8,128)(2,1)} %w0.1), channel_id=1, source_target_pairs={{0,1},{1,128},{128,129},{129,0},{2,3},{3,130},{130,131},{131,2},{4... | collective-permute-start | bytes 1572872 | tf_op jit(solution)/shard_map/ppermute | solution.py:20
  4.2 24.9 %collective-permute-start.2 = (bf16[1024,256]{1,0:T(8,128)(2,1)}, bf16[1024,256]{1,0:T(8,128)(2,1)}, u32[]{:S(2)}, u32[]{:S(2)}) collective-permute-start(bf16[1024,256]{1,0:T(8,128)(2,1)} %w0.1), channel_id=1, source_target_pairs={{0,129},{1,0},{128,1},{129,128},{2,131},{3,2},{130,3},{131,130},{4... | collective-permute-start | bytes 1572872 | tf_op jit(solution)/shard_map/ppermute | solution.py:20
  9.3 19.8 %all-to-all-start = ((bf16[8,12,1024]{2,1,0:T(8,128)(2,1)}), bf16[8,12,1024]{2,1,0:T(8,128)(2,1)S(1)}, u32[]{:S(2)}, u32[]{:S(2)}) async-start(bf16[8,12,1024]{2,1,0:T(8,128)(2,1)} %shard_map.131), calls=%async_computation | async-start | bytes 524288 | tf_op jit(solution)/shard_map/all_to_all | solution.py:324
  17.8 18.3 %collective-permute-start.4 = (bf16[24,256]{1,0:T(8,128)(2,1)S(1)}, bf16[24,256]{1,0:T(8,128)(2,1)S(1)}, u32[]{:S(2)}, u32[]{:S(2)}) collective-permute-start(bf16[24,256]{1,0:T(8,128)(2,1)S(1)} %reshape.35), channel_id=1, source_target_pairs={{0,1},{1,0},{2,3},{3,2},{4,5},{5,4},{6,7},{7,6},{8,129},{9,128},{1... | collective-permute-start | bytes 36872 | tf_op jit(solution)/shard_map/ppermute | solution.py:330
  23.8 12.4 %collective-permute-start.3 = (bf16[24,256]{1,0:T(8,128)(2,1)S(1)}, bf16[24,256]{1,0:T(8,128)(2,1)S(1)}, u32[]{:S(2)}, u32[]{:S(2)}) collective-permute-start(bf16[24,256]{1,0:T(8,128)(2,1)S(1)} %reshape.34), channel_id=1, source_target_pairs={{0,0},{1,1},{2,2},{3,3},{4,4},{5,5},{6,6},{7,7},{8,128},{9,129},{1... | collective-permute-start | bytes 36872 | tf_op jit(solution)/shard_map/ppermute | solution.py:329
  29.1 45.6 %copy-start = (bf16[1024,896]{1,0:T(8,128)(2,1)S(1)}, bf16[1024,896]{1,0:T(8,128)(2,1)}, u32[]{:S(2)}) copy-start(bf16[1024,896]{1,0:T(8,128)(2,1)} %refs_7_.3) | copy-start | bytes 5505028
  31.6 11.3 %all-to-all-start.1 = ((bf16[8,2,24,256]{3,2,1,0:T(8,128)(2,1)}), bf16[8,2,24,256]{3,2,1,0:T(8,128)(2,1)S(1)}, u32[]{:S(2)}, u32[]{:S(2)}) async-start(bf16[8,2,24,256]{3,2,1,0:T(8,128)(2,1)} %shard_map.132), calls=%async_computation.1 | async-start | bytes 393216 | tf_op jit(solution)/shard_map/all_to_all | solution.py:333
  43.0 0.7 collective-permute-start.7
  70.0 9.0 %collective-permute-start.10 = (bf16[8,24,512]{2,1,0:T(8,128)(2,1)S(1)}, bf16[8,24,512]{2,1,0:T(8,128)(2,1)S(1)}, u32[]{:S(2)}, u32[]{:S(2)}) collective-permute-start(bf16[8,24,512]{2,1,0:T(8,128)(2,1)S(1)} %all_to_all.20.p0.refs_2_), channel_id=1, source_target_pairs={{0,129},{1,0},{128,1},{129,128},{2,131},{3,2},{130,3},{131,130},{4... | collective-permute-start | bytes 589832 | tf_op jit(solution)/shard_map/ppermute | solution.py:20
  70.0 9.0 %collective-permute-start.9 = (bf16[8,24,512]{2,1,0:T(8,128)(2,1)S(1)}, bf16[8,24,512]{2,1,0:T(8,128)(2,1)S(1)}, u32[]{:S(2)}, u32[]{:S(2)}) collective-permute-start(bf16[8,24,512]{2,1,0:T(8,128)(2,1)S(1)} %all_to_all.20.p0.refs_2_), channel_id=1, source_target_pairs={{0,128},{1,129},{128,0},{129,1},{2,130},{3,131},{130,2},{131,3},{4... | collective-permute-start | bytes 589832 | tf_op jit(solution)/shard_map/ppermute | solution.py:20
  72.0 7.9 %collective-permute-start.8 = (bf16[8,24,512]{2,1,0:T(8,128)(2,1)S(1)}, bf16[8,24,512]{2,1,0:T(8,128)(2,1)S(1)}, u32[]{:S(2)}, u32[]{:S(2)}) collective-permute-start(bf16[8,24,512]{2,1,0:T(8,128)(2,1)S(1)} %all_to_all.20.p0.refs_2_), channel_id=1, source_target_pairs={{0,1},{1,128},{128,129},{129,0},{2,3},{3,130},{130,131},{131,2},{4... | collective-permute-start | bytes 589832 | tf_op jit(solution)/shard_map/ppermute | solution.py:20
  74.7 1.5 %copy-start.1 = (bf16[1024,896]{1,0:T(8,128)(2,1)S(1)}, bf16[1024,896]{1,0:T(8,128)(2,1)}, u32[]{:S(2)}) copy-start(bf16[1024,896]{1,0:T(8,128)(2,1)} %refs_8_.3) | copy-start | bytes 5505028
  81.5 2.3 %collective-permute-start.11 = (bf16[4,48,1920]{2,1,0:T(8,128)(2,1)S(1)}, bf16[4,48,1920]{2,1,0:T(8,128)(2,1)S(1)}, u32[]{:S(2)}, u32[]{:S(2)}) collective-permute-start(bf16[4,48,1920]{2,1,0:T(8,128)(2,1)S(1)} %shard_map.135), channel_id=1, source_target_pairs={{0,2},{2,0},{1,3},{3,1},{4,6},{6,4},{5,7},{7,5},{8,10},{10,8},{9,1... | collective-permute-start | bytes 2211848 | tf_op jit(solution)/shard_map/ppermute | solution.py:42
  83.2 24.7 %copy-start.2 = (bf16[896,1024]{1,0:T(8,128)(2,1)S(1)}, bf16[896,1024]{1,0:T(8,128)(2,1)}, u32[]{:S(2)}) copy-start(bf16[896,1024]{1,0:T(8,128)(2,1)} %w.3) | copy-start | bytes 5505028
  84.5 11.9 %collective-permute-start.12 = (bf16[48,1920]{1,0:T(8,128)(2,1)S(1)}, bf16[48,1920]{1,0:T(8,128)(2,1)S(1)}, u32[]{:S(2)}, u32[]{:S(2)}) collective-permute-start(bf16[48,1920]{1,0:T(8,128)(2,1)S(1)} %get-tuple-element.13), channel_id=1, source_target_pairs={{0,4},{4,8},{8,12},{12,0},{1,5},{5,9},{9,13},{13,1},{2,6},{6,10},{... | collective-permute-start | bytes 552968 | tf_op jit(solution)/shard_map/ppermute | solution.py:20
  84.6 11.8 %collective-permute-start.13 = (bf16[48,1920]{1,0:T(8,128)(2,1)S(1)}, bf16[48,1920]{1,0:T(8,128)(2,1)S(1)}, u32[]{:S(2)}, u32[]{:S(2)}) collective-permute-start(bf16[48,1920]{1,0:T(8,128)(2,1)S(1)} %get-tuple-element.14), channel_id=1, source_target_pairs={{0,8},{4,12},{8,0},{12,4},{1,9},{5,13},{9,1},{13,5},{2,10},{6,14},... | collective-permute-start | bytes 552968 | tf_op jit(solution)/shard_map/ppermute | solution.py:20
  85.4 11.7 %collective-permute-start.14 = (bf16[48,1920]{1,0:T(8,128)(2,1)S(1)}, bf16[48,1920]{1,0:T(8,128)(2,1)S(1)}, u32[]{:S(2)}, u32[]{:S(2)}) collective-permute-start(bf16[48,1920]{1,0:T(8,128)(2,1)S(1)} %get-tuple-element.15), channel_id=1, source_target_pairs={{0,12},{4,0},{8,4},{12,8},{1,13},{5,1},{9,5},{13,9},{2,14},{6,2},{... | collective-permute-start | bytes 552968 | tf_op jit(solution)/shard_map/ppermute | solution.py:20
  97.7 6.1 %collective-permute-start.17 = (bf16[48,896]{1,0:T(8,128)(2,1)S(1)}, bf16[48,896]{1,0:T(8,128)(2,1)S(1)}, u32[]{:S(2)}, u32[]{:S(2)}) collective-permute-start(bf16[48,896]{1,0:T(8,128)(2,1)S(1)} %shard_map.137.p0), channel_id=1, source_target_pairs={{0,12},{4,0},{8,4},{12,8},{1,13},{5,1},{9,5},{13,9},{2,14},{6,2},{... | collective-permute-start | bytes 258056 | tf_op jit(solution)/shard_map/ppermute | solution.py:20
  100.3 6.4 %collective-permute-start.16 = (bf16[48,896]{1,0:T(8,128)(2,1)S(1)}, bf16[48,896]{1,0:T(8,128)(2,1)S(1)}, u32[]{:S(2)}, u32[]{:S(2)}) collective-permute-start(bf16[48,896]{1,0:T(8,128)(2,1)S(1)} %shard_map.137.p0), channel_id=1, source_target_pairs={{0,8},{4,12},{8,0},{12,4},{1,9},{5,13},{9,1},{13,5},{2,10},{6,14},... | collective-permute-start | bytes 258056 | tf_op jit(solution)/shard_map/ppermute | solution.py:20
  100.3 6.9 %collective-permute-start.15 = (bf16[48,896]{1,0:T(8,128)(2,1)S(1)}, bf16[48,896]{1,0:T(8,128)(2,1)S(1)}, u32[]{:S(2)}, u32[]{:S(2)}) collective-permute-start(bf16[48,896]{1,0:T(8,128)(2,1)S(1)} %shard_map.137.p0), channel_id=1, source_target_pairs={{0,4},{4,8},{8,12},{12,0},{1,5},{5,9},{9,13},{13,1},{2,6},{6,10},{... | collective-permute-start | bytes 258056 | tf_op jit(solution)/shard_map/ppermute | solution.py:20
  107.9 1.7 %collective-permute-start.18 = (bf16[4,48,896]{2,1,0:T(8,128)(2,1)S(1)}, bf16[4,48,896]{2,1,0:T(8,128)(2,1)S(1)}, u32[]{:S(2)}, u32[]{:S(2)}) collective-permute-start(bf16[4,48,896]{2,1,0:T(8,128)(2,1)S(1)} %shard_map.138.mine), channel_id=1, source_target_pairs={{0,2},{2,0},{1,3},{3,1},{4,6},{6,4},{5,7},{7,5},{8,10},{10,8},{9,1... | collective-permute-start | bytes 1032200 | tf_op jit(solution)/shard_map/ppermute | solution.py:42
  110.8 13.3 %collective-permute-start.19 = (bf16[4,24,1024]{2,1,0:T(8,128)(2,1)S(1)}, bf16[4,24,1024]{2,1,0:T(8,128)(2,1)S(1)}, u32[]{:S(2)}, u32[]{:S(2)}) collective-permute-start(bf16[4,24,1024]{2,1,0:T(8,128)(2,1)S(1)} %get-tuple-element.17), channel_id=1, source_target_pairs={{0,1},{1,128},{128,129},{129,0},{2,3},{3,130},{130,131},{131,2},{4... | collective-permute-start | bytes 589832 | tf_op jit(solution)/shard_map/ppermute | solution.py:20
  113.6 10.6 %collective-permute-start.20 = (bf16[4,24,1024]{2,1,0:T(8,128)(2,1)S(1)}, bf16[4,24,1024]{2,1,0:T(8,128)(2,1)S(1)}, u32[]{:S(2)}, u32[]{:S(2)}) collective-permute-start(bf16[4,24,1024]{2,1,0:T(8,128)(2,1)S(1)} %get-tuple-element.18), channel_id=1, source_target_pairs={{0,128},{1,129},{128,0},{129,1},{2,130},{3,131},{130,2},{131,3},{4... | collective-permute-start | bytes 589832 | tf_op jit(solution)/shard_map/ppermute | solution.py:20
  113.8 11.9 %collective-permute-start.21 = (bf16[4,24,1024]{2,1,0:T(8,128)(2,1)S(1)}, bf16[4,24,1024]{2,1,0:T(8,128)(2,1)S(1)}, u32[]{:S(2)}, u32[]{:S(2)}) collective-permute-start(bf16[4,24,1024]{2,1,0:T(8,128)(2,1)S(1)} %get-tuple-element.19), channel_id=1, source_target_pairs={{0,129},{1,0},{128,1},{129,128},{2,131},{3,2},{130,3},{131,130},{4... | collective-permute-start | bytes 589832 | tf_op jit(solution)/shard_map/ppermute | solution.py:20
  114.5 15.9 %collective-permute-start.5 = (bf16[24,256]{1,0:T(8,128)(2,1)S(1)}, bf16[24,256]{1,0:T(8,128)(2,1)S(1)}, u32[]{:S(2)}, u32[]{:S(2)}) collective-permute-start(bf16[24,256]{1,0:T(8,128)(2,1)S(1)} %get-tuple-element.24), channel_id=1, source_target_pairs={{0,0},{1,1},{2,2},{3,3},{4,4},{5,5},{6,6},{7,7},{8,128},{9,129},{1... | collective-permute-start | bytes 36872 | tf_op jit(solution)/shard_map/ppermute | solution.py:341
  119.6 10.8 %collective-permute-start.6 = (bf16[24,256]{1,0:T(8,128)(2,1)S(1)}, bf16[24,256]{1,0:T(8,128)(2,1)S(1)}, u32[]{:S(2)}, u32[]{:S(2)}) collective-permute-start(bf16[24,256]{1,0:T(8,128)(2,1)S(1)} %get-tuple-element.25), channel_id=1, source_target_pairs={{0,1},{1,0},{2,3},{3,2},{4,5},{5,4},{6,7},{7,6},{8,129},{9,128},{1... | collective-permute-start | bytes 36872 | tf_op jit(solution)/shard_map/ppermute | solution.py:342
  127.0 15.3 %all-to-all-start.3 = ((bf16[8,12,1024]{2,1,0:T(8,128)(2,1)}), bf16[8,12,1024]{2,1,0:T(8,128)(2,1)S(1)}, u32[]{:S(2)}, u32[]{:S(2)}) async-start(bf16[8,12,1024]{2,1,0:T(8,128)(2,1)} %shard_map.141), calls=%async_computation.3 | async-start | bytes 524288 | tf_op jit(solution)/shard_map/all_to_all | solution.py:357
